TPU v7x, 32 devices: a whole 2x2x4 slice. The times are simulated.
32 devices in a mesh: outer: 4 (over y, x), inner: 8 (over z, core).
Axes of the slice: x: 2, y: 2, z: 4, core: 2. Of those that a mesh axis runs over, the one named last changes fastest.
Arguments:
- queries: bfloat16 [8192, 512], P(('outer', 'inner')), may hold values from -56 to 56
- keys: bfloat16 [8192, 512], P(('outer', 'inner')), may hold values from -48 to 48
- values: bfloat16 [8192, 512], P(('outer', 'inner')), may hold values from -6 to 6
- out_weight: bfloat16 [512, 768], replicated, may hold values from -0.25 to 0.25
- slide_lengths: int32 [16], replicated, may hold values from 1 to 6144, 8192 in all
Outputs:
- mixed_output: bfloat16 [8192, 768], P(('outer', 'inner'))
Inputs may be any that keep to these rules, and one draw needn't show every extreme that they name: `slide_lengths`: the lengths sum to 8192.
All inputs are finite; a program needn't handle non-finite values.
Results may differ from a plain program's by a relative error of at most 0.0052.
Values may be sent and summed in bfloat16 or wider, within the bound.
No kernel may reach another device: no remote copies, remote signals or barrier semaphores. Data moves between devices by JAX's collectives and lax.ppermute only.
A program may use at most 64 MiB of HBM per device.

v0:
```python
import jax
import jax.numpy as jnp
from jax import lax
from jax.sharding import PartitionSpec as P

HEADS = 8
HEAD_DIM = 64
SPARSE = 1024


masked_score = -1e30


def from_partner(block, axis, distance):
    count = lax.axis_size(axis)
    route = []
    for low in range(count):
        high = low | 1 << distance
        if high != low and high < count:
            route += [(low, high), (high, low)]
    return lax.ppermute(block, axis, route)


def slide_index(positions, slide_ends):
    return jnp.sum((positions[:, None] >= slide_ends[None, :]).astype(jnp.int32), axis=1)


def segment_attention(query_rows, key_rows, value_rows, query_slides, key_slides):
    scores = jnp.dot(query_rows, key_rows.T, preferred_element_type=jnp.float32) * HEAD_DIM ** (
        -0.5
    )
    scores = jnp.where(query_slides[:, None] == key_slides[None, :], scores, masked_score)
    row_max = jnp.max(scores, axis=1, keepdims=True)
    expos = jnp.exp(scores - row_max)
    totals = jnp.sum(expos, axis=1, keepdims=True)
    probs = expos.astype(jnp.bfloat16)
    branch = jnp.dot(probs, value_rows, preferred_element_type=jnp.float32) / totals
    return (branch, row_max[:, 0] + jnp.log(totals[:, 0]))


def mix_levels(first, second, third):
    largest = jnp.maximum(jnp.maximum(first[1], second[1]), third[1])
    weighted = jnp.zeros_like(first[0])
    weight_sum = jnp.zeros_like(first[1])
    for branch, branch_lse in (first, second, third):
        factor = jnp.exp(branch_lse - largest)
        weighted = weighted + factor[:, None] * branch
        weight_sum = weight_sum + factor
    return weighted / weight_sum[:, None]


def select_rows(matrix, step_rate):
    row_count = matrix.shape[0] // step_rate
    grouped = matrix.reshape(row_count, step_rate, HEADS, HEAD_DIM)
    picked = [grouped[:, head_index % step_rate, head_index, :] for head_index in range(HEADS)]
    return jnp.stack(picked, axis=1).reshape(row_count, HEADS * HEAD_DIM)


def spread_rows(branch, branch_lse, step_rate, offset):
    row_count = branch.shape[0]
    full_branch = jnp.zeros((row_count, step_rate, branch.shape[1]), jnp.float32)
    full_branch = (
        full_branch.at[:, offset, :].set(branch).reshape(row_count * step_rate, branch.shape[1])
    )
    full_lse = jnp.full((row_count, step_rate), masked_score, jnp.float32)
    full_lse = full_lse.at[:, offset].set(branch_lse).reshape(row_count * step_rate)
    return (full_branch, full_lse)


def shards(queries, keys, values, out_weight, slide_lengths):
    tok_dev = queries.shape[0]
    inner_count = lax.axis_size("inner")
    outer_count = lax.axis_size("outer")
    inner_index = lax.axis_index("inner")
    outer_index = lax.axis_index("outer")
    device_index = outer_index * inner_count + inner_index
    mid_rate = tok_dev * inner_count // SPARSE
    top_rate = mid_rate * outer_count
    local_group = SPARSE // tok_dev
    slide_ends = jnp.cumsum(slide_lengths)
    first_token = device_index * tok_dev
    mid_start = outer_index * tok_dev * inner_count
    local_keys = keys
    local_values = values
    for bit_index in range(local_group.bit_length() - 1):
        partner = from_partner((local_keys, local_values), "inner", bit_index)
        upper_half = inner_index // (1 << bit_index) % 2 == 1
        local_keys = jnp.concatenate(
            [
                jnp.where(upper_half, partner[0], local_keys),
                jnp.where(upper_half, local_keys, partner[0]),
            ],
            axis=0,
        )
        local_values = jnp.concatenate(
            [
                jnp.where(upper_half, partner[1], local_values),
                jnp.where(upper_half, local_values, partner[1]),
            ],
            axis=0,
        )
    local_start = first_token - inner_index % local_group * tok_dev
    local_levels = []
    for head_index in range(HEADS):
        columns = slice(head_index * HEAD_DIM, (head_index + 1) * HEAD_DIM)
        query_slides = slide_index(first_token + jnp.arange(tok_dev, dtype=jnp.int32), slide_ends)
        key_slides = slide_index(local_start + jnp.arange(SPARSE, dtype=jnp.int32), slide_ends)
        local_levels.append(
            segment_attention(
                queries[:, columns],
                local_keys[:, columns],
                local_values[:, columns],
                query_slides,
                key_slides,
            )
        )
    upper_levels = []
    mid_keys, mid_values = (
        lax.all_gather(select_rows(keys, mid_rate), "inner", axis=0, tiled=True),
        lax.all_gather(select_rows(values, mid_rate), "inner", axis=0, tiled=True),
    )
    top_keys, top_values = (
        lax.all_gather(select_rows(keys, top_rate), ("outer", "inner"), axis=0, tiled=True),
        lax.all_gather(select_rows(values, top_rate), ("outer", "inner"), axis=0, tiled=True),
    )
    level_table = ((mid_rate, mid_keys, mid_values, mid_start), (top_rate, top_keys, top_values, 0))
    for head_index in range(HEADS):
        columns = slice(head_index * HEAD_DIM, (head_index + 1) * HEAD_DIM)
        levels = []
        for step_rate, level_keys, level_values, key_start in level_table:
            offset = head_index % step_rate
            row_count = tok_dev // step_rate
            query_rows = queries[:, columns].reshape(row_count, step_rate, HEAD_DIM)[:, offset, :]
            query_slides = slide_index(
                first_token + jnp.arange(row_count, dtype=jnp.int32) * step_rate + offset,
                slide_ends,
            )
            key_slides = slide_index(
                key_start + jnp.arange(SPARSE, dtype=jnp.int32) * step_rate + offset, slide_ends
            )
            branch, branch_lse = segment_attention(
                query_rows,
                level_keys[:, columns],
                level_values[:, columns],
                query_slides,
                key_slides,
            )
            levels.append(spread_rows(branch, branch_lse, step_rate, offset))
        upper_levels.append((levels[0], levels[1]))
    head_outputs = []
    for head_index in range(HEADS):
        head_outputs.append(
            mix_levels(
                local_levels[head_index], upper_levels[head_index][0], upper_levels[head_index][1]
            )
        )
    attention = jnp.concatenate(head_outputs, axis=1).astype(jnp.bfloat16)
    return jnp.dot(attention, out_weight, preferred_element_type=jnp.float32).astype(jnp.bfloat16)


def solution(mesh):
    in_specs = (
        P(("outer", "inner"), None),
        P(("outer", "inner"), None),
        P(("outer", "inner"), None),
        P(),
        P(),
    )
    out_specs = P(("outer", "inner"), None)
    return jax.shard_map(shards, mesh=mesh, in_specs=in_specs, out_specs=out_specs, check_vma=False)
```

profile of v0, /device:TPU:0, one launch (start us, length us, event | category | flops | bytes accessed | tf_op | source)
XLA Modules:
  0.0 221.8 jit_solution(13979306512932093592)
XLA Ops:
  6.5 1.3 reshape.1939
  23.5 3.1 %collective-permute-start.1 = (bf16[512,512]{1,0:T(8,128)(2,1)S(1)}, bf16[512,512]{1,0:T(8,128)(2,1)S(1)}, u32[]{:S(2)}, u32[]{:S(2)}) collective-permute-start(bf16[512,512]{1,0:T(8,128)(2,1)S(1)} %pad_maximum_fusion), channel_id=1, source_target_pairs={{0,2},{2,0},{1,3},{3,1},{4,6},{6,4},{5,7},{7,5},{8,10},{10,8},{9,1... | collective-permute-start | bytes 1572872 | tf_op jit(solution)/shard_map/ppermute | solution.py:21
  27.2 1.5 slice.1063
  28.7 1.5 copy.852
  30.2 1.4 slice.981
  31.7 1.5 slice.1007
  33.1 1.5 slice.1017
  34.6 1.5 slice.1027
  36.0 1.5 slice.1037
  37.5 1.5 slice.1047
  38.9 1.5 slice.1057
  40.4 1.5 slice.1065
  63.9 9.2 %collective-permute-done.3 = bf16[512,512]{1,0:T(8,128)(2,1)S(1)} collective-permute-done((bf16[512,512]{1,0:T(8,128)(2,1)S(1)}, bf16[512,512]{1,0:T(8,128)(2,1)S(1)}, u32[]{:S(2)}, u32[]{:S(2)}) %collective-permute-start.3) | collective-permute-done | bytes 524320 | tf_op jit(solution)/shard_map/ppermute | solution.py:21
  73.9 1.2 fusion.326
  78.3 1.2 fusion.332
  82.6 1.2 fusion.338
  86.9 1.2 fusion.344
  90.5 1.2 fusion.341
  94.8 1.2 fusion.323
  99.0 1.2 fusion.329
  101.4 1.2 fusion.335
  102.8 1.7 fusion.91
  104.5 1.5 copy.901
  106.0 1.7 fusion.93
  111.5 15.5 %all-gather.7.cloned.1.call-done = bf16[1024,512]{1,0:T(8,128)(2,1)} async-done(((bf16[32,512]{1,0:T(8,128)(2,1)}), bf16[1024,512]{1,0:T(8,128)(2,1)}) %all-gather.7.cloned.1.call-update) | async-done | bytes 1048592 | tf_op jit(solution)/shard_map/all_gather | solution.py:123
  127.6 1.3 fusion.343
  131.7 1.3 fusion.340
  136.1 1.3 fusion.337
  140.6 1.3 fusion.334
  145.0 1.3 fusion.331
  150.1 1.4 reshape.1978
  152.0 1.3 fusion.328
  156.8 1.3 fusion.322
  159.2 1.2 fusion.285
  161.8 1.3 reshape.1947
  163.8 1.3 fusion.325
  169.1 1.3 reshape.1960
  170.4 12.5 %all-gather.11.cloned.1.call-done = bf16[1024,512]{1,0:T(8,128)(2,1)} async-done(((bf16[32,512]{1,0:T(8,128)(2,1)}), bf16[1024,512]{1,0:T(8,128)(2,1)}) %all-gather.11.cloned.1.call-update) | async-done | bytes 1048592 | tf_op jit(solution)/shard_map/all_gather | solution.py:124
  182.9 1.2 convolution_divide_fusion.23
  184.8 1.3 convolution_divide_fusion.22
  186.9 1.2 convolution_divide_fusion.21
  188.9 1.3 convolution_divide_fusion.20
  190.9 1.2 convolution_divide_fusion.19
  192.8 1.3 convolution_divide_fusion.18
  194.7 1.2 convolution_divide_fusion.17
  196.6 1.3 convolution_divide_fusion.16
  204.3 1.6 fusion.73
  214.1 1.1 convolution_convert_fusion
  (547 shorter events, 107.3 us)
Async XLA Ops:
  6.5 207.6 %copy-start = (bf16[512,768]{1,0:T(8,128)(2,1)S(1)}, bf16[512,768]{1,0:T(8,128)(2,1)}, u32[]{:S(2)}) copy-start(bf16[512,768]{1,0:T(8,128)(2,1)} %param.72) | copy-start | bytes 2359300
  6.5 66.8 %all-gather.5.cloned.1.call-start = ((), (), s32[]{:S(2)}) async-start(), calls=%async_computation | async-start | bytes 1179648 | tf_op jit(solution)/shard_map/all_gather | solution.py:119
  9.9 65.4 %all-gather.9.cloned.1.call-start = ((), (), s32[]{:S(2)}) async-start(), calls=%async_computation.2 | async-start | bytes 1179648 | tf_op jit(solution)/shard_map/all_gather | solution.py:120
  12.3 114.6 %all-gather.7.cloned.1.call-start = ((), (), s32[]{:S(2)}) async-start(), calls=%async_computation.1 | async-start | bytes 1081344 | tf_op jit(solution)/shard_map/all_gather | solution.py:123
  13.7 169.2 %all-gather.11.cloned.1.call-start = ((), (), s32[]{:S(2)}) async-start(), calls=%async_computation.3 | async-start | bytes 1081344 | tf_op jit(solution)/shard_map/all_gather | solution.py:124
  13.8 9.6 %collective-permute-start = (bf16[256,512]{1,0:T(8,128)(2,1)S(1)}, bf16[256,512]{1,0:T(8,128)(2,1)S(1)}, u32[]{:S(2)}, u32[]{:S(2)}) collective-permute-start(bf16[256,512]{1,0:T(8,128)(2,1)S(1)} %copy-done.16), channel_id=1, source_target_pairs={{0,1},{1,0},{2,3},{3,2},{4,5},{5,4},{6,7},{7,6},{8,9},{9,8},{10,11... | collective-permute-start | bytes 786440 | tf_op jit(solution)/shard_map/ppermute | solution.py:21
  14.3 9.1 %collective-permute-start.2 = (bf16[256,512]{1,0:T(8,128)(2,1)S(1)}, bf16[256,512]{1,0:T(8,128)(2,1)S(1)}, u32[]{:S(2)}, u32[]{:S(2)}) collective-permute-start(bf16[256,512]{1,0:T(8,128)(2,1)S(1)} %copy-done.15), channel_id=1, source_target_pairs={{0,1},{1,0},{2,3},{3,2},{4,5},{5,4},{6,7},{7,6},{8,9},{9,8},{10,11... | collective-permute-start | bytes 786440 | tf_op jit(solution)/shard_map/ppermute | solution.py:21
  14.9 7.5 %copy-start.14 = (bf16[256,512]{1,0:T(8,128)(2,1)S(1)}, bf16[256,512]{1,0:T(8,128)(2,1)}, u32[]{:S(2)}) copy-start(bf16[256,512]{1,0:T(8,128)(2,1)} %param.69) | copy-start | bytes 786436
  23.5 30.4 %collective-permute-start.1 = (bf16[512,512]{1,0:T(8,128)(2,1)S(1)}, bf16[512,512]{1,0:T(8,128)(2,1)S(1)}, u32[]{:S(2)}, u32[]{:S(2)}) collective-permute-start(bf16[512,512]{1,0:T(8,128)(2,1)S(1)} %pad_maximum_fusion), channel_id=1, source_target_pairs={{0,2},{2,0},{1,3},{3,1},{4,6},{6,4},{5,7},{7,5},{8,10},{10,8},{9,1... | collective-permute-start | bytes 1572872 | tf_op jit(solution)/shard_map/ppermute | solution.py:21
  44.6 6.3 %copy-start.131 = (s32[32]{0:T(128)S(1)}, s32[32]{0:T(128)}, u32[]{:S(2)}) copy-start(s32[32]{0:T(128)} %get-tuple-element.557) | copy-start | bytes 388
  44.6 6.3 %copy-start.132 = (s32[32]{0:T(128)S(1)}, s32[32]{0:T(128)}, u32[]{:S(2)}) copy-start(s32[32]{0:T(128)} %get-tuple-element.558) | copy-start | bytes 388
  44.6 6.3 %copy-start.133 = (s32[32]{0:T(128)S(1)}, s32[32]{0:T(128)}, u32[]{:S(2)}) copy-start(s32[32]{0:T(128)} %get-tuple-element.559) | copy-start | bytes 388
  44.7 6.3 %copy-start.135 = (s32[32]{0:T(128)S(1)}, s32[32]{0:T(128)}, u32[]{:S(2)}) copy-start(s32[32]{0:T(128)} %get-tuple-element.550) | copy-start | bytes 388
  44.7 6.3 %copy-start.136 = (s32[32]{0:T(128)S(1)}, s32[32]{0:T(128)}, u32[]{:S(2)}) copy-start(s32[32]{0:T(128)} %get-tuple-element.551) | copy-start | bytes 388
  50.9 43.9 %copy-start.126 = (s32[128]{0:T(128)}, s32[128]{0:T(128)S(1)}, u32[]{:S(2)}) copy-start(s32[128]{0:T(128)S(1)} %get-tuple-element.409) | copy-start | bytes 1540
  50.9 1.4 copy-start.59
  53.7 41.0 %copy-start.81 = (s32[1024]{0:T(1024)}, s32[1024]{0:T(1024)S(1)}, u32[]{:S(2)}) copy-start(s32[1024]{0:T(1024)S(1)} %get-tuple-element.398) | copy-start | bytes 12292
  53.8 19.3 %collective-permute-start.3 = (bf16[512,512]{1,0:T(8,128)(2,1)S(1)}, bf16[512,512]{1,0:T(8,128)(2,1)S(1)}, u32[]{:S(2)}, u32[]{:S(2)}) collective-permute-start(bf16[512,512]{1,0:T(8,128)(2,1)S(1)} %pad_maximum_fusion.1), channel_id=1, source_target_pairs={{0,2},{2,0},{1,3},{3,1},{4,6},{6,4},{5,7},{7,5},{8,10},{10,8},{9,1... | collective-permute-start | bytes 1572872 | tf_op jit(solution)/shard_map/ppermute | solution.py:21
  54.4 2.5 %copy-start.13 = (f32[256,1024]{0,1:T(8,128)}, f32[256,1024]{0,1:T(8,128)S(1)}, u32[]{:S(2)}) copy-start(f32[256,1024]{0,1:T(8,128)S(1)} %get-tuple-element.499) | copy-start | bytes 3145732
  54.5 2.5 %copy-start.47 = (f32[256]{0:T(256)}, f32[256]{0:T(256)S(1)}, u32[]{:S(2)}) copy-start(f32[256]{0:T(256)S(1)} %get-tuple-element.498) | copy-start | bytes 3076
  54.9 2.9 %copy-start.11 = (f32[256,1024]{0,1:T(8,128)}, f32[256,1024]{0,1:T(8,128)S(1)}, u32[]{:S(2)}) copy-start(f32[256,1024]{0,1:T(8,128)S(1)} %get-tuple-element.505) | copy-start | bytes 3145732
  54.9 2.9 %copy-start.45 = (f32[256]{0:T(256)}, f32[256]{0:T(256)S(1)}, u32[]{:S(2)}) copy-start(f32[256]{0:T(256)S(1)} %get-tuple-element.504) | copy-start | bytes 3076
  55.3 3.3 %copy-start.9 = (f32[256,1024]{0,1:T(8,128)}, f32[256,1024]{0,1:T(8,128)S(1)}, u32[]{:S(2)}) copy-start(f32[256,1024]{0,1:T(8,128)S(1)} %get-tuple-element.511) | copy-start | bytes 3145732
  55.3 3.3 %copy-start.43 = (f32[256]{0:T(256)}, f32[256]{0:T(256)S(1)}, u32[]{:S(2)}) copy-start(f32[256]{0:T(256)S(1)} %get-tuple-element.510) | copy-start | bytes 3076
  55.7 3.6 %copy-start.7 = (f32[256,1024]{0,1:T(8,128)}, f32[256,1024]{0,1:T(8,128)S(1)}, u32[]{:S(2)}) copy-start(f32[256,1024]{0,1:T(8,128)S(1)} %get-tuple-element.517) | copy-start | bytes 3145732
  55.7 3.6 %copy-start.41 = (f32[256]{0:T(256)}, f32[256]{0:T(256)S(1)}, u32[]{:S(2)}) copy-start(f32[256]{0:T(256)S(1)} %get-tuple-element.516) | copy-start | bytes 3076
  56.1 4.0 %copy-start.5 = (f32[256,1024]{0,1:T(8,128)}, f32[256,1024]{0,1:T(8,128)S(1)}, u32[]{:S(2)}) copy-start(f32[256,1024]{0,1:T(8,128)S(1)} %get-tuple-element.523) | copy-start | bytes 3145732
  56.1 4.0 %copy-start.39 = (f32[256]{0:T(256)}, f32[256]{0:T(256)S(1)}, u32[]{:S(2)}) copy-start(f32[256]{0:T(256)S(1)} %get-tuple-element.522) | copy-start | bytes 3076
  56.5 4.4 %copy-start.1 = (f32[256,1024]{0,1:T(8,128)}, f32[256,1024]{0,1:T(8,128)S(1)}, u32[]{:S(2)}) copy-start(f32[256,1024]{0,1:T(8,128)S(1)} %get-tuple-element.529) | copy-start | bytes 3145732
  56.5 4.4 %copy-start.35 = (f32[256]{0:T(256)}, f32[256]{0:T(256)S(1)}, u32[]{:S(2)}) copy-start(f32[256]{0:T(256)S(1)} %get-tuple-element.528) | copy-start | bytes 3076
  57.0 4.8 %copy-start.33 = (f32[256]{0:T(256)}, f32[256]{0:T(256)S(1)}, u32[]{:S(2)}) copy-start(f32[256]{0:T(256)S(1)} %get-tuple-element.540) | copy-start | bytes 3076
  104.5 1.5 copy-start.112
  111.4 15.6 %copy-start.67 = (bf16[32,1,64]{2,1,0:T(2,128)(2,1)S(1)}, bf16[32,1,64]{2,1,0:T(2,128)(2,1)}, u32[]{:S(2)}) copy-start(bf16[32,1,64]{2,1,0:T(2,128)(2,1)} %slice.1065) | copy-start | bytes 12292
  111.4 15.6 %copy-start.80 = (s32[1024]{0:T(1024)S(1)}, s32[1024]{0:T(1024)}, u32[]{:S(2)}) copy-start(s32[1024]{0:T(1024)} %get-tuple-element.397) | copy-start | bytes 12292
  137.4 4.4 %copy-start.29 = (f32[32,1024]{1,0:T(8,128)}, f32[32,1024]{1,0:T(8,128)S(1)}, u32[]{:S(2)}) copy-start(f32[32,1024]{1,0:T(8,128)S(1)} %get-tuple-element.531) | copy-start | bytes 393220
  146.4 6.9 %copy-start.30 = (f32[32,1024]{1,0:T(8,128)}, f32[32,1024]{1,0:T(8,128)S(1)}, u32[]{:S(2)}) copy-start(f32[32,1024]{1,0:T(8,128)S(1)} %get-tuple-element.519) | copy-start | bytes 393220
  169.0 13.8 %copy-start.104 = (f32[32]{0:T(128)S(1)}, f32[32]{0:T(128)}, u32[]{:S(2)}) copy-start(f32[32]{0:T(128)} %copy-done.103) | copy-start | bytes 388
  169.0 13.8 %copy-start.106 = (f32[32]{0:T(128)S(1)}, f32[32]{0:T(128)}, u32[]{:S(2)}) copy-start(f32[32]{0:T(128)} %copy-done.105) | copy-start | bytes 388
  197.9 3.0 %copy-start.40 = (f32[256]{0:T(256)S(1)}, f32[256]{0:T(256)}, u32[]{:S(2)}) copy-start(f32[256]{0:T(256)} %copy-done.39) | copy-start | bytes 3076
  197.9 3.7 %copy-start.36 = (f32[256]{0:T(256)S(1)}, f32[256]{0:T(256)}, u32[]{:S(2)}) copy-start(f32[256]{0:T(256)} %copy-done.35) | copy-start | bytes 3076
  197.9 4.4 %copy-start.38 = (f32[256]{0:T(256)S(1)}, f32[256]{0:T(256)}, u32[]{:S(2)}) copy-start(f32[256]{0:T(256)} %copy-done.37) | copy-start | bytes 3076
  197.9 5.1 %copy-start.34 = (f32[256]{0:T(256)S(1)}, f32[256]{0:T(256)}, u32[]{:S(2)}) copy-start(f32[256]{0:T(256)} %copy-done.33) | copy-start | bytes 3076
  198.0 5.6 %copy-start.20 = (f32[256,64]{0,1:T(8,128)S(1)}, f32[256,64]{0,1:T(8,128)}, u32[]{:S(2)}) copy-start(f32[256,64]{0,1:T(8,128)} %copy.806) | copy-start | bytes 196612
  198.7 4.9 %copy-start.77 = (f32[256]{0:T(256)S(1)}, f32[256]{0:T(256)}, u32[]{:S(2)}) copy-start(f32[256]{0:T(256)} %fusion.97) | copy-start | bytes 3076
  204.3 1.7 copy-start.12
  204.3 1.7 copy-start.18
  204.3 1.7 copy-start.23
  204.3 1.7 copy-start.76
  (99 other events, 76.6 us)
Sparse Core Ops, SparseCore 0:
  10.1 29.8 all-gather.4
  41.6 27.6 all-gather.8
  72.3 54.6 all-gather.6
  129.8 52.9 all-gather.10
where the time goes:
time: 225 us; the launch traced here: 222 us
  local copies, waits for them, and re-layouts  82.4 us (37%)
  matrix products  48.7 us (22%)
  waiting for transfers between devices  37.2 us (17%)
  other arithmetic  34.3 us (15%)
  between operations  15.2 us (7%)
  starting transfers between devices  3.89 us (2%)
    unnamed x330, local copies, waits for them, and re-layouts  35.9 us
    dot_general x24, matrix products, segment_attention(): jnp.dot(probs, value_rows, preferred_element_type=jnp.float32) / totals  24.2 us
    dot_general x24, matrix products, segment_attention(): jnp.dot(query_rows, key_rows.T, preferred_element_type=jnp.float32)  23.4 us
    slice x20, local copies, waits for them, and re-layouts, shards(): queries[:, columns].reshape(row_count, step_rate, HEAD_DIM)[:, offset, :]  16.8 us
    all_gather x1, waiting for transfers between devices, shards(): lax.all_gather(select_rows(keys, top_rate), ('outer', 'inner'), axis=0, t...  15.5 us
    reshape x16, local copies, waits for them, and re-layouts, spread_rows(): full_lse.at[:, offset].set(branch_lse).reshape(row_count * step_rate)  12.7 us
    all_gather x1, waiting for transfers between devices, shards(): lax.all_gather(select_rows(values, top_rate), ('outer', 'inner'), axis=0,...  12.5 us
    another operation x16, other arithmetic  11 us
  transfers between devices with their start and end apart: 8, of which 3 were waited for; matrix products, arithmetic and copies ran while one was open for 49% of the time, Pallas kernels for 0%

commit v1 on v0

v1 whole, which is shorter than its diff:
```python
import functools

import jax
import jax.numpy as jnp
from jax import lax
from jax.experimental import pallas as pl
from jax.experimental.pallas import tpu as pltpu
from jax.sharding import PartitionSpec as P

HEADS = 8
HEAD_DIM = 64
SPARSE = 1024
LANES = 128
FAR = 1 << 30
BARRED = -(2.0**100)
F32 = jnp.float32
BF16 = jnp.bfloat16


def exchange(block, axis, distance):
    count = lax.axis_size(axis)
    return lax.ppermute(block, axis, [(i, i ^ distance) for i in range(count)])


def shift_of(value):
    return value.bit_length() - 1


class Plan:
    def __init__(self, rows, inner, outer):
        self.rows = rows
        self.inner = inner
        self.outer = outer
        self.mid = rows * inner // SPARSE
        self.top = self.mid * outer
        self.group = SPARSE // rows
        self.mid_rows = rows // self.mid
        self.top_rows = rows // self.top
        self.top_tile = max(16, self.top_rows)
        assert HEADS == 2 * self.group and 2 * HEAD_DIM == LANES

    def me(self):
        return lax.axis_index("outer") * self.inner + lax.axis_index("inner")

    def pair(self):
        return lax.axis_index("inner") & (self.group - 1)

    def source_row(self, k):
        a = k >> shift_of(self.mid_rows)
        c = (k & (self.mid_rows - 1)) >> shift_of(self.top_rows)
        b = k & (self.top_rows - 1)
        return self.top * b + self.mid * c + a


def dot(a, b, dims):
    return lax.dot_general(a, b, (dims, ((), ())), preferred_element_type=F32)


def pick(wrapped, head, rows):
    return jnp.where(wrapped == ((rows - head) & (rows - 1)), 1.0, 0.0).astype(BF16)


def pack_kernel(plan, q_ref, k_ref, v_ref, *outs):
    rows, group = plan.rows, plan.group
    mains, mids = outs[:group], outs[group:]
    k = lax.broadcasted_iota(jnp.int32, (rows, rows), 0)
    i = lax.broadcasted_iota(jnp.int32, (rows, rows), 1)
    wrapped = (plan.source_row(k) - i) & (rows - 1)
    first = lax.broadcasted_iota(jnp.int32, (rows, 3 * LANES), 1) % LANES < HEAD_DIM
    scale = jnp.where(
        lax.broadcasted_iota(jnp.int32, (rows, 3 * LANES), 1) < LANES, HEAD_DIM**-0.5, 1.0
    )
    for x in range(group):
        pair = plan.pair() ^ x
        columns = pl.ds(pl.multiple_of(pair * LANES, LANES), LANES)
        block = jnp.concatenate([q_ref[:, columns], k_ref[:, columns], v_ref[:, columns]], axis=1)
        one = dot(pick(wrapped, 2 * pair, rows), block, ((1,), (0,)))
        two = dot(pick(wrapped, 2 * pair + 1, rows), block, ((1,), (0,)))
        packed = (jnp.where(first, one, two) * scale).astype(BF16)
        mains[x][...] = packed
        mids[x][...] = packed[: plan.mid_rows, LANES:]


def features(plan, table_ref, t, base, slot_shift, count, kind):
    r = lax.broadcasted_iota(jnp.int32, (count, LANES), 0)
    lane = lax.broadcasted_iota(jnp.int32, (count, LANES), 1)
    head = 2 * plan.pair() + t
    source = plan.me() ^ (base + (r >> slot_shift))
    k = r & ((1 << slot_shift) - 1)
    position = source * plan.rows + ((plan.source_row(k) + head) & (plan.rows - 1))
    starts = table_ref[2 * t : 2 * t + 1, :]
    ends = table_ref[2 * t + 1 : 2 * t + 2, :]
    inside = (position >= starts) & (position < ends)
    own = (lane < HEAD_DIM) if t == 0 else (lane >= HEAD_DIM)
    return inside, own


def as_query(block, inside, own):
    return jnp.where(own, block.astype(F32), jnp.where(inside, BARRED, 0.0)).astype(BF16)


def as_key(block, inside, own):
    return jnp.where(own, block.astype(F32), jnp.where(inside, 0.0, 1.0)).astype(BF16)


def as_value(block, own):
    return jnp.where(own, block.astype(F32), 1.0)


def row_iota(count):
    return lax.broadcasted_iota(jnp.int32, (count, LANES), 0)


def share(total):
    return total / pltpu.roll(total, HEAD_DIM, axis=1)


def local_kernel(plan, table_ref, *refs):
    rows, group, mid_rows, tile = plan.rows, plan.group, plan.mid_rows, plan.top_tile
    mains, refs = refs[:group], refs[group:]
    rest, (sums_one, sums_two, maxima) = refs[:group], refs[group : group + 3]
    q_s, k_s, v_s, v2_s, vt_s = refs[group + 3 :]
    row = row_iota(rows)
    for t in range(2):
        for x in range(group):
            here = pl.ds(x * rows, rows)
            inside, own = features(plan, table_ref, t, x, shift_of(rows), rows, None)
            q_s[t, here, :] = as_query(mains[x][:, :LANES], inside, own)
            k_s[t, here, :] = as_key(mains[x][:, LANES : 2 * LANES], inside, own)
            value = as_value(mains[x][:, 2 * LANES :], own)
            v_s[t, here, :] = value.astype(BF16)
            v2_s[t, here, :] = jnp.where(row < mid_rows, 2.0 * value, value).astype(BF16)
            vt_s[t, here, :] = jnp.where(row < plan.top_rows, value, 0.0).astype(BF16)
    for x in range(group):
        here = pl.ds(x * rows, rows)
        out = []
        big = []
        for t in range(2):
            scores = dot(q_s[t, here, :], k_s[t], ((1,), (1,)))
            largest = jnp.max(scores, axis=1, keepdims=True)
            probs = jnp.exp(scores - largest).astype(BF16)
            mid_sum = dot(probs[:mid_rows], v2_s[t], ((1,), (0,)))
            top_sum = dot(probs[:tile], vt_s[t], ((1,), (0,)))
            rest_sum = dot(probs[mid_rows:], v_s[t], ((1,), (0,)))
            sums = (sums_one, sums_two)[t]
            sums[pl.ds(x * mid_rows, mid_rows), :] = mid_sum
            sums[pl.ds(x * mid_rows, tile), :] += jnp.where(
                row_iota(tile) < plan.top_rows, top_sum, 0.0
            )
            out.append(share(rest_sum))
            big.append(jnp.broadcast_to(largest[:mid_rows], (mid_rows, LANES)))
        lane = lax.broadcasted_iota(jnp.int32, (rows - mid_rows, LANES), 1)
        rest[x][...] = jnp.where(lane < HEAD_DIM, out[0], out[1]).astype(BF16)
        lane = lax.broadcasted_iota(jnp.int32, (mid_rows, LANES), 1)
        maxima[pl.ds(x * mid_rows, mid_rows), :] = jnp.where(lane < HEAD_DIM, big[0], big[1])


def upper_kernel(plan, table_ref, sums_one, sums_two, maxima, *refs):
    group, mid_rows, tile = plan.group, plan.mid_rows, plan.top_tile
    mains, refs = refs[:group], refs[group:]
    mids, refs = refs[: plan.inner - group], refs[plan.inner - group :]
    tops, outs = refs[: plan.outer - 1], refs[plan.outer - 1 :]
    count = group * mid_rows
    lane = lax.broadcasted_iota(jnp.int32, (count, LANES), 1)
    row = row_iota(count) & (mid_rows - 1)
    queries = jnp.concatenate([main[...] for main in mains], axis=0)
    mid_kv = jnp.concatenate([mid[...] for mid in mids], axis=0)
    top_kv = jnp.concatenate([top[...] for top in tops], axis=0)
    results = []
    for t in range(2):
        inside, own = features(plan, table_ref, t, 0, shift_of(mid_rows), count, None)
        q = as_query(queries, inside, own)
        n_mid = mid_kv.shape[0]
        inside, own = features(plan, table_ref, t, group, shift_of(mid_rows), n_mid, None)
        key = as_key(mid_kv[:, :LANES], inside, own)
        value = as_value(mid_kv[:, LANES:], own)
        key_row = row_iota(n_mid) & (mid_rows - 1)
        top_value = jnp.where(key_row < plan.top_rows, value, 0.0).astype(BF16)
        sums = (sums_one, sums_two)[t][...]
        old = maxima[:, t * HEAD_DIM : t * HEAD_DIM + 1]
        scores = dot(q, key, ((1,), (1,)))
        new = jnp.maximum(old, jnp.max(scores, axis=1, keepdims=True))
        probs = jnp.exp(scores - new).astype(BF16)
        sums = sums * jnp.exp(old - new) + dot(probs, value.astype(BF16), ((1,), (0,)))

        def leading(array):
            return jnp.concatenate(
                [array[x * mid_rows : x * mid_rows + tile] for x in range(group)], axis=0
            )

        top_count = group * tile
        is_top = (row_iota(top_count) & (tile - 1)) < plan.top_rows
        extra = dot(leading(probs), top_value, ((1,), (0,)))
        n_top = top_kv.shape[0]
        inside, own = features(plan, table_ref, t, plan.inner, shift_of(plan.top_rows), n_top, None)
        key = as_key(top_kv[:, :LANES], inside, own)
        value = as_value(top_kv[:, LANES:], own).astype(BF16)
        scores = dot(leading(q), key, ((1,), (1,)))
        old = leading(new)
        new = jnp.maximum(old, jnp.max(scores, axis=1, keepdims=True))
        probs = jnp.exp(scores - new).astype(BF16)
        head = leading(sums)
        lead = (head + extra) * jnp.exp(old - new) + dot(probs, value, ((1,), (0,)))
        lead = jnp.where(is_top, lead, head)
        parts = []
        for x in range(group):
            parts.append(lead[x * tile : (x + 1) * tile])
            if tile < mid_rows:
                parts.append(sums[x * mid_rows + tile : (x + 1) * mid_rows])
        results.append(share(jnp.concatenate(parts, axis=0)))
    both = jnp.where(lane < HEAD_DIM, results[0], results[1]).astype(BF16)
    for x in range(group):
        outs[x][...] = both[x * mid_rows : (x + 1) * mid_rows]


def project_kernel(plan, weight_ref, *refs):
    rows, group = plan.rows, plan.group
    mids, rests, (out_ref, flat) = refs[:group], refs[group : 2 * group], refs[2 * group :]
    i = lax.broadcasted_iota(jnp.int32, (rows, rows), 0)
    k = lax.broadcasted_iota(jnp.int32, (rows, rows), 1)
    wrapped = (plan.source_row(k) - i) & (rows - 1)
    lane = lax.broadcasted_iota(jnp.int32, (rows, LANES), 1)
    for x in range(group):
        pair = plan.pair() ^ x
        block = jnp.concatenate([mids[x][...], rests[x][...]], axis=0)
        one = dot(pick(wrapped, 2 * pair, rows), block, ((1,), (0,)))
        two = dot(pick(wrapped, 2 * pair + 1, rows), block, ((1,), (0,)))
        columns = pl.ds(pl.multiple_of(pair * LANES, LANES), LANES)
        flat[:, columns] = jnp.where(lane < HEAD_DIM, one, two).astype(BF16)
    out_ref[...] = dot(flat[...], weight_ref[...], ((1,), (0,))).astype(BF16)


def slide_table(slide_lengths):
    slides = slide_lengths.shape[0]
    lane = jnp.arange(LANES, dtype=jnp.int32)
    index = jnp.arange(slides, dtype=jnp.int32)
    table = []
    for t in range(2):
        slide = lane - (HEAD_DIM if t == 0 else 0)
        valid = (slide >= 0) & (slide < slides)
        for bound in range(2):
            before = index[None, :] < (slide + bound)[:, None]
            total = jnp.sum(jnp.where(before, slide_lengths[None, :], 0), axis=1)
            table.append(jnp.where(valid, total, FAR))
    return jnp.stack(table + table, axis=0).astype(jnp.int32)


def shards(queries, keys, values, out_weight, slide_lengths):
    plan = Plan(queries.shape[0], lax.axis_size("inner"), lax.axis_size("outer"))
    rows, group, mid_rows = plan.rows, plan.group, plan.mid_rows
    table = slide_table(slide_lengths)
    vmem = pl.BlockSpec(memory_space=pltpu.VMEM)

    def shape(count, width, kind=BF16):
        return jax.ShapeDtypeStruct((count, width), kind)

    packed = pl.pallas_call(
        functools.partial(pack_kernel, plan),
        in_specs=[vmem] * 3,
        out_specs=[vmem] * (2 * group),
        out_shape=[shape(rows, 3 * LANES)] * group + [shape(mid_rows, 2 * LANES)] * group,
        name="pack",
    )(queries, keys, values)
    mains, mids = packed[:group], packed[group:]
    mains = [mains[0]] + [exchange(mains[x], "inner", x) for x in range(1, group)]
    others = [exchange(mids[x & (group - 1)], "inner", x) for x in range(group, plan.inner)]
    top_own = jnp.concatenate(
        [main[: plan.top_rows, LANES:] for main in mains]
        + [other[: plan.top_rows] for other in others],
        axis=0,
    )
    tops = [exchange(top_own, "outer", x) for x in range(1, plan.outer)]

    count = group * rows
    local = pl.pallas_call(
        functools.partial(local_kernel, plan),
        in_specs=[vmem] * (1 + group),
        out_specs=[vmem] * (group + 3),
        out_shape=[shape(rows - mid_rows, LANES)] * group
        + [shape(group * mid_rows, LANES, F32)] * 3,
        scratch_shapes=[pltpu.VMEM((2, count, LANES), BF16)] * 5,
        name="local",
    )(table, *mains)
    rests, state = local[:group], local[group:]
    rests = [rests[0]] + [exchange(rests[x], "inner", x) for x in range(1, group)]

    first = pl.BlockSpec((mid_rows, LANES), lambda i: (0, 0))

    def whole(array):
        return pl.BlockSpec(array.shape, lambda i: (0, 0))

    operands = [table, *state]
    tail = [*others, *tops]
    upper = pl.pallas_call(
        functools.partial(upper_kernel, plan),
        grid=(1,),
        in_specs=[whole(a) for a in operands] + [first] * group + [whole(a) for a in tail],
        out_specs=[first] * group,
        out_shape=[shape(mid_rows, LANES)] * group,
        name="upper",
    )(*operands, *mains, *tail)
    upper = [upper[0]] + [exchange(upper[x], "inner", x) for x in range(1, group)]

    return pl.pallas_call(
        functools.partial(project_kernel, plan),
        in_specs=[vmem] * (1 + 2 * group),
        out_specs=vmem,
        out_shape=shape(rows, out_weight.shape[1]),
        scratch_shapes=[pltpu.VMEM((rows, HEADS * HEAD_DIM), BF16)],
        name="project",
    )(out_weight, *upper, *rests)


def solution(mesh):
    tokens = P(("outer", "inner"), None)
    return jax.shard_map(
        shards,
        mesh=mesh,
        in_specs=(tokens, tokens, tokens, P(), P()),
        out_specs=tokens,
        check_vma=False,
    )
```

time: 225 us -> 54.3 us (0.24); the launches traced: 222 us -> 54.1 us
  local copies, waits for them, and re-layouts: 82.4 us -> 2.66 us
  matrix products: 48.7 us -> 0 us
  other arithmetic: 34.3 us -> 0.11 us
  waiting for transfers between devices: 37.2 us -> 18.8 us
  Pallas kernels: 0 us -> 16.9 us
  between operations: 15.2 us -> 0.25 us
  starting transfers between devices: 3.89 us -> 15.3 us
    dot_general x49 -> x0, matrix products: 48.7 us -> none  [the longest x24 24.2 us: segment_attention(): jnp.dot(probs, value_rows, preferred_element_type=jnp.float32) / totals]
    unnamed x330 -> x41, local copies, waits for them, and re-layouts: 35.9 us -> 2.05 us
    all_gather x4 -> x0, waiting for transfers between devices: 28 us -> none  [the longest x1 15.5 us: shards(): lax.all_gather(select_rows(keys, top_rate), ('outer', 'inner'), axis=0, t...]
    reshape x46 -> x0, local copies, waits for them, and re-layouts: 22.7 us -> none  [the longest x16 12.7 us: spread_rows(): full_lse.at[:, offset].set(branch_lse).reshape(row_count * step_rate)]
    slice x41 -> x0, local copies, waits for them, and re-layouts: 20.4 us -> none  [the longest x20 16.8 us: shards(): queries[:, columns].reshape(row_count, step_rate, HEAD_DIM)[:, offset, :]]
    pallas_call x0 -> x4, Pallas kernels: none -> 16.9 us  [the longest x1 6.82 us: shards(): pl.pallas_call(functools.partial(local_kernel, plan), in_specs=[vmem] * (...]
    ppermute x4 -> x16, starting transfers between devices: 3.77 us -> 15.3 us  [exchange(): return lax.ppermute(block, axis, [(i, i ^ distance) for i in range(count)])]
    reduce_sum x28 -> x1, other arithmetic: 11.5 us -> 0.09 us  [slide_table(): total = jnp.sum(jnp.where(before, slide_lengths[None, :], 0), axis=1)]
  transfers between devices with their start and end apart: 8 -> 16, of which waited for: 3 -> 4; matrix products, arithmetic and copies ran while one was open for 49% -> 3% of each run, Pallas kernels for 0% -> 21%
where the time goes in v1:
time: 54.3 us; the launch traced here: 54.1 us
  waiting for transfers between devices  18.8 us (35%)
  Pallas kernels  16.9 us (31%)
  starting transfers between devices  15.3 us (28%)
  local copies, waits for them, and re-layouts  2.66 us (5%)
    ppermute x16, waiting for transfers between devices, exchange(): return lax.ppermute(block, axis, [(i, i ^ distance) for i in range(count)])  18.8 us
    ppermute x16, starting transfers between devices, exchange(): return lax.ppermute(block, axis, [(i, i ^ distance) for i in range(count)])  15.3 us
    pallas_call x1, Pallas kernels, shards(): pl.pallas_call(functools.partial(local_kernel, plan), in_specs=[vmem] * (...  6.82 us
    pallas_call x1, Pallas kernels, shards(): pl.pallas_call(functools.partial(upper_kernel, plan), grid=(1,), in_specs...  4.7 us
    pallas_call x1, Pallas kernels, shards(): pl.pallas_call(functools.partial(project_kernel, plan), in_specs=[vmem] *...  2.85 us
    pallas_call x1, Pallas kernels, shards(): pl.pallas_call(functools.partial(pack_kernel, plan), in_specs=[vmem] * 3,...  2.53 us
    unnamed x41, local copies, waits for them, and re-layouts  2.05 us
  transfers between devices with their start and end apart: 16, of which 4 were waited for; matrix products, arithmetic and copies ran while one was open for 3% of the time, Pallas kernels for 21%

profile of v1, /device:TPU:0, one launch (start us, length us, event | category | flops | bytes accessed | tf_op | source)
XLA Modules:
  0.0 54.1 jit_solution(14254394539581546412)
XLA Ops:
  0.0 2.5 %pack.1 = (bf16[256,384]{1,0:T(8,128)(2,1)}, bf16[256,384]{1,0:T(8,128)(2,1)}, bf16[256,384]{1,0:T(8,128)(2,1)}, bf16[256,384]{1,0:T(8,128)(2,1)}, bf16[128,256]...) custom-call(bf16[256,512]{1,0:T(8,128)(2,1)} %q_ref.1, ...), custom_call_target="tpu_custom_call" | custom-call | tf_op jit(solution)/shard_map/pack/pallas_call | solution.py:257
  2.5 4.1 %collective-permute-start.3 = (bf16[128,256]{1,0:T(8,128)(2,1)}, bf16[128,256]{1,0:T(8,128)(2,1)S(1)}, u32[]{:S(2)}, u32[]{:S(2)}) collective-permute-start(bf16[128,256]{1,0:T(8,128)(2,1)} %get-tuple-element.31), channel_id=1, source_target_pairs={{0,4},{1,5},{2,6},{3,7},{4,0},{5,1},{6,2},{7,3},{8,12},{9,13},{10,... | collective-permute-start | bytes 196616 | tf_op jit(solution)/shard_map/ppermute | solution.py:22
  6.6 0.0 collective-permute-start.4
  6.6 3.1 %collective-permute-start.5 = (bf16[128,256]{1,0:T(8,128)(2,1)}, bf16[128,256]{1,0:T(8,128)(2,1)S(1)}, u32[]{:S(2)}, u32[]{:S(2)}) collective-permute-start(bf16[128,256]{1,0:T(8,128)(2,1)} %get-tuple-element.33), channel_id=1, source_target_pairs={{0,6},{1,7},{2,4},{3,5},{4,2},{5,3},{6,0},{7,1},{8,14},{9,15},{10,... | collective-permute-start | bytes 196616 | tf_op jit(solution)/shard_map/ppermute | solution.py:22
  9.7 0.6 %collective-permute-start.6 = (bf16[128,256]{1,0:T(8,128)(2,1)}, bf16[128,256]{1,0:T(8,128)(2,1)S(1)}, u32[]{:S(2)}, u32[]{:S(2)}) collective-permute-start(bf16[128,256]{1,0:T(8,128)(2,1)} %get-tuple-element.34), channel_id=1, source_target_pairs={{0,7},{1,6},{2,5},{3,4},{4,3},{5,2},{6,1},{7,0},{8,15},{9,14},{10,... | collective-permute-start | bytes 196616 | tf_op jit(solution)/shard_map/ppermute | solution.py:22
  10.2 0.3 collective-permute-start
  10.6 0.7 %constant_dynamic-update-slice_fusion.7 = bf16[256,256]{1,0:T(8,128)(2,1)S(1)} fusion(bf16[256,384]{1,0:T(8,128)(2,1)} %get-tuple-element.24.refs_0_), kind=kLoop, calls=%fused_computation.7 | loop fusion | bytes 32768
  11.3 0.1 select_reduce_fusion
  11.4 0.5 collective-permute-done.refs_1_
  11.9 0.0 collective-permute-start.1
  11.9 8.5 %collective-permute-done.1.refs_2_ = bf16[256,384]{1,0:T(8,128)(2,1)S(1)} collective-permute-done((bf16[256,384]{1,0:T(8,128)(2,1)}, bf16[256,384]{1,0:T(8,128)(2,1)S(1)}, u32[]{:S(2)}, u32[]{:S(2)}) %collective-permute-start.1) | collective-permute-done | bytes 196640 | tf_op jit(solution)/shard_map/ppermute | solution.py:22
  20.4 0.0 collective-permute-start.2
  20.4 7.2 %collective-permute-done.2.refs_3_ = bf16[256,384]{1,0:T(8,128)(2,1)S(1)} collective-permute-done((bf16[256,384]{1,0:T(8,128)(2,1)}, bf16[256,384]{1,0:T(8,128)(2,1)S(1)}, u32[]{:S(2)}, u32[]{:S(2)}) %collective-permute-start.2) | collective-permute-done | bytes 196640 | tf_op jit(solution)/shard_map/ppermute | solution.py:22
  27.6 0.0 collective-permute-done.3.refs_4_
  27.6 0.0 copy-start.6
  27.6 0.0 collective-permute-done.4.refs_5_
  27.7 0.0 collective-permute-done.5.refs_6_
  27.7 0.0 collective-permute-done.6.refs_7_
  27.7 0.0 copy-start.9
  27.7 2.6 %collective-permute-start.9 = (bf16[256,256]{1,0:T(8,128)(2,1)S(1)}, bf16[256,256]{1,0:T(8,128)(2,1)S(1)}, u32[]{:S(2)}, u32[]{:S(2)}) collective-permute-start(bf16[256,256]{1,0:T(8,128)(2,1)S(1)} %constant_dynamic-update-slice_fusion), channel_id=1, source_target_pairs={{0,24},{8,16},{16,8},{24,0},{1,25},{9,17},{17,9},{25,1},{2,26},{10... | collective-permute-start | bytes 393224 | tf_op jit(solution)/shard_map/ppermute | solution.py:22
  30.3 0.5 collective-permute-start.8
  30.8 0.5 collective-permute-start.7
  31.3 0.6 %stack.2.table_ref = s32[8,128]{1,0:T(8,128)} concatenate(s32[1,128]{1,0:T(1,128)S(1)} %get-tuple-element.50, s32[1,128]{1,0:T(1,128)S(1)} %get-tuple-element.49, s32[1,128]{1,0:T(1,128)S(1)} %get-tuple-element.48, s32[1,128]{1,0:T(1,128)S(1)} %get-tuple-element.47, s32[1,128]{1,0:T(1,128)S(1)} %get-tuple-element.50, s32[1,128]{1,0:T(1,128)S(1)} %get-tuple-element.49, ...), dimensions={0} | concatenate | bytes 8192 | tf_op jit(solution)/shard_map/stack | solution.py:245
  31.9 0.0 copy-done.1
  31.9 6.8 %local.1 = (bf16[128,128]{1,0:T(8,128)(2,1)}, bf16[128,128]{1,0:T(8,128)(2,1)}, bf16[128,128]{1,0:T(8,128)(2,1)}, bf16[128,128]{1,0:T(8,128)(2,1)}, f32[512,128]...) custom-call(s32[8,128]{1,0:T(8,128)} %stack.2.table_ref, bf16[256,384]{1,0:T(8,128)(2,1)} %get-tuple-element.24.refs_0_, ...), custom_call_target="tpu_custom_call" | custom-call | tf_op jit(solution)/shard_map/local/pallas_call | solution.py:275
  38.8 0.1 collective-permute-start.13
  38.8 0.1 collective-permute-start.14
  38.9 0.0 collective-permute-done.9.refs_10_
  38.9 1.8 %collective-permute-start.15 = (bf16[128,128]{1,0:T(8,128)(2,1)}, bf16[128,128]{1,0:T(8,128)(2,1)S(1)}, u32[]{:S(2)}, u32[]{:S(2)}) collective-permute-start(bf16[128,128]{1,0:T(8,128)(2,1)} %get-tuple-element.42), channel_id=1, source_target_pairs={{0,3},{1,2},{2,1},{3,0},{4,7},{5,6},{6,5},{7,4},{8,11},{9,10},{10,... | collective-permute-start | bytes 98312 | tf_op jit(solution)/shard_map/ppermute | solution.py:22
  40.7 0.0 collective-permute-done.8.refs_9_
  40.7 0.0 collective-permute-done.7.refs_8_
  40.7 0.6 %copy-done.4 = bf16[256,256]{1,0:T(8,128)(2,1)} copy-done((bf16[256,256]{1,0:T(8,128)(2,1)}, bf16[256,256]{1,0:T(8,128)(2,1)S(1)}, u32[]{:S(2)}) %copy-start.4) | copy-done | bytes 131096
  41.4 0.0 copy-done.5
  41.4 4.7 %upper.1 = (bf16[128,128]{1,0:T(8,128)(2,1)}, bf16[128,128]{1,0:T(8,128)(2,1)}, bf16[128,128]{1,0:T(8,128)(2,1)}, bf16[128,128]{1,0:T(8,128)(2,1)}) custom-call(s32[8,128]{1,0:T(8,128)} %stack.2.table_ref, f32[512,128]{1,0:T(8,128)} %get-tuple-element.28.sums_one, f32[512,128]{1,0:T(8,128)} %get-tuple-element.29.sums_two, ...), custom_call_target="tpu_custom_call" | custom-call | tf_op jit(solution)/shard_map/upper/pallas_call | solution.py:294
  46.1 0.4 collective-permute-start.10
  46.5 0.1 collective-permute-start.11
  46.6 0.0 collective-permute-done.13.refs_5_
  46.6 1.4 %collective-permute-start.12 = (bf16[128,128]{1,0:T(8,128)(2,1)}, bf16[128,128]{1,0:T(8,128)(2,1)S(1)}, u32[]{:S(2)}, u32[]{:S(2)}) collective-permute-start(bf16[128,128]{1,0:T(8,128)(2,1)} %get-tuple-element.38), channel_id=1, source_target_pairs={{0,3},{1,2},{2,1},{3,0},{4,7},{5,6},{6,5},{7,4},{8,11},{9,10},{10,... | collective-permute-start | bytes 98312 | tf_op jit(solution)/shard_map/ppermute | solution.py:22
  48.0 0.0 collective-permute-done.14.refs_6_
  48.0 0.0 collective-permute-done.15.refs_7_
  48.0 0.0 collective-permute-done.10.refs_1_
  48.0 0.0 copy-start.13
  48.0 2.6 %collective-permute-done.11.refs_2_ = bf16[128,128]{1,0:T(8,128)(2,1)S(1)} collective-permute-done((bf16[128,128]{1,0:T(8,128)(2,1)}, bf16[128,128]{1,0:T(8,128)(2,1)S(1)}, u32[]{:S(2)}, u32[]{:S(2)}) %collective-permute-start.11) | collective-permute-done | bytes 32800 | tf_op jit(solution)/shard_map/ppermute | solution.py:22
  50.6 0.0 collective-permute-done.12.refs_3_
  50.6 0.0 copy-done.11
  50.6 0.6 %copy-done.14 = bf16[128,128]{1,0:T(8,128)(2,1)} copy-done((bf16[128,128]{1,0:T(8,128)(2,1)}, bf16[128,128]{1,0:T(8,128)(2,1)S(1)}, u32[]{:S(2)}) %copy-start.14) | copy-done | bytes 32792
  51.2 0.0 copy-done.15
  51.2 2.9 %project.1 = bf16[256,768]{1,0:T(8,128)(2,1)} custom-call(bf16[512,768]{1,0:T(8,128)(2,1)} %weight_ref.1, bf16[128,128]{1,0:T(8,128)(2,1)} %get-tuple-element.35.refs_0_, bf16[128,128]{1,0:T(8,128)(2,1)} %copy-done.13, bf16[128,128]{1,0:T(8,128)(2,1)} %copy-done.14, bf16[128,128]{1,0:T(8,128)(2,1)} %copy-done.15, ...), custom_call_target="tpu_custom_call" | custom-call | tf_op jit(solution)/shard_map/project/pallas_call | solution.py:304
  (37 shorter events, 0.1 us)
Async XLA Ops:
  2.5 25.1 %collective-permute-start.3 = (bf16[128,256]{1,0:T(8,128)(2,1)}, bf16[128,256]{1,0:T(8,128)(2,1)S(1)}, u32[]{:S(2)}, u32[]{:S(2)}) collective-permute-start(bf16[128,256]{1,0:T(8,128)(2,1)} %get-tuple-element.31), channel_id=1, source_target_pairs={{0,4},{1,5},{2,6},{3,7},{4,0},{5,1},{6,2},{7,3},{8,12},{9,13},{10,... | collective-permute-start | bytes 196616 | tf_op jit(solution)/shard_map/ppermute | solution.py:22
  6.6 21.1 %collective-permute-start.4 = (bf16[128,256]{1,0:T(8,128)(2,1)}, bf16[128,256]{1,0:T(8,128)(2,1)S(1)}, u32[]{:S(2)}, u32[]{:S(2)}) collective-permute-start(bf16[128,256]{1,0:T(8,128)(2,1)} %get-tuple-element.32), channel_id=1, source_target_pairs={{0,5},{1,4},{2,7},{3,6},{4,1},{5,0},{6,3},{7,2},{8,13},{9,12},{10,... | collective-permute-start | bytes 196616 | tf_op jit(solution)/shard_map/ppermute | solution.py:22
  6.6 21.1 %collective-permute-start.5 = (bf16[128,256]{1,0:T(8,128)(2,1)}, bf16[128,256]{1,0:T(8,128)(2,1)S(1)}, u32[]{:S(2)}, u32[]{:S(2)}) collective-permute-start(bf16[128,256]{1,0:T(8,128)(2,1)} %get-tuple-element.33), channel_id=1, source_target_pairs={{0,6},{1,7},{2,4},{3,5},{4,2},{5,3},{6,0},{7,1},{8,14},{9,15},{10,... | collective-permute-start | bytes 196616 | tf_op jit(solution)/shard_map/ppermute | solution.py:22
  9.7 18.0 %collective-permute-start.6 = (bf16[128,256]{1,0:T(8,128)(2,1)}, bf16[128,256]{1,0:T(8,128)(2,1)S(1)}, u32[]{:S(2)}, u32[]{:S(2)}) collective-permute-start(bf16[128,256]{1,0:T(8,128)(2,1)} %get-tuple-element.34), channel_id=1, source_target_pairs={{0,7},{1,6},{2,5},{3,4},{4,3},{5,2},{6,1},{7,0},{8,15},{9,14},{10,... | collective-permute-start | bytes 196616 | tf_op jit(solution)/shard_map/ppermute | solution.py:22
  10.2 1.7 %collective-permute-start = (bf16[256,384]{1,0:T(8,128)(2,1)}, bf16[256,384]{1,0:T(8,128)(2,1)S(1)}, u32[]{:S(2)}, u32[]{:S(2)}) collective-permute-start(bf16[256,384]{1,0:T(8,128)(2,1)} %get-tuple-element.25), channel_id=1, source_target_pairs={{0,1},{1,0},{2,3},{3,2},{4,5},{5,4},{6,7},{7,6},{8,9},{9,8},{10,11... | collective-permute-start | bytes 589832 | tf_op jit(solution)/shard_map/ppermute | solution.py:22
  10.6 0.7 %copy-start.16 = (s32[16]{0:T(128)S(1)}, s32[16]{0:T(128)}, u32[]{:S(2)}) copy-start(s32[16]{0:T(128)} %param.9) | copy-start | bytes 196
  11.9 20.0 %copy-start = (bf16[256,384]{1,0:T(8,128)(2,1)}, bf16[256,384]{1,0:T(8,128)(2,1)S(1)}, u32[]{:S(2)}) copy-start(bf16[256,384]{1,0:T(8,128)(2,1)S(1)} %collective-permute-done.refs_1_) | copy-start | bytes 589828
  11.9 8.5 %collective-permute-start.1 = (bf16[256,384]{1,0:T(8,128)(2,1)}, bf16[256,384]{1,0:T(8,128)(2,1)S(1)}, u32[]{:S(2)}, u32[]{:S(2)}) collective-permute-start(bf16[256,384]{1,0:T(8,128)(2,1)} %get-tuple-element.26), channel_id=1, source_target_pairs={{0,2},{1,3},{2,0},{3,1},{4,6},{5,7},{6,4},{7,5},{8,10},{9,11},{10,... | collective-permute-start | bytes 589832 | tf_op jit(solution)/shard_map/ppermute | solution.py:22
  20.4 11.5 %copy-start.1 = (bf16[256,384]{1,0:T(8,128)(2,1)}, bf16[256,384]{1,0:T(8,128)(2,1)S(1)}, u32[]{:S(2)}) copy-start(bf16[256,384]{1,0:T(8,128)(2,1)S(1)} %collective-permute-done.1.refs_2_) | copy-start | bytes 589828
  20.4 7.2 %collective-permute-start.2 = (bf16[256,384]{1,0:T(8,128)(2,1)}, bf16[256,384]{1,0:T(8,128)(2,1)S(1)}, u32[]{:S(2)}, u32[]{:S(2)}) collective-permute-start(bf16[256,384]{1,0:T(8,128)(2,1)} %get-tuple-element.27), channel_id=1, source_target_pairs={{0,3},{1,2},{2,1},{3,0},{4,7},{5,6},{6,5},{7,4},{8,11},{9,10},{10,... | collective-permute-start | bytes 589832 | tf_op jit(solution)/shard_map/ppermute | solution.py:22
  27.6 4.3 %copy-start.2 = (bf16[256,384]{1,0:T(8,128)(2,1)}, bf16[256,384]{1,0:T(8,128)(2,1)S(1)}, u32[]{:S(2)}) copy-start(bf16[256,384]{1,0:T(8,128)(2,1)S(1)} %collective-permute-done.2.refs_3_) | copy-start | bytes 589828
  27.6 11.1 %copy-start.6 = (bf16[128,256]{1,0:T(8,128)(2,1)}, bf16[128,256]{1,0:T(8,128)(2,1)S(1)}, u32[]{:S(2)}) copy-start(bf16[128,256]{1,0:T(8,128)(2,1)S(1)} %collective-permute-done.3.refs_4_) | copy-start | bytes 196612
  27.7 11.1 %copy-start.7 = (bf16[128,256]{1,0:T(8,128)(2,1)}, bf16[128,256]{1,0:T(8,128)(2,1)S(1)}, u32[]{:S(2)}) copy-start(bf16[128,256]{1,0:T(8,128)(2,1)S(1)} %collective-permute-done.4.refs_5_) | copy-start | bytes 196612
  27.7 11.1 %copy-start.8 = (bf16[128,256]{1,0:T(8,128)(2,1)}, bf16[128,256]{1,0:T(8,128)(2,1)S(1)}, u32[]{:S(2)}) copy-start(bf16[128,256]{1,0:T(8,128)(2,1)S(1)} %collective-permute-done.5.refs_6_) | copy-start | bytes 196612
  27.7 11.0 %copy-start.9 = (bf16[128,256]{1,0:T(8,128)(2,1)}, bf16[128,256]{1,0:T(8,128)(2,1)S(1)}, u32[]{:S(2)}) copy-start(bf16[128,256]{1,0:T(8,128)(2,1)S(1)} %collective-permute-done.6.refs_7_) | copy-start | bytes 196612
  27.7 11.2 %collective-permute-start.9 = (bf16[256,256]{1,0:T(8,128)(2,1)S(1)}, bf16[256,256]{1,0:T(8,128)(2,1)S(1)}, u32[]{:S(2)}, u32[]{:S(2)}) collective-permute-start(bf16[256,256]{1,0:T(8,128)(2,1)S(1)} %constant_dynamic-update-slice_fusion), channel_id=1, source_target_pairs={{0,24},{8,16},{16,8},{24,0},{1,25},{9,17},{17,9},{25,1},{2,26},{10... | collective-permute-start | bytes 393224 | tf_op jit(solution)/shard_map/ppermute | solution.py:22
  30.3 10.4 %collective-permute-start.8 = (bf16[256,256]{1,0:T(8,128)(2,1)S(1)}, bf16[256,256]{1,0:T(8,128)(2,1)S(1)}, u32[]{:S(2)}, u32[]{:S(2)}) collective-permute-start(bf16[256,256]{1,0:T(8,128)(2,1)S(1)} %constant_dynamic-update-slice_fusion), channel_id=1, source_target_pairs={{0,16},{8,24},{16,0},{24,8},{1,17},{9,25},{17,1},{25,9},{2,18},{10... | collective-permute-start | bytes 393224 | tf_op jit(solution)/shard_map/ppermute | solution.py:22
  30.8 9.9 %collective-permute-start.7 = (bf16[256,256]{1,0:T(8,128)(2,1)S(1)}, bf16[256,256]{1,0:T(8,128)(2,1)S(1)}, u32[]{:S(2)}, u32[]{:S(2)}) collective-permute-start(bf16[256,256]{1,0:T(8,128)(2,1)S(1)} %constant_dynamic-update-slice_fusion), channel_id=1, source_target_pairs={{0,8},{8,0},{16,24},{24,16},{1,9},{9,1},{17,25},{25,17},{2,10},{10... | collective-permute-start | bytes 393224 | tf_op jit(solution)/shard_map/ppermute | solution.py:22
  38.8 7.8 %collective-permute-start.13 = (bf16[128,128]{1,0:T(8,128)(2,1)}, bf16[128,128]{1,0:T(8,128)(2,1)S(1)}, u32[]{:S(2)}, u32[]{:S(2)}) collective-permute-start(bf16[128,128]{1,0:T(8,128)(2,1)} %get-tuple-element.40), channel_id=1, source_target_pairs={{0,1},{1,0},{2,3},{3,2},{4,5},{5,4},{6,7},{7,6},{8,9},{9,8},{10,11... | collective-permute-start | bytes 98312 | tf_op jit(solution)/shard_map/ppermute | solution.py:22
  38.8 9.1 %collective-permute-start.14 = (bf16[128,128]{1,0:T(8,128)(2,1)}, bf16[128,128]{1,0:T(8,128)(2,1)S(1)}, u32[]{:S(2)}, u32[]{:S(2)}) collective-permute-start(bf16[128,128]{1,0:T(8,128)(2,1)} %get-tuple-element.41), channel_id=1, source_target_pairs={{0,2},{1,3},{2,0},{3,1},{4,6},{5,7},{6,4},{7,5},{8,10},{9,11},{10,... | collective-permute-start | bytes 98312 | tf_op jit(solution)/shard_map/ppermute | solution.py:22
  38.9 1.8 %copy-start.3 = (bf16[256,256]{1,0:T(8,128)(2,1)}, bf16[256,256]{1,0:T(8,128)(2,1)S(1)}, u32[]{:S(2)}) copy-start(bf16[256,256]{1,0:T(8,128)(2,1)S(1)} %collective-permute-done.9.refs_10_) | copy-start | bytes 393220
  38.9 9.0 %collective-permute-start.15 = (bf16[128,128]{1,0:T(8,128)(2,1)}, bf16[128,128]{1,0:T(8,128)(2,1)S(1)}, u32[]{:S(2)}, u32[]{:S(2)}) collective-permute-start(bf16[128,128]{1,0:T(8,128)(2,1)} %get-tuple-element.42), channel_id=1, source_target_pairs={{0,3},{1,2},{2,1},{3,0},{4,7},{5,6},{6,5},{7,4},{8,11},{9,10},{10,... | collective-permute-start | bytes 98312 | tf_op jit(solution)/shard_map/ppermute | solution.py:22
  40.7 0.7 %copy-start.4 = (bf16[256,256]{1,0:T(8,128)(2,1)}, bf16[256,256]{1,0:T(8,128)(2,1)S(1)}, u32[]{:S(2)}) copy-start(bf16[256,256]{1,0:T(8,128)(2,1)S(1)} %collective-permute-done.8.refs_9_) | copy-start | bytes 393220
  40.7 0.7 %copy-start.5 = (bf16[256,256]{1,0:T(8,128)(2,1)}, bf16[256,256]{1,0:T(8,128)(2,1)S(1)}, u32[]{:S(2)}) copy-start(bf16[256,256]{1,0:T(8,128)(2,1)S(1)} %collective-permute-done.7.refs_8_) | copy-start | bytes 393220
  46.1 1.9 %collective-permute-start.10 = (bf16[128,128]{1,0:T(8,128)(2,1)}, bf16[128,128]{1,0:T(8,128)(2,1)S(1)}, u32[]{:S(2)}, u32[]{:S(2)}) collective-permute-start(bf16[128,128]{1,0:T(8,128)(2,1)} %get-tuple-element.36), channel_id=1, source_target_pairs={{0,1},{1,0},{2,3},{3,2},{4,5},{5,4},{6,7},{7,6},{8,9},{9,8},{10,11... | collective-permute-start | bytes 98312 | tf_op jit(solution)/shard_map/ppermute | solution.py:22
  46.5 4.1 %collective-permute-start.11 = (bf16[128,128]{1,0:T(8,128)(2,1)}, bf16[128,128]{1,0:T(8,128)(2,1)S(1)}, u32[]{:S(2)}, u32[]{:S(2)}) collective-permute-start(bf16[128,128]{1,0:T(8,128)(2,1)} %get-tuple-element.37), channel_id=1, source_target_pairs={{0,2},{1,3},{2,0},{3,1},{4,6},{5,7},{6,4},{7,5},{8,10},{9,11},{10,... | collective-permute-start | bytes 98312 | tf_op jit(solution)/shard_map/ppermute | solution.py:22
  46.6 4.0 %copy-start.10 = (bf16[128,128]{1,0:T(8,128)(2,1)}, bf16[128,128]{1,0:T(8,128)(2,1)S(1)}, u32[]{:S(2)}) copy-start(bf16[128,128]{1,0:T(8,128)(2,1)S(1)} %collective-permute-done.13.refs_5_) | copy-start | bytes 98308
  46.6 4.0 %collective-permute-start.12 = (bf16[128,128]{1,0:T(8,128)(2,1)}, bf16[128,128]{1,0:T(8,128)(2,1)S(1)}, u32[]{:S(2)}, u32[]{:S(2)}) collective-permute-start(bf16[128,128]{1,0:T(8,128)(2,1)} %get-tuple-element.38), channel_id=1, source_target_pairs={{0,3},{1,2},{2,1},{3,0},{4,7},{5,6},{6,5},{7,4},{8,11},{9,10},{10,... | collective-permute-start | bytes 98312 | tf_op jit(solution)/shard_map/ppermute | solution.py:22
  48.0 2.6 %copy-start.11 = (bf16[128,128]{1,0:T(8,128)(2,1)}, bf16[128,128]{1,0:T(8,128)(2,1)S(1)}, u32[]{:S(2)}) copy-start(bf16[128,128]{1,0:T(8,128)(2,1)S(1)} %collective-permute-done.14.refs_6_) | copy-start | bytes 98308
  48.0 2.6 %copy-start.12 = (bf16[128,128]{1,0:T(8,128)(2,1)}, bf16[128,128]{1,0:T(8,128)(2,1)S(1)}, u32[]{:S(2)}) copy-start(bf16[128,128]{1,0:T(8,128)(2,1)S(1)} %collective-permute-done.15.refs_7_) | copy-start | bytes 98308
  48.0 2.6 %copy-start.13 = (bf16[128,128]{1,0:T(8,128)(2,1)}, bf16[128,128]{1,0:T(8,128)(2,1)S(1)}, u32[]{:S(2)}) copy-start(bf16[128,128]{1,0:T(8,128)(2,1)S(1)} %collective-permute-done.10.refs_1_) | copy-start | bytes 98308
  50.6 0.6 %copy-start.14 = (bf16[128,128]{1,0:T(8,128)(2,1)}, bf16[128,128]{1,0:T(8,128)(2,1)S(1)}, u32[]{:S(2)}) copy-start(bf16[128,128]{1,0:T(8,128)(2,1)S(1)} %collective-permute-done.11.refs_2_) | copy-start | bytes 98308
  50.6 0.6 %copy-start.15 = (bf16[128,128]{1,0:T(8,128)(2,1)}, bf16[128,128]{1,0:T(8,128)(2,1)S(1)}, u32[]{:S(2)}) copy-start(bf16[128,128]{1,0:T(8,128)(2,1)S(1)} %collective-permute-done.12.refs_3_) | copy-start | bytes 98308

commit v2 on v1

v2 whole, which is shorter than its diff:
```python
import functools

import jax
import jax.numpy as jnp
from jax import lax
from jax.experimental import pallas as pl
from jax.experimental.pallas import tpu as pltpu
from jax.sharding import PartitionSpec as P

HEADS = 8
HEAD_DIM = 64
SPARSE = 1024
LANES = 128
FAR = 1 << 30
BARRED = -(2.0**100)
F32 = jnp.float32
BF16 = jnp.bfloat16


def exchange(block, axis, distance):
    count = lax.axis_size(axis)
    return lax.ppermute(block, axis, [(i, i ^ distance) for i in range(count)])


def shift_of(value):
    return value.bit_length() - 1


class Plan:
    def __init__(self, rows, inner, outer):
        self.rows = rows
        self.inner = inner
        self.outer = outer
        self.mid = rows * inner // SPARSE
        self.top = self.mid * outer
        self.group = SPARSE // rows
        self.mid_rows = rows // self.mid
        self.top_rows = rows // self.top
        self.top_tile = max(16, self.top_rows)
        assert HEADS == 2 * self.group and 2 * HEAD_DIM == LANES

    def me(self):
        return lax.axis_index("outer") * self.inner + lax.axis_index("inner")

    def pair(self):
        return lax.axis_index("inner") & (self.group - 1)

    def source_row(self, k):
        a = k >> shift_of(self.mid_rows)
        c = (k & (self.mid_rows - 1)) >> shift_of(self.top_rows)
        b = k & (self.top_rows - 1)
        return self.top * b + self.mid * c + a


def dot(a, b, dims):
    return lax.dot_general(a, b, (dims, ((), ())), preferred_element_type=F32)


def pick(wrapped, head, rows):
    return jnp.where(wrapped == ((rows - head) & (rows - 1)), 1.0, 0.0).astype(BF16)


def pack_kernel(plan, slots, q_ref, k_ref, v_ref, *refs):
    rows, n = plan.rows, len(slots)
    outs, (taken, sems) = refs[: 3 * n], refs[3 * n :]
    copies = []
    for s, x in enumerate(slots):
        columns = pl.ds(pl.multiple_of((plan.pair() ^ x) * LANES, LANES), LANES)
        for part, ref in enumerate((q_ref, k_ref, v_ref)):
            copy = pltpu.make_async_copy(
                ref.at[:, columns], taken.at[s, part], sems.at[s, part]
            )
            copy.start()
            copies.append(copy)
    k = lax.broadcasted_iota(jnp.int32, (rows, rows), 0)
    i = lax.broadcasted_iota(jnp.int32, (rows, rows), 1)
    wrapped = (plan.source_row(k) - i) & (rows - 1)
    first = lax.broadcasted_iota(jnp.int32, (rows, LANES), 1) < HEAD_DIM
    for s, x in enumerate(slots):
        pair = plan.pair() ^ x
        one_hot = [pick(wrapped, 2 * pair + t, rows) for t in range(2)]
        for part in range(3):
            copies[3 * s + part].wait()
        block = jnp.concatenate([taken[s, part] for part in range(3)], axis=1)
        one, two = [dot(m, block, ((1,), (0,))) for m in one_hot]
        query = jnp.where(first, one[:, :LANES], two[:, :LANES]) * HEAD_DIM**-0.5
        kv_one = jnp.where(
            first, one[:, LANES : 2 * LANES], pltpu.roll(one[:, 2 * LANES :], HEAD_DIM, axis=1)
        ).astype(BF16)
        kv_two = jnp.where(
            first, pltpu.roll(two[:, 2 * LANES :], HEAD_DIM, axis=1), two[:, LANES : 2 * LANES]
        ).astype(BF16)
        lead, second, mid = outs[3 * s : 3 * s + 3]
        lead[:, :LANES] = query.astype(BF16)
        lead[:, LANES:] = kv_one
        second[...] = kv_two
        mid[:, :LANES] = kv_one[: plan.mid_rows]
        mid[:, LANES:] = kv_two[: plan.mid_rows]


def features(plan, table_ref, t, base, slot_shift, count):
    r = lax.broadcasted_iota(jnp.int32, (count, LANES), 0)
    lane = lax.broadcasted_iota(jnp.int32, (count, LANES), 1)
    head = 2 * plan.pair() + t
    source = plan.me() ^ (base + (r >> slot_shift))
    k = r & ((1 << slot_shift) - 1)
    position = source * plan.rows + ((plan.source_row(k) + head) & (plan.rows - 1))
    starts = table_ref[2 * t : 2 * t + 1, :]
    ends = table_ref[2 * t + 1 : 2 * t + 2, :]
    inside = (position >= starts) & (position < ends)
    own = (lane < HEAD_DIM) if t == 0 else (lane >= HEAD_DIM)
    return inside, own


def as_query(block, inside, own):
    return jnp.where(own, block.astype(F32), jnp.where(inside, BARRED, 0.0)).astype(BF16)


def as_key(block, inside, own):
    return jnp.where(own, block.astype(F32), jnp.where(inside, 0.0, 1.0)).astype(BF16)


def as_value(block, own):
    return jnp.where(own, 1.0, block.astype(F32))


def row_iota(count):
    return lax.broadcasted_iota(jnp.int32, (count, LANES), 0)


def share(sums):
    return pltpu.roll(sums, HEAD_DIM, axis=1) / sums


def local_kernel(plan, t, table_ref, *refs):
    rows, group, mid_rows, tile = plan.rows, plan.group, plan.mid_rows, plan.top_tile
    leads, refs = refs[:group], refs[group:]
    if t:
        seconds, before, refs = refs[:group], refs[group], refs[group + 1 :]
        rests, refs = refs[:group], refs[group:]
    else:
        rest, refs = refs[0], refs[1:]
    sums_ref, maxima_ref, q_s, k_s, v_s, v2_s, vt_s = refs
    row = row_iota(rows)
    for x in range(group):
        here = pl.ds(x * rows, rows)
        inside, own = features(plan, table_ref, t, x, shift_of(rows), rows)
        kv = seconds[x][...] if t else leads[x][:, LANES:]
        q_s[here, :] = as_query(leads[x][:, :LANES], inside, own)
        k_s[here, :] = as_key(kv, inside, own)
        value = as_value(kv, own)
        v_s[here, :] = value.astype(BF16)
        v2_s[here, :] = jnp.where(row < mid_rows, 2.0 * value, value).astype(BF16)
        vt_s[here, :] = jnp.where(row < plan.top_rows, value, 0.0).astype(BF16)
    lane = lax.broadcasted_iota(jnp.int32, (rows - mid_rows, LANES), 1)
    for x in range(group):
        here = pl.ds(x * rows, rows)
        mid_here = pl.ds(x * mid_rows, mid_rows)
        rest_here = pl.ds(x * (rows - mid_rows), rows - mid_rows)
        scores = dot(q_s[here, :], k_s[...], ((1,), (1,)))
        largest = jnp.max(scores, axis=1, keepdims=True)
        probs = jnp.exp(scores - largest).astype(BF16)
        mid_sum = dot(probs[:mid_rows], v2_s[...], ((1,), (0,)))
        top_sum = dot(probs[:tile], vt_s[...], ((1,), (0,)))
        rest_sum = share(dot(probs[mid_rows:], v_s[...], ((1,), (0,))))
        top_sum = jnp.where(row_iota(tile) < plan.top_rows, top_sum, 0.0)
        sums_ref[mid_here, :] = mid_sum
        sums_ref[pl.ds(x * mid_rows, tile), :] += top_sum
        maxima_ref[mid_here, :] = jnp.broadcast_to(largest[:mid_rows], (mid_rows, LANES))
        if t:
            both = jnp.where(lane < HEAD_DIM, before[rest_here, :], rest_sum)
            rests[x][...] = both.astype(BF16)
        else:
            rest[rest_here, :] = rest_sum


def mid_kernel(plan, table_ref, *refs):
    group, mid_rows, tile = plan.group, plan.mid_rows, plan.top_tile
    states, refs = refs[:4], refs[4:]
    leads, refs = refs[:group], refs[group:]
    rests, refs = refs[:group], refs[group:]
    mids, refs = refs[: plan.inner - group], refs[plan.inner - group :]
    outs, lead_states = refs[:group], refs[group:]
    count = group * mid_rows
    queries = jnp.concatenate([lead[:mid_rows, :LANES] for lead in leads], axis=0)
    results = []
    for t in range(2):
        inside, own = features(plan, table_ref, t, 0, shift_of(mid_rows), count)
        q = as_query(queries, inside, own)
        kv = jnp.concatenate([mid[:, t * LANES : (t + 1) * LANES] for mid in mids], axis=0)
        n = kv.shape[0]
        inside, own = features(plan, table_ref, t, group, shift_of(mid_rows), n)
        value = as_value(kv, own)
        is_top = (row_iota(n) & (mid_rows - 1)) < plan.top_rows
        top_value = jnp.where(is_top, value, 0.0).astype(BF16)
        old = states[2 * t + 1][:, :1]
        scores = dot(q, as_key(kv, inside, own), ((1,), (1,)))
        new = jnp.maximum(old, jnp.max(scores, axis=1, keepdims=True))
        probs = jnp.exp(scores - new).astype(BF16)
        sums = states[2 * t][...] * jnp.exp(old - new)
        sums = sums + dot(probs, value.astype(BF16), ((1,), (0,)))

        def leading(array):
            return jnp.concatenate(
                [array[x * mid_rows : x * mid_rows + tile] for x in range(group)], axis=0
            )

        extra = dot(leading(probs), top_value, ((1,), (0,)))
        lead_states[3 * t][...] = leading(sums) + extra
        lead_states[3 * t + 1][...] = jnp.broadcast_to(leading(new), (group * tile, LANES))
        lead_states[3 * t + 2][...] = leading(q)
        if plan.top_rows < tile:
            keep = (row_iota(group * tile) & (tile - 1)) < plan.top_rows
            lead_states[3 * t][...] = leading(sums) + jnp.where(keep, extra, 0.0)
        results.append(share(sums))
    lane = lax.broadcasted_iota(jnp.int32, (count, LANES), 1)
    both = jnp.where(lane < HEAD_DIM, results[0], results[1]).astype(BF16)
    for x in range(group):
        outs[x][: mid_rows - tile] = both[x * mid_rows + tile : (x + 1) * mid_rows]
        outs[x][mid_rows - tile :] = rests[x][...]


def top_kernel(plan, table_ref, *refs):
    group, tile = plan.group, plan.top_tile
    states, refs = refs[:6], refs[6:]
    tops, outs = refs[: plan.outer - 1], refs[plan.outer - 1 :]
    count = group * tile
    shift = shift_of(plan.top_rows)
    is_top = (row_iota(count) & (tile - 1)) < plan.top_rows
    results = []
    for t in range(2):
        keys, values = [], []
        for e in range(1, plan.outer):
            kv = tops[e - 1][:, t * LANES : (t + 1) * LANES]
            inside, own = features(plan, table_ref, t, e * plan.inner, shift, kv.shape[0])
            keys.append(as_key(kv, inside, own))
            values.append(as_value(kv, own).astype(BF16))
        sums, old, q = states[3 * t][...], states[3 * t + 1][:, :1], states[3 * t + 2][...]
        scores = dot(q, jnp.concatenate(keys, axis=0), ((1,), (1,)))
        new = jnp.maximum(old, jnp.max(scores, axis=1, keepdims=True))
        probs = jnp.exp(scores - new).astype(BF16)
        merged = sums * jnp.exp(old - new)
        merged = merged + dot(probs, jnp.concatenate(values, axis=0), ((1,), (0,)))
        results.append(share(jnp.where(is_top, merged, sums)))
    lane = lax.broadcasted_iota(jnp.int32, (count, LANES), 1)
    both = jnp.where(lane < HEAD_DIM, results[0], results[1]).astype(BF16)
    for x in range(group):
        outs[x][...] = both[x * tile : (x + 1) * tile]


def project_kernel(plan, weight_ref, *refs):
    rows, group = plan.rows, plan.group
    tops, mids, (out_ref, flat) = refs[:group], refs[group : 2 * group], refs[2 * group :]
    i = lax.broadcasted_iota(jnp.int32, (rows, rows), 0)
    k = lax.broadcasted_iota(jnp.int32, (rows, rows), 1)
    wrapped = (plan.source_row(k) - i) & (rows - 1)
    lane = lax.broadcasted_iota(jnp.int32, (rows, LANES), 1)
    for x in range(group):
        pair = plan.pair() ^ x
        block = jnp.concatenate([tops[x][...], mids[x][...]], axis=0)
        one = dot(pick(wrapped, 2 * pair, rows), block, ((1,), (0,)))
        two = dot(pick(wrapped, 2 * pair + 1, rows), block, ((1,), (0,)))
        columns = pl.ds(pl.multiple_of(pair * LANES, LANES), LANES)
        flat[:, columns] = jnp.where(lane < HEAD_DIM, one, two).astype(BF16)
    out_ref[...] = dot(flat[...], weight_ref[...], ((1,), (0,))).astype(BF16)


def slide_table(slide_lengths):
    slides = slide_lengths.shape[0]
    lane = jnp.arange(LANES, dtype=jnp.int32)
    index = jnp.arange(slides, dtype=jnp.int32)
    table = []
    for t in range(2):
        slide = lane - (HEAD_DIM if t == 0 else 0)
        valid = (slide >= 0) & (slide < slides)
        for bound in range(2):
            before = index[None, :] < (slide + bound)[:, None]
            total = jnp.sum(jnp.where(before, slide_lengths[None, :], 0), axis=1)
            table.append(jnp.where(valid, total, FAR))
    return jnp.stack(table + table, axis=0).astype(jnp.int32)


def shape(count, width, kind=BF16):
    return jax.ShapeDtypeStruct((count, width), kind)


def call(kernel, operands, results, scratch=(), in_specs=None):
    vmem = pl.BlockSpec(memory_space=pltpu.VMEM)
    return pl.pallas_call(
        kernel,
        in_specs=in_specs or [vmem] * len(operands),
        out_specs=[vmem] * len(results),
        out_shape=results,
        scratch_shapes=scratch,
        compiler_params=pltpu.CompilerParams(vmem_limit_bytes=24 << 20),
    )(*operands)


def shards(queries, keys, values, out_weight, slide_lengths):
    plan = Plan(queries.shape[0], lax.axis_size("inner"), lax.axis_size("outer"))
    rows, group, mid_rows, tile = plan.rows, plan.group, plan.mid_rows, plan.top_tile
    table = slide_table(slide_lengths)

    held = [pltpu.with_memory_space_constraint(a, pltpu.HBM) for a in (queries, keys, values)]
    leads, seconds, mids = [None] * group, [None] * group, [None] * group
    for slots in (list(range(group // 2, group)), list(range(group // 2))):
        packed = call(
            functools.partial(pack_kernel, plan, slots),
            held,
            [shape(rows, 2 * LANES), shape(rows, LANES), shape(mid_rows, 2 * LANES)] * len(slots),
            [pltpu.VMEM((len(slots), 3, rows, LANES), BF16), pltpu.SemaphoreType.DMA((len(slots), 3))],
            [pl.BlockSpec(memory_space=pltpu.HBM)] * 3,
        )
        for s, x in enumerate(slots):
            leads[x], seconds[x], mids[x] = packed[3 * s : 3 * s + 3]
    leads = [leads[0]] + [exchange(leads[x], "inner", x) for x in range(1, group)]
    seconds = [seconds[0]] + [exchange(seconds[x], "inner", x) for x in range(1, group)]
    others = [exchange(mids[x & (group - 1)], "inner", x) for x in range(group, plan.inner)]

    own = jnp.concatenate(
        [
            jnp.concatenate([leads[x][: plan.top_rows, LANES:], seconds[x][: plan.top_rows]], axis=1)
            for x in range(group)
        ]
        + [other[: plan.top_rows] for other in others],
        axis=0,
    )
    tops = [exchange(own, "outer", x) for x in range(1, plan.outer)]

    count = group * rows
    scratch = [pltpu.VMEM((count, LANES), BF16)] * 5
    state = [shape(group * mid_rows, LANES, F32)] * 2
    rest_one, sums_one, maxima_one = call(
        functools.partial(local_kernel, plan, 0),
        (table, *leads),
        [shape(group * (rows - mid_rows), LANES, F32), *state],
        scratch,
    )
    *rests, sums_two, maxima_two = call(
        functools.partial(local_kernel, plan, 1),
        (table, *leads, *seconds, rest_one),
        [shape(rows - mid_rows, LANES)] * group + state,
        scratch,
    )
    lead_state = [shape(group * tile, LANES, F32)] * 2 + [shape(group * tile, LANES)]
    middle = call(
        functools.partial(mid_kernel, plan),
        (table, sums_one, maxima_one, sums_two, maxima_two, *leads, *rests, *others),
        [shape(rows - tile, LANES)] * group + lead_state * 2,
    )
    middles, lead_state = middle[:group], middle[group:]
    uppers = call(
        functools.partial(top_kernel, plan),
        (table, *lead_state, *tops),
        [shape(tile, LANES)] * group,
    )
    back = []
    for parts in (uppers, middles):
        back += [parts[0]] + [exchange(parts[x], "inner", x) for x in range(1, group)]
    return call(
        functools.partial(project_kernel, plan),
        (out_weight, *back),
        [shape(rows, out_weight.shape[1])],
        [pltpu.VMEM((rows, HEADS * HEAD_DIM), BF16)],
    )[0]


def solution(mesh):
    tokens = P(("outer", "inner"), None)

    return jax.shard_map(
        shards,
        mesh=mesh,
        in_specs=(tokens, tokens, tokens, P(), P()),
        out_specs=tokens,
        check_vma=False,
    )
```

time: 54.3 us -> 47.8 us (0.88)
  waiting for transfers between devices: 18.8 us -> 12.1 us
  starting transfers between devices: 15.3 us -> 21.2 us
  Pallas kernels: 16.9 us -> 13.4 us
  local copies, waits for them, and re-layouts: 2.66 us -> 0.71 us
    ppermute x16 -> x19, waiting for transfers between devices: 18.8 us -> 12.1 us  [exchange(): return lax.ppermute(block, axis, [(i, i ^ distance) for i in range(count)])]
    ppermute x16 -> x19, starting transfers between devices: 15.3 us -> 21.2 us  [exchange(): return lax.ppermute(block, axis, [(i, i ^ distance) for i in range(count)])]
    pallas_call x4 -> x7, Pallas kernels: 16.9 us -> 13.4 us  [call(): pl.pallas_call(kernel, in_specs=in_specs or [vmem] * len(operands), out_s...]
    unnamed x41 -> x7, local copies, waits for them, and re-layouts: 2.05 us -> 0.67 us
    another operation x1, local copies, waits for them, and re-layouts: 0.61 us -> 0.03 us  [slide_table(): return jnp.stack(table + table, axis=0).astype(jnp.int32)]
  transfers between devices with their start and end apart: 16 -> 19, of which waited for: 4 -> 5; matrix products, arithmetic and copies ran while one was open for 3% -> 0% of each run, Pallas kernels for 21% -> 21%
where the time goes in v2:
time: 47.8 us; the launch traced here: 47.6 us
  starting transfers between devices  21.2 us (44%)
  Pallas kernels  13.4 us (28%)
  waiting for transfers between devices  12.1 us (25%)
  local copies, waits for them, and re-layouts  0.71 us (1%)
    ppermute x19, starting transfers between devices, exchange(): return lax.ppermute(block, axis, [(i, i ^ distance) for i in range(count)])  21.2 us
    pallas_call x7, Pallas kernels, call(): pl.pallas_call(kernel, in_specs=in_specs or [vmem] * len(operands), out_s...  13.4 us
    ppermute x19, waiting for transfers between devices, exchange(): return lax.ppermute(block, axis, [(i, i ^ distance) for i in range(count)])  12.1 us
  transfers between devices with their start and end apart: 19, of which 5 were waited for; matrix products, arithmetic and copies ran while one was open for 0% of the time, Pallas kernels for 21%

profile of v2, /device:TPU:0, one launch (start us, length us, event | category | flops | bytes accessed | tf_op | source)
XLA Modules:
  0.0 47.6 jit_solution(18083701705497399962)
XLA Ops:
  0.0 1.7 %shard_map.55 = (bf16[256,256]{1,0:T(8,128)(2,1)S(1)}, bf16[256,128]{1,0:T(8,128)(2,1)S(1)}, bf16[128,256]{1,0:T(8,128)(2,1)S(1)}, bf16[256,256]{1,0:T(8,128)(2,...) custom-call(bf16[256,512]{1,0:T(8,128)(2,1)} %q_ref.3, bf16[256,512]{1,0:T(8,128)(2,1)} %k_ref.3, ...), custom_call_target="tpu_custom_call" | custom-call | tf_op jit(solution)/shard_map/pallas_call | solution.py:289
  1.7 0.6 %collective-permute-start = (bf16[256,256]{1,0:T(8,128)(2,1)S(1)}, bf16[256,256]{1,0:T(8,128)(2,1)S(1)}, u32[]{:S(2)}, u32[]{:S(2)}) collective-permute-start(bf16[256,256]{1,0:T(8,128)(2,1)S(1)} %get-tuple-element.41), channel_id=1, source_target_pairs={{0,1},{1,0},{2,3},{3,2},{4,5},{5,4},{6,7},{7,6},{8,9},{9,8},{10,11... | collective-permute-start | bytes 393224 | tf_op jit(solution)/shard_map/ppermute | solution.py:22
  2.3 1.7 %shard_map.56 = (bf16[256,256]{1,0:T(8,128)(2,1)S(1)}, bf16[256,128]{1,0:T(8,128)(2,1)S(1)}, bf16[128,256]{1,0:T(8,128)(2,1)S(1)}, bf16[256,256]{1,0:T(8,128)(2,...) custom-call(bf16[256,512]{1,0:T(8,128)(2,1)} %q_ref.3, bf16[256,512]{1,0:T(8,128)(2,1)} %k_ref.3, ...), custom_call_target="tpu_custom_call" | custom-call | tf_op jit(solution)/shard_map/pallas_call | solution.py:289
  4.0 2.6 %collective-permute-start.1 = (bf16[256,256]{1,0:T(8,128)(2,1)S(1)}, bf16[256,256]{1,0:T(8,128)(2,1)S(1)}, u32[]{:S(2)}, u32[]{:S(2)}) collective-permute-start(bf16[256,256]{1,0:T(8,128)(2,1)S(1)} %get-tuple-element.42), channel_id=1, source_target_pairs={{0,2},{1,3},{2,0},{3,1},{4,6},{5,7},{6,4},{7,5},{8,10},{9,11},{10,... | collective-permute-start | bytes 393224 | tf_op jit(solution)/shard_map/ppermute | solution.py:22
  6.6 0.2 collective-permute-start.3
  6.9 0.4 collective-permute-start.4
  7.2 1.3 %collective-permute-start.5 = (bf16[256,128]{1,0:T(8,128)(2,1)S(1)}, bf16[256,128]{1,0:T(8,128)(2,1)S(1)}, u32[]{:S(2)}, u32[]{:S(2)}) collective-permute-start(bf16[256,128]{1,0:T(8,128)(2,1)S(1)} %get-tuple-element.49), channel_id=1, source_target_pairs={{0,3},{1,2},{2,1},{3,0},{4,7},{5,6},{6,5},{7,4},{8,11},{9,10},{10,... | collective-permute-start | bytes 196616 | tf_op jit(solution)/shard_map/ppermute | solution.py:22
  8.5 0.6 %copy-done.1 = s32[16]{0:T(128)S(1)} copy-done((s32[16]{0:T(128)S(1)}, s32[16]{0:T(128)}, u32[]{:S(2)}) %copy-start.1) | copy-done | bytes 88
  9.2 0.1 select_reduce_fusion
  9.3 0.0 collective-permute-done.3.refs_5_
  9.3 0.5 %collective-permute-start.2 = (bf16[256,256]{1,0:T(8,128)(2,1)S(1)}, bf16[256,256]{1,0:T(8,128)(2,1)S(1)}, u32[]{:S(2)}, u32[]{:S(2)}) collective-permute-start(bf16[256,256]{1,0:T(8,128)(2,1)S(1)} %get-tuple-element.43), channel_id=1, source_target_pairs={{0,3},{1,2},{2,1},{3,0},{4,7},{5,6},{6,5},{7,4},{8,11},{9,10},{10,... | collective-permute-start | bytes 393224 | tf_op jit(solution)/shard_map/ppermute | solution.py:22
  9.8 2.6 %collective-permute-done.4.refs_6_ = bf16[256,128]{1,0:T(8,128)(2,1)S(1)} collective-permute-done((bf16[256,128]{1,0:T(8,128)(2,1)S(1)}, bf16[256,128]{1,0:T(8,128)(2,1)S(1)}, u32[]{:S(2)}, u32[]{:S(2)}) %collective-permute-start.4) | collective-permute-done | bytes 65568 | tf_op jit(solution)/shard_map/ppermute | solution.py:22
  12.4 3.0 %collective-permute-start.6 = (bf16[128,256]{1,0:T(8,128)(2,1)S(1)}, bf16[128,256]{1,0:T(8,128)(2,1)S(1)}, u32[]{:S(2)}, u32[]{:S(2)}) collective-permute-start(bf16[128,256]{1,0:T(8,128)(2,1)S(1)} %get-tuple-element.57), channel_id=1, source_target_pairs={{0,4},{1,5},{2,6},{3,7},{4,0},{5,1},{6,2},{7,3},{8,12},{9,13},{10,... | collective-permute-start | bytes 196616 | tf_op jit(solution)/shard_map/ppermute | solution.py:22
  15.4 0.0 collective-permute-done.5.refs_7_
  15.4 1.1 %collective-permute-start.7 = (bf16[128,256]{1,0:T(8,128)(2,1)S(1)}, bf16[128,256]{1,0:T(8,128)(2,1)S(1)}, u32[]{:S(2)}, u32[]{:S(2)}) collective-permute-start(bf16[128,256]{1,0:T(8,128)(2,1)S(1)} %get-tuple-element.58), channel_id=1, source_target_pairs={{0,5},{1,4},{2,7},{3,6},{4,1},{5,0},{6,3},{7,2},{8,13},{9,12},{10,... | collective-permute-start | bytes 196616 | tf_op jit(solution)/shard_map/ppermute | solution.py:22
  16.6 0.0 collective-permute-done.refs_1_.refs_5_
  16.6 1.3 %collective-permute-start.8 = (bf16[128,256]{1,0:T(8,128)(2,1)S(1)}, bf16[128,256]{1,0:T(8,128)(2,1)S(1)}, u32[]{:S(2)}, u32[]{:S(2)}) collective-permute-start(bf16[128,256]{1,0:T(8,128)(2,1)S(1)} %get-tuple-element.59), channel_id=1, source_target_pairs={{0,6},{1,7},{2,4},{3,5},{4,2},{5,3},{6,0},{7,1},{8,14},{9,15},{10,... | collective-permute-start | bytes 196616 | tf_op jit(solution)/shard_map/ppermute | solution.py:22
  17.9 0.0 collective-permute-done.1.refs_2_.refs_6_
  17.9 1.4 %collective-permute-start.9 = (bf16[128,256]{1,0:T(8,128)(2,1)S(1)}, bf16[128,256]{1,0:T(8,128)(2,1)S(1)}, u32[]{:S(2)}, u32[]{:S(2)}) collective-permute-start(bf16[128,256]{1,0:T(8,128)(2,1)S(1)} %get-tuple-element.60), channel_id=1, source_target_pairs={{0,7},{1,6},{2,5},{3,4},{4,3},{5,2},{6,1},{7,0},{8,15},{9,14},{10,... | collective-permute-start | bytes 196616 | tf_op jit(solution)/shard_map/ppermute | solution.py:22
  19.3 0.0 collective-permute-done.2.refs_3_.refs_7_
  19.3 0.0 collective-permute-done.6.refs_12_
  19.3 6.4 %collective-permute-done.7.refs_13_ = bf16[128,256]{1,0:T(8,128)(2,1)S(1)} collective-permute-done((bf16[128,256]{1,0:T(8,128)(2,1)S(1)}, bf16[128,256]{1,0:T(8,128)(2,1)S(1)}, u32[]{:S(2)}, u32[]{:S(2)}) %collective-permute-start.7) | collective-permute-done | bytes 65568 | tf_op jit(solution)/shard_map/ppermute | solution.py:22
  25.7 0.0 collective-permute-done.8.refs_14_
  25.7 0.0 collective-permute-done.9.refs_15_
  25.8 1.6 %collective-permute-start.10 = (bf16[256,256]{1,0:T(8,128)(2,1)S(1)}, bf16[256,256]{1,0:T(8,128)(2,1)S(1)}, u32[]{:S(2)}, u32[]{:S(2)}) collective-permute-start(bf16[256,256]{1,0:T(8,128)(2,1)S(1)} %constant_dynamic-update-slice_fusion), channel_id=1, source_target_pairs={{0,8},{8,0},{16,24},{24,16},{1,9},{9,1},{17,25},{25,17},{2,10},{10... | collective-permute-start | bytes 393224 | tf_op jit(solution)/shard_map/ppermute | solution.py:22
  27.3 1.5 %collective-permute-start.11 = (bf16[256,256]{1,0:T(8,128)(2,1)S(1)}, bf16[256,256]{1,0:T(8,128)(2,1)S(1)}, u32[]{:S(2)}, u32[]{:S(2)}) collective-permute-start(bf16[256,256]{1,0:T(8,128)(2,1)S(1)} %constant_dynamic-update-slice_fusion), channel_id=1, source_target_pairs={{0,16},{8,24},{16,0},{24,8},{1,17},{9,25},{17,1},{25,9},{2,18},{10... | collective-permute-start | bytes 393224 | tf_op jit(solution)/shard_map/ppermute | solution.py:22
  28.8 0.5 collective-permute-start.12
  29.3 2.6 %shard_map.57 = (f32[512,128]{1,0:T(8,128)S(1)}, f32[512,128]{1,0:T(8,128)S(1)}, f32[512,128]{1,0:T(8,128)S(1)}) custom-call(s32[8,128]{1,0:T(8,128)S(1)} %stack.2.table_ref, bf16[256,256]{1,0:T(8,128)(2,1)S(1)} %get-tuple-element.40.refs_0_.refs_4_, bf16[256,256]{1,0:T(8,128)(2,1)S(1)} %collective-permute-done.refs_1_.refs_5_, ...), custom_call_target="tpu_custom_call" | custom-call | tf_op jit(solution)/shard_map/pallas_call | solution.py:289
  31.9 2.6 %shard_map.58 = (bf16[128,128]{1,0:T(8,128)(2,1)S(1)}, bf16[128,128]{1,0:T(8,128)(2,1)S(1)}, bf16[128,128]{1,0:T(8,128)(2,1)S(1)}, bf16[128,128]{1,0:T(8,128)(2,...) custom-call(s32[8,128]{1,0:T(8,128)S(1)} %stack.2.table_ref, ...), custom_call_target="tpu_custom_call" | custom-call | tf_op jit(solution)/shard_map/pallas_call | solution.py:289
  34.5 0.0 copy-start
  34.6 1.9 %shard_map.59 = (bf16[224,128]{1,0:T(8,128)(2,1)S(1)}, bf16[224,128]{1,0:T(8,128)(2,1)S(1)}, bf16[224,128]{1,0:T(8,128)(2,1)S(1)}, bf16[224,128]{1,0:T(8,128)(2,...) custom-call(s32[8,128]{1,0:T(8,128)S(1)} %stack.2.table_ref, ...), custom_call_target="tpu_custom_call" | custom-call | tf_op jit(solution)/shard_map/pallas_call | solution.py:289
  36.5 0.1 collective-permute-start.16
  36.6 2.9 %collective-permute-start.17 = (bf16[224,128]{1,0:T(8,128)(2,1)S(1)}, bf16[224,128]{1,0:T(8,128)(2,1)S(1)}, u32[]{:S(2)}, u32[]{:S(2)}) collective-permute-start(bf16[224,128]{1,0:T(8,128)(2,1)S(1)} %get-tuple-element.73), channel_id=1, source_target_pairs={{0,2},{1,3},{2,0},{3,1},{4,6},{5,7},{6,4},{7,5},{8,10},{9,11},{10,... | collective-permute-start | bytes 172040 | tf_op jit(solution)/shard_map/ppermute | solution.py:22
  39.5 0.0 collective-permute-done.10.refs_6_
  39.5 0.0 collective-permute-start.18
  39.5 0.0 collective-permute-done.11.refs_7_
  39.5 0.0 collective-permute-done.12.refs_8_
  39.5 1.2 %shard_map.60 = (bf16[32,128]{1,0:T(8,128)(2,1)S(1)}, bf16[32,128]{1,0:T(8,128)(2,1)S(1)}, bf16[32,128]{1,0:T(8,128)(2,1)S(1)}, bf16[32,128]{1,0:T(8,128)(2,1)S(1)}) custom-call(s32[8,128]{1,0:T(8,128)S(1)} %stack.2.table_ref, f32[128,128]{1,0:T(8,128)S(1)} %get-tuple-element.61.refs_0_, f32[128,128]{1,0:T(8,128)S(1)} %get-tuple-element.62.refs_1_, ...), custom_call_target="tpu_custom_call" | custom-call | tf_op jit(solution)/shard_map/pallas_call | solution.py:289
  40.7 0.2 collective-permute-start.13
  40.9 1.9 %collective-permute-start.14 = (bf16[32,128]{1,0:T(8,128)(2,1)S(1)}, bf16[32,128]{1,0:T(8,128)(2,1)S(1)}, u32[]{:S(2)}, u32[]{:S(2)}) collective-permute-start(bf16[32,128]{1,0:T(8,128)(2,1)S(1)} %get-tuple-element.69), channel_id=1, source_target_pairs={{0,2},{1,3},{2,0},{3,1},{4,6},{5,7},{6,4},{7,5},{8,10},{9,11},{10,... | collective-permute-start | bytes 24584 | tf_op jit(solution)/shard_map/ppermute | solution.py:22
  42.9 0.0 collective-permute-done.16.refs_5_
  42.9 0.0 collective-permute-start.15
  42.9 0.0 collective-permute-done.17.refs_6_
  42.9 0.5 collective-permute-done.18.refs_7_
  43.4 0.0 collective-permute-done.13.refs_1_
  43.4 1.2 %collective-permute-done.14.refs_2_ = bf16[32,128]{1,0:T(8,128)(2,1)S(1)} collective-permute-done((bf16[32,128]{1,0:T(8,128)(2,1)S(1)}, bf16[32,128]{1,0:T(8,128)(2,1)S(1)}, u32[]{:S(2)}, u32[]{:S(2)}) %collective-permute-start.14) | collective-permute-done | bytes 8224 | tf_op jit(solution)/shard_map/ppermute | solution.py:22
  44.6 1.4 %collective-permute-done.15.refs_3_ = bf16[32,128]{1,0:T(8,128)(2,1)S(1)} collective-permute-done((bf16[32,128]{1,0:T(8,128)(2,1)S(1)}, bf16[32,128]{1,0:T(8,128)(2,1)S(1)}, u32[]{:S(2)}, u32[]{:S(2)}) %collective-permute-start.15) | collective-permute-done | bytes 8224 | tf_op jit(solution)/shard_map/ppermute | solution.py:22
  46.0 1.6 %shard_map.61 = bf16[256,768]{1,0:T(8,128)(2,1)} custom-call(bf16[512,768]{1,0:T(8,128)(2,1)S(1)} %copy-done, bf16[32,128]{1,0:T(8,128)(2,1)S(1)} %get-tuple-element.67.refs_0_, bf16[32,128]{1,0:T(8,128)(2,1)S(1)} %collective-permute-done.13.refs_1_, bf16[32,128]{1,0:T(8,128)(2,1)S(1)} %collective-permute-done.14.refs_2_, ...), custom_call_target="tpu_custom_call" | custom-call | tf_op jit(solution)/shard_map/pallas_call | solution.py:289
  (24 shorter events, 0.1 us)
Async XLA Ops:
  1.7 14.8 %collective-permute-start = (bf16[256,256]{1,0:T(8,128)(2,1)S(1)}, bf16[256,256]{1,0:T(8,128)(2,1)S(1)}, u32[]{:S(2)}, u32[]{:S(2)}) collective-permute-start(bf16[256,256]{1,0:T(8,128)(2,1)S(1)} %get-tuple-element.41), channel_id=1, source_target_pairs={{0,1},{1,0},{2,3},{3,2},{4,5},{5,4},{6,7},{7,6},{8,9},{9,8},{10,11... | collective-permute-start | bytes 393224 | tf_op jit(solution)/shard_map/ppermute | solution.py:22
  4.0 13.9 %collective-permute-start.1 = (bf16[256,256]{1,0:T(8,128)(2,1)S(1)}, bf16[256,256]{1,0:T(8,128)(2,1)S(1)}, u32[]{:S(2)}, u32[]{:S(2)}) collective-permute-start(bf16[256,256]{1,0:T(8,128)(2,1)S(1)} %get-tuple-element.42), channel_id=1, source_target_pairs={{0,2},{1,3},{2,0},{3,1},{4,6},{5,7},{6,4},{7,5},{8,10},{9,11},{10,... | collective-permute-start | bytes 393224 | tf_op jit(solution)/shard_map/ppermute | solution.py:22
  6.6 2.6 %collective-permute-start.3 = (bf16[256,128]{1,0:T(8,128)(2,1)S(1)}, bf16[256,128]{1,0:T(8,128)(2,1)S(1)}, u32[]{:S(2)}, u32[]{:S(2)}) collective-permute-start(bf16[256,128]{1,0:T(8,128)(2,1)S(1)} %get-tuple-element.47), channel_id=1, source_target_pairs={{0,1},{1,0},{2,3},{3,2},{4,5},{5,4},{6,7},{7,6},{8,9},{9,8},{10,11... | collective-permute-start | bytes 196616 | tf_op jit(solution)/shard_map/ppermute | solution.py:22
  6.9 5.5 %collective-permute-start.4 = (bf16[256,128]{1,0:T(8,128)(2,1)S(1)}, bf16[256,128]{1,0:T(8,128)(2,1)S(1)}, u32[]{:S(2)}, u32[]{:S(2)}) collective-permute-start(bf16[256,128]{1,0:T(8,128)(2,1)S(1)} %get-tuple-element.48), channel_id=1, source_target_pairs={{0,2},{1,3},{2,0},{3,1},{4,6},{5,7},{6,4},{7,5},{8,10},{9,11},{10,... | collective-permute-start | bytes 196616 | tf_op jit(solution)/shard_map/ppermute | solution.py:22
  7.2 8.2 %collective-permute-start.5 = (bf16[256,128]{1,0:T(8,128)(2,1)S(1)}, bf16[256,128]{1,0:T(8,128)(2,1)S(1)}, u32[]{:S(2)}, u32[]{:S(2)}) collective-permute-start(bf16[256,128]{1,0:T(8,128)(2,1)S(1)} %get-tuple-element.49), channel_id=1, source_target_pairs={{0,3},{1,2},{2,1},{3,0},{4,7},{5,6},{6,5},{7,4},{8,11},{9,10},{10,... | collective-permute-start | bytes 196616 | tf_op jit(solution)/shard_map/ppermute | solution.py:22
  8.5 0.7 %copy-start.1 = (s32[16]{0:T(128)S(1)}, s32[16]{0:T(128)}, u32[]{:S(2)}) copy-start(s32[16]{0:T(128)} %param.9) | copy-start | bytes 196
  9.3 10.0 %collective-permute-start.2 = (bf16[256,256]{1,0:T(8,128)(2,1)S(1)}, bf16[256,256]{1,0:T(8,128)(2,1)S(1)}, u32[]{:S(2)}, u32[]{:S(2)}) collective-permute-start(bf16[256,256]{1,0:T(8,128)(2,1)S(1)} %get-tuple-element.43), channel_id=1, source_target_pairs={{0,3},{1,2},{2,1},{3,0},{4,7},{5,6},{6,5},{7,4},{8,11},{9,10},{10,... | collective-permute-start | bytes 393224 | tf_op jit(solution)/shard_map/ppermute | solution.py:22
  12.4 6.9 %collective-permute-start.6 = (bf16[128,256]{1,0:T(8,128)(2,1)S(1)}, bf16[128,256]{1,0:T(8,128)(2,1)S(1)}, u32[]{:S(2)}, u32[]{:S(2)}) collective-permute-start(bf16[128,256]{1,0:T(8,128)(2,1)S(1)} %get-tuple-element.57), channel_id=1, source_target_pairs={{0,4},{1,5},{2,6},{3,7},{4,0},{5,1},{6,2},{7,3},{8,12},{9,13},{10,... | collective-permute-start | bytes 196616 | tf_op jit(solution)/shard_map/ppermute | solution.py:22
  15.4 10.3 %collective-permute-start.7 = (bf16[128,256]{1,0:T(8,128)(2,1)S(1)}, bf16[128,256]{1,0:T(8,128)(2,1)S(1)}, u32[]{:S(2)}, u32[]{:S(2)}) collective-permute-start(bf16[128,256]{1,0:T(8,128)(2,1)S(1)} %get-tuple-element.58), channel_id=1, source_target_pairs={{0,5},{1,4},{2,7},{3,6},{4,1},{5,0},{6,3},{7,2},{8,13},{9,12},{10,... | collective-permute-start | bytes 196616 | tf_op jit(solution)/shard_map/ppermute | solution.py:22
  16.6 9.2 %collective-permute-start.8 = (bf16[128,256]{1,0:T(8,128)(2,1)S(1)}, bf16[128,256]{1,0:T(8,128)(2,1)S(1)}, u32[]{:S(2)}, u32[]{:S(2)}) collective-permute-start(bf16[128,256]{1,0:T(8,128)(2,1)S(1)} %get-tuple-element.59), channel_id=1, source_target_pairs={{0,6},{1,7},{2,4},{3,5},{4,2},{5,3},{6,0},{7,1},{8,14},{9,15},{10,... | collective-permute-start | bytes 196616 | tf_op jit(solution)/shard_map/ppermute | solution.py:22
  17.9 7.8 %collective-permute-start.9 = (bf16[128,256]{1,0:T(8,128)(2,1)S(1)}, bf16[128,256]{1,0:T(8,128)(2,1)S(1)}, u32[]{:S(2)}, u32[]{:S(2)}) collective-permute-start(bf16[128,256]{1,0:T(8,128)(2,1)S(1)} %get-tuple-element.60), channel_id=1, source_target_pairs={{0,7},{1,6},{2,5},{3,4},{4,3},{5,2},{6,1},{7,0},{8,15},{9,14},{10,... | collective-permute-start | bytes 196616 | tf_op jit(solution)/shard_map/ppermute | solution.py:22
  25.8 13.7 %collective-permute-start.10 = (bf16[256,256]{1,0:T(8,128)(2,1)S(1)}, bf16[256,256]{1,0:T(8,128)(2,1)S(1)}, u32[]{:S(2)}, u32[]{:S(2)}) collective-permute-start(bf16[256,256]{1,0:T(8,128)(2,1)S(1)} %constant_dynamic-update-slice_fusion), channel_id=1, source_target_pairs={{0,8},{8,0},{16,24},{24,16},{1,9},{9,1},{17,25},{25,17},{2,10},{10... | collective-permute-start | bytes 393224 | tf_op jit(solution)/shard_map/ppermute | solution.py:22
  27.3 12.2 %collective-permute-start.11 = (bf16[256,256]{1,0:T(8,128)(2,1)S(1)}, bf16[256,256]{1,0:T(8,128)(2,1)S(1)}, u32[]{:S(2)}, u32[]{:S(2)}) collective-permute-start(bf16[256,256]{1,0:T(8,128)(2,1)S(1)} %constant_dynamic-update-slice_fusion), channel_id=1, source_target_pairs={{0,16},{8,24},{16,0},{24,8},{1,17},{9,25},{17,1},{25,9},{2,18},{10... | collective-permute-start | bytes 393224 | tf_op jit(solution)/shard_map/ppermute | solution.py:22
  28.8 10.7 %collective-permute-start.12 = (bf16[256,256]{1,0:T(8,128)(2,1)S(1)}, bf16[256,256]{1,0:T(8,128)(2,1)S(1)}, u32[]{:S(2)}, u32[]{:S(2)}) collective-permute-start(bf16[256,256]{1,0:T(8,128)(2,1)S(1)} %constant_dynamic-update-slice_fusion), channel_id=1, source_target_pairs={{0,24},{8,16},{16,8},{24,0},{1,25},{9,17},{17,9},{25,1},{2,26},{10... | collective-permute-start | bytes 393224 | tf_op jit(solution)/shard_map/ppermute | solution.py:22
  34.5 11.4 %copy-start = (bf16[512,768]{1,0:T(8,128)(2,1)S(1)}, bf16[512,768]{1,0:T(8,128)(2,1)}, u32[]{:S(2)}) copy-start(bf16[512,768]{1,0:T(8,128)(2,1)} %weight_ref.1) | copy-start | bytes 2359300
  36.5 6.4 %collective-permute-start.16 = (bf16[224,128]{1,0:T(8,128)(2,1)S(1)}, bf16[224,128]{1,0:T(8,128)(2,1)S(1)}, u32[]{:S(2)}, u32[]{:S(2)}) collective-permute-start(bf16[224,128]{1,0:T(8,128)(2,1)S(1)} %get-tuple-element.72), channel_id=1, source_target_pairs={{0,1},{1,0},{2,3},{3,2},{4,5},{5,4},{6,7},{7,6},{8,9},{9,8},{10,11... | collective-permute-start | bytes 172040 | tf_op jit(solution)/shard_map/ppermute | solution.py:22
  36.6 6.3 %collective-permute-start.17 = (bf16[224,128]{1,0:T(8,128)(2,1)S(1)}, bf16[224,128]{1,0:T(8,128)(2,1)S(1)}, u32[]{:S(2)}, u32[]{:S(2)}) collective-permute-start(bf16[224,128]{1,0:T(8,128)(2,1)S(1)} %get-tuple-element.73), channel_id=1, source_target_pairs={{0,2},{1,3},{2,0},{3,1},{4,6},{5,7},{6,4},{7,5},{8,10},{9,11},{10,... | collective-permute-start | bytes 172040 | tf_op jit(solution)/shard_map/ppermute | solution.py:22
  39.5 3.9 %collective-permute-start.18 = (bf16[224,128]{1,0:T(8,128)(2,1)S(1)}, bf16[224,128]{1,0:T(8,128)(2,1)S(1)}, u32[]{:S(2)}, u32[]{:S(2)}) collective-permute-start(bf16[224,128]{1,0:T(8,128)(2,1)S(1)} %get-tuple-element.74), channel_id=1, source_target_pairs={{0,3},{1,2},{2,1},{3,0},{4,7},{5,6},{6,5},{7,4},{8,11},{9,10},{10,... | collective-permute-start | bytes 172040 | tf_op jit(solution)/shard_map/ppermute | solution.py:22
  40.7 2.6 %collective-permute-start.13 = (bf16[32,128]{1,0:T(8,128)(2,1)S(1)}, bf16[32,128]{1,0:T(8,128)(2,1)S(1)}, u32[]{:S(2)}, u32[]{:S(2)}) collective-permute-start(bf16[32,128]{1,0:T(8,128)(2,1)S(1)} %get-tuple-element.68), channel_id=1, source_target_pairs={{0,1},{1,0},{2,3},{3,2},{4,5},{5,4},{6,7},{7,6},{8,9},{9,8},{10,11... | collective-permute-start | bytes 24584 | tf_op jit(solution)/shard_map/ppermute | solution.py:22
  40.9 3.7 %collective-permute-start.14 = (bf16[32,128]{1,0:T(8,128)(2,1)S(1)}, bf16[32,128]{1,0:T(8,128)(2,1)S(1)}, u32[]{:S(2)}, u32[]{:S(2)}) collective-permute-start(bf16[32,128]{1,0:T(8,128)(2,1)S(1)} %get-tuple-element.69), channel_id=1, source_target_pairs={{0,2},{1,3},{2,0},{3,1},{4,6},{5,7},{6,4},{7,5},{8,10},{9,11},{10,... | collective-permute-start | bytes 24584 | tf_op jit(solution)/shard_map/ppermute | solution.py:22
  42.9 3.1 %collective-permute-start.15 = (bf16[32,128]{1,0:T(8,128)(2,1)S(1)}, bf16[32,128]{1,0:T(8,128)(2,1)S(1)}, u32[]{:S(2)}, u32[]{:S(2)}) collective-permute-start(bf16[32,128]{1,0:T(8,128)(2,1)S(1)} %get-tuple-element.70), channel_id=1, source_target_pairs={{0,3},{1,2},{2,1},{3,0},{4,7},{5,6},{6,5},{7,4},{8,11},{9,10},{10,... | collective-permute-start | bytes 24584 | tf_op jit(solution)/shard_map/ppermute | solution.py:22

commit v3 on v2

v3 whole, which is shorter than its diff:
```python
import functools

import jax
import jax.numpy as jnp
from jax import lax
from jax.experimental import pallas as pl
from jax.experimental.pallas import tpu as pltpu
from jax.sharding import PartitionSpec as P

HEADS = 8
HEAD_DIM = 64
SPARSE = 1024
LANES = 128
FAR = 1 << 30
BARRED = -(2.0**100)
F32 = jnp.float32
BF16 = jnp.bfloat16


def exchange(block, axis, distance):
    count = lax.axis_size(axis)
    return lax.ppermute(block, axis, [(i, i ^ distance) for i in range(count)])


def shift_of(value):
    return value.bit_length() - 1


class Plan:
    def __init__(self, rows, inner, outer):
        self.rows = rows
        self.inner = inner
        self.outer = outer
        self.mid = rows * inner // SPARSE
        self.top = self.mid * outer
        self.group = SPARSE // rows
        self.mid_rows = rows // self.mid
        self.top_rows = rows // self.top
        self.top_tile = max(16, self.top_rows)
        assert self.group == 4 and HEADS == 2 * self.group and 2 * HEAD_DIM == LANES

    def me(self):
        return lax.axis_index("outer") * self.inner + lax.axis_index("inner")

    def pair(self):
        return lax.axis_index("inner") & (self.group - 1)

    def source_row(self, k):
        a = k >> shift_of(self.mid_rows)
        c = (k & (self.mid_rows - 1)) >> shift_of(self.top_rows)
        b = k & (self.top_rows - 1)
        return self.top * b + self.mid * c + a


def dot(a, b, dims):
    return lax.dot_general(a, b, (dims, ((), ())), preferred_element_type=F32)


def pick(wrapped, head, rows):
    return jnp.where(wrapped == ((rows - head) & (rows - 1)), 1.0, 0.0).astype(BF16)


def pack_kernel(plan, lengths_ref, q_ref, k_ref, v_ref, *refs):
    rows, mid_rows, tile = plan.rows, plan.mid_rows, plan.top_tile
    own, near, *outs, table, taken, lengths, sems, length_sem = refs
    leads, seconds, heads, tails = [outs[n : n + 2] for n in range(0, 8, 2)]
    copies = []
    for x in (2, 3, 0, 1):
        columns = pl.ds(pl.multiple_of((plan.pair() ^ x) * LANES, LANES), LANES)
        for part, ref in enumerate((q_ref, k_ref, v_ref)):
            copy = pltpu.make_async_copy(ref.at[:, columns], taken.at[x, part], sems.at[x, part])
            copy.start()
            copies.append(copy)
    length_copy = pltpu.make_async_copy(lengths_ref, lengths, length_sem)
    length_copy.start()
    k = lax.broadcasted_iota(jnp.int32, (rows, rows), 0)
    i = lax.broadcasted_iota(jnp.int32, (rows, rows), 1)
    wrapped = (plan.source_row(k) - i) & (rows - 1)
    first = lax.broadcasted_iota(jnp.int32, (rows, LANES), 1) < HEAD_DIM
    for s, x in enumerate((2, 3, 0, 1)):
        pair = plan.pair() ^ x
        one_hot = [pick(wrapped, 2 * pair + t, rows) for t in range(2)]
        for part in range(3):
            copies[3 * s + part].wait()
        block = jnp.concatenate([taken[x, part] for part in range(3)], axis=1)
        one, two = [dot(m, block, ((1,), (0,))) for m in one_hot]
        query = jnp.where(first, one[:, :LANES], two[:, :LANES]) * HEAD_DIM**-0.5
        kv_one = jnp.where(
            first, one[:, LANES : 2 * LANES], pltpu.roll(one[:, 2 * LANES :], HEAD_DIM, axis=1)
        ).astype(BF16)
        kv_two = jnp.where(
            first, pltpu.roll(two[:, 2 * LANES :], HEAD_DIM, axis=1), two[:, LANES : 2 * LANES]
        ).astype(BF16)
        lead = leads[x - 2] if x >= 2 else (own, near)[x]
        lead[:, :LANES] = query.astype(BF16)
        lead[:, LANES : 2 * LANES] = kv_one
        if x >= 2:
            seconds[x - 2][...] = kv_two
        else:
            lead[:, 2 * LANES :] = kv_two
        at = (x & 1) * 2 * LANES
        for out, low, high in ((heads[x >> 1], 0, tile), (tails[x >> 1], tile, mid_rows)):
            out[:, at : at + LANES] = kv_one[low:high]
            out[:, at + LANES : at + 2 * LANES] = kv_two[low:high]
    length_copy.wait()
    slide_table(lengths, table)


def block_positions(plan, t, rows):
    head = 2 * plan.pair() + t
    return (plan.source_row(row_iota(rows)) + head) & (plan.rows - 1)


def block_inside(plan, table_ref, t, positions, slot):
    base = (plan.me() ^ slot) * plan.rows
    starts = table_ref[2 * t : 2 * t + 1, :] - base
    ends = table_ref[2 * t + 1 : 2 * t + 2, :] - base
    return (positions >= starts) & (positions < ends)


def features(plan, table_ref, t, base, slot_shift, count):
    r = lax.broadcasted_iota(jnp.int32, (count, LANES), 0)
    lane = lax.broadcasted_iota(jnp.int32, (count, LANES), 1)
    head = 2 * plan.pair() + t
    source = plan.me() ^ (base + (r >> slot_shift))
    k = r & ((1 << slot_shift) - 1)
    position = source * plan.rows + ((plan.source_row(k) + head) & (plan.rows - 1))
    starts = table_ref[2 * t : 2 * t + 1, :]
    ends = table_ref[2 * t + 1 : 2 * t + 2, :]
    inside = (position >= starts) & (position < ends)
    own = (lane < HEAD_DIM) if t == 0 else (lane >= HEAD_DIM)
    return inside, own


def as_query(block, inside, own):
    return jnp.where(own, block.astype(F32), jnp.where(inside, BARRED, 0.0)).astype(BF16)


def as_key(block, inside, own):
    return jnp.where(own, block.astype(F32), jnp.where(inside, 0.0, 1.0)).astype(BF16)


def as_value(block, own):
    return jnp.where(own, 1.0, block.astype(F32))


def row_iota(count):
    return lax.broadcasted_iota(jnp.int32, (count, LANES), 0)


def share(sums):
    return pltpu.roll(sums, HEAD_DIM, axis=1) / sums


def chunks(own, near, leads, seconds):
    part = lambda ref, n: ref.at[:, n * LANES : (n + 1) * LANES]
    queries = [part(ref, 0) for ref in (own, near, *leads)]
    firsts = [part(ref, 1) for ref in (own, near, *leads)]
    return queries, firsts, [part(own, 2), part(near, 2), *seconds]


def local_kernel(plan, t, table_ref, own, near, *refs):
    rows, group, mid_rows, tile = plan.rows, plan.group, plan.mid_rows, plan.top_tile
    leads, seconds, refs = refs[:2], refs[2 : 2 + 2 * t], refs[2 + 2 * t :]
    if t:
        before, rests, refs = refs[0], refs[1 : 1 + group], refs[1 + group :]
    else:
        rest, refs = refs[0], refs[1:]
    sums_ref, maxima_ref, q_s, k_s, v_s, v2_s, vt_s = refs
    queries, firsts, seconds = chunks(own, near, leads, seconds)
    positions = block_positions(plan, t, rows)
    lane = lax.broadcasted_iota(jnp.int32, (rows, LANES), 1)
    keys = (lane < HEAD_DIM) if t == 0 else (lane >= HEAD_DIM)
    is_top = row_iota(mid_rows) < plan.top_rows
    for x in range(group):
        here = pl.ds(x * rows, rows)
        mid_here = pl.ds(x * mid_rows, mid_rows)
        inside = block_inside(plan, table_ref, t, positions, x)
        kv = (seconds if t else firsts)[x][...].astype(F32)
        q_s[here, :] = as_query(queries[x][...], inside, keys)
        k_s[here, :] = as_key(kv, inside, keys)
        value = as_value(kv, keys)
        low = value.astype(BF16)
        v_s[here, :] = low
        v2_s[pl.ds(x * rows, mid_rows), :] = (2.0 * value[:mid_rows]).astype(BF16)
        v2_s[pl.ds(x * rows + mid_rows, rows - mid_rows), :] = low[mid_rows:]
        vt_s[mid_here, :] = jnp.where(is_top, value[:mid_rows], 0.0).astype(BF16)
    lane = lax.broadcasted_iota(jnp.int32, (rows - mid_rows, LANES), 1)
    for x in range(group):
        here = pl.ds(x * rows, rows)
        mid_here = pl.ds(x * mid_rows, mid_rows)
        rest_here = pl.ds(x * (rows - mid_rows), rows - mid_rows)
        scores = dot(q_s[here, :], k_s[...], ((1,), (1,)))
        largest = jnp.max(scores, axis=1, keepdims=True)
        probs = jnp.exp(scores - largest).astype(BF16)
        mid_sum = dot(probs[:mid_rows], v2_s[...], ((1,), (0,)))
        top_probs = [probs[:tile, y * rows : y * rows + mid_rows] for y in range(group)]
        top_sum = dot(jnp.concatenate(top_probs, axis=1), vt_s[...], ((1,), (0,)))
        rest_sum = share(dot(probs[mid_rows:], v_s[...], ((1,), (0,))))
        top_sum = jnp.where(row_iota(tile) < plan.top_rows, top_sum, 0.0)
        sums_ref[mid_here, :] = mid_sum
        sums_ref[pl.ds(x * mid_rows, tile), :] += top_sum
        maxima_ref[mid_here, :] = jnp.broadcast_to(largest[:mid_rows], (mid_rows, LANES))
        if t:
            both = jnp.where(lane < HEAD_DIM, before[rest_here, :], rest_sum)
            rests[x][...] = both.astype(BF16)
        else:
            rest[rest_here, :] = rest_sum


def other_chunks(arrays):
    width = 2 * LANES
    slots = []
    for n in range(0, len(arrays), 2):
        if isinstance(arrays[n], jax.Array):
            slots += [arrays[n][:, :width], arrays[n + 1][:, width:]]
        else:
            slots += [arrays[n].at[:, :width], arrays[n + 1].at[:, width:]]
    return slots


def mid_kernel(plan, table_ref, *refs):
    group, mid_rows, tile = plan.group, plan.mid_rows, plan.top_tile
    n = plan.inner - group
    states, refs = refs[:4], refs[4:]
    queries, refs = [ref.at[:, :LANES] for ref in refs[:4]], refs[4:]
    heads, tails, refs = other_chunks(refs[:n]), other_chunks(refs[n : 2 * n]), refs[2 * n :]
    outs, lead_states, (k_s, v_s, vt_s) = refs[:group], refs[group : group + 6], refs[group + 6 :]
    count = group * mid_rows
    queries = jnp.concatenate([query[:mid_rows, :] for query in queries], axis=0)
    key_lane = lax.broadcasted_iota(jnp.int32, (mid_rows, LANES), 1)
    results = []
    for t in range(2):
        inside, own = features(plan, table_ref, t, 0, shift_of(mid_rows), count)
        q = as_query(queries, inside, own)
        positions = block_positions(plan, t, mid_rows)
        keys = (key_lane < HEAD_DIM) if t == 0 else (key_lane >= HEAD_DIM)
        columns = slice(t * LANES, (t + 1) * LANES)
        for y in range(n):
            inside = block_inside(plan, table_ref, t, positions, group + y)
            parts = (
                (heads[y], 0, tile, y * tile),
                (tails[y], tile, mid_rows, n * tile + y * (mid_rows - tile)),
            )
            for ref, low, high, at in parts:
                kv = ref[:, columns].astype(F32)
                there = pl.ds(at, high - low)
                value = as_value(kv, keys[low:high])
                k_s[there, :] = as_key(kv, inside[low:high], keys[low:high])
                v_s[there, :] = value.astype(BF16)
                if low == 0:
                    is_top = row_iota(tile) < plan.top_rows
                    vt_s[there, :] = jnp.where(is_top, value, 0.0).astype(BF16)
        old = states[2 * t + 1][:, :1]
        scores = dot(q, k_s[...], ((1,), (1,)))
        new = jnp.maximum(old, jnp.max(scores, axis=1, keepdims=True))
        probs = jnp.exp(scores - new).astype(BF16)
        sums = states[2 * t][...] * jnp.exp(old - new)
        sums = sums + dot(probs, v_s[...], ((1,), (0,)))

        def leading(array):
            return jnp.concatenate(
                [array[x * mid_rows : x * mid_rows + tile] for x in range(group)], axis=0
            )

        extra = dot(leading(probs[:, : n * tile]), vt_s[...], ((1,), (0,)))
        keep = (row_iota(group * tile) & (tile - 1)) < plan.top_rows
        lead_states[3 * t][...] = leading(sums) + jnp.where(keep, extra, 0.0)
        lead_states[3 * t + 1][...] = jnp.broadcast_to(leading(new), (group * tile, LANES))
        lead_states[3 * t + 2][...] = leading(q)
        results.append(share(sums))
    lane = lax.broadcasted_iota(jnp.int32, (count, LANES), 1)
    both = jnp.where(lane < HEAD_DIM, results[0], results[1]).astype(BF16)
    for x in range(group):
        outs[x][...] = both[x * mid_rows + tile : (x + 1) * mid_rows]


def top_kernel(plan, table_ref, *refs):
    group, tile = plan.group, plan.top_tile
    states, refs = refs[:6], refs[6:]
    middles, refs = refs[:group], refs[group:]
    tops, outs = refs[: plan.outer - 1], refs[plan.outer - 1 :]
    count = group * tile
    shift = shift_of(plan.top_rows)
    is_top = (row_iota(count) & (tile - 1)) < plan.top_rows
    results = []
    for t in range(2):
        keys, values = [], []
        for e in range(1, plan.outer):
            kv = tops[e - 1][:, t * LANES : (t + 1) * LANES]
            inside, own = features(plan, table_ref, t, e * plan.inner, shift, kv.shape[0])
            keys.append(as_key(kv, inside, own))
            values.append(as_value(kv, own).astype(BF16))
        sums, old, q = states[3 * t][...], states[3 * t + 1][:, :1], states[3 * t + 2][...]
        scores = dot(q, jnp.concatenate(keys, axis=0), ((1,), (1,)))
        new = jnp.maximum(old, jnp.max(scores, axis=1, keepdims=True))
        probs = jnp.exp(scores - new).astype(BF16)
        merged = sums * jnp.exp(old - new)
        merged = merged + dot(probs, jnp.concatenate(values, axis=0), ((1,), (0,)))
        results.append(share(jnp.where(is_top, merged, sums)))
    lane = lax.broadcasted_iota(jnp.int32, (count, LANES), 1)
    both = jnp.where(lane < HEAD_DIM, results[0], results[1]).astype(BF16)
    for x in range(group):
        outs[x][:tile] = both[x * tile : (x + 1) * tile]
        outs[x][tile:] = middles[x][...]


def unpermute(plan, parts, low, high, out):
    rows = plan.rows
    i = lax.broadcasted_iota(jnp.int32, (rows, high - low), 0)
    k = lax.broadcasted_iota(jnp.int32, (rows, high - low), 1) + low
    wrapped = (plan.source_row(k) - i) & (rows - 1)
    lane = lax.broadcasted_iota(jnp.int32, (rows, LANES), 1)
    for x in range(plan.group):
        pair = plan.pair() ^ x
        one = dot(pick(wrapped, 2 * pair, rows), parts[x][...], ((1,), (0,)))
        two = dot(pick(wrapped, 2 * pair + 1, rows), parts[x][...], ((1,), (0,)))
        columns = pl.ds(pl.multiple_of(pair * LANES, LANES), LANES)
        value = jnp.where(lane < HEAD_DIM, one, two)
        if low == 0:
            value = value + out[1][:, columns].astype(F32)
        out[0][:, columns] = value.astype(BF16)


def order_kernel(plan, *refs):
    unpermute(plan, refs[:-1], plan.mid_rows, plan.rows, (refs[-1],))


def project_kernel(plan, weight_ref, rest_ref, *refs):
    uppers, (out_ref, flat) = refs[: plan.group], refs[plan.group :]
    unpermute(plan, uppers, 0, plan.mid_rows, (flat, rest_ref))
    out_ref[...] = dot(flat[...], weight_ref[...], ((1,), (0,))).astype(BF16)


def slide_table(lengths_ref, table_ref):
    row = lax.broadcasted_iota(jnp.int32, (8, LANES), 0)
    lane = lax.broadcasted_iota(jnp.int32, (8, LANES), 1)
    slide = lane - jnp.where(row < 2, HEAD_DIM, 0)
    table = jnp.full((8, LANES), FAR, jnp.int32)
    start = jnp.int32(0)
    for s in range(lengths_ref.shape[0]):
        end = start + lengths_ref[s]
        table = jnp.where(slide == s, jnp.where((row & 1) == 1, end, start), table)
        start = end
    table_ref[...] = table


def shape(count, width, kind=BF16):
    return jax.ShapeDtypeStruct((count, width), kind)


def call(kernel, operands, results, scratch=(), in_specs=None):
    vmem = pl.BlockSpec(memory_space=pltpu.VMEM)
    return pl.pallas_call(
        kernel,
        in_specs=in_specs or [vmem] * len(operands),
        out_specs=[vmem] * len(results),
        out_shape=results,
        scratch_shapes=scratch,
        compiler_params=pltpu.CompilerParams(vmem_limit_bytes=24 << 20),
    )(*operands)


def shards(queries, keys, values, out_weight, slide_lengths):
    plan = Plan(queries.shape[0], lax.axis_size("inner"), lax.axis_size("outer"))
    rows, group, mid_rows, tile = plan.rows, plan.group, plan.mid_rows, plan.top_tile
    hbm = pl.BlockSpec(memory_space=pltpu.HBM)
    own, near, *packed, table = call(
        functools.partial(pack_kernel, plan),
        [
            pltpu.with_memory_space_constraint(a, pltpu.HBM)
            for a in (slide_lengths, queries, keys, values)
        ],
        [shape(rows, 3 * LANES)] * 2
        + [shape(rows, 2 * LANES)] * 2
        + [shape(rows, LANES)] * 2
        + [shape(tile, 4 * LANES)] * 2
        + [shape(mid_rows - tile, 4 * LANES)] * 2
        + [shape(8, LANES, jnp.int32)],
        [
            pltpu.VMEM((group, 3, rows, LANES), BF16),
            pltpu.SMEM(slide_lengths.shape, jnp.int32),
            pltpu.SemaphoreType.DMA((group, 3)),
            pltpu.SemaphoreType.DMA,
        ],
        [hbm] * 4,
    )
    leads, seconds, heads, tails = [packed[n : n + 2] for n in range(0, 8, 2)]
    leads = [exchange(leads[n], "inner", 2 + n) for n in range(2)]
    seconds = [exchange(seconds[n], "inner", 2 + n) for n in range(2)]
    near = exchange(near, "inner", 1)
    other_heads, other_tails = [], []
    for x in range(group, plan.inner, 2):
        for parts, slots in ((heads, other_heads), (tails, other_tails)):
            other = exchange(parts[x >> 1 & 1], "inner", x)
            slots += [other, exchange(other, "inner", 1)]

    top = plan.top_rows
    firsts = [a[:top, LANES : 2 * LANES] for a in (own, near, *leads)]
    lasts = [a[:top, 2 * LANES :] for a in (own, near)] + [a[:top] for a in seconds]
    kv = [jnp.concatenate(slot, axis=1) for slot in zip(firsts, lasts)]
    top_own = jnp.concatenate(kv + [slot[:top] for slot in other_chunks(other_heads)], axis=0)
    tops = [exchange(top_own, "outer", x) for x in range(1, plan.outer)]

    count = group * rows
    scratch = [pltpu.VMEM((count, LANES), BF16)] * 4
    scratch += [pltpu.VMEM((group * mid_rows, LANES), BF16)]
    state = [shape(group * mid_rows, LANES, F32)] * 2
    rest_one, sums_one, maxima_one = call(
        functools.partial(local_kernel, plan, 0),
        (table, own, near, *leads),
        [shape(group * (rows - mid_rows), LANES, F32), *state],
        scratch,
    )
    *rests, sums_two, maxima_two = call(
        functools.partial(local_kernel, plan, 1),
        (table, own, near, *leads, *seconds, rest_one),
        [shape(rows - mid_rows, LANES)] * group + state,
        scratch,
    )
    rests = [rests[0]] + [exchange(rests[x], "inner", x) for x in range(1, group)]
    lead_state = [shape(group * tile, LANES, F32)] * 2 + [shape(group * tile, LANES)]
    n_mid = (plan.inner - group) * mid_rows
    middle = call(
        functools.partial(mid_kernel, plan),
        (
            table,
            *(sums_one, maxima_one, sums_two, maxima_two),
            *(own, near, *leads),
            *other_heads,
            *other_tails,
        ),
        [shape(mid_rows - tile, LANES)] * group + lead_state * 2,
        [pltpu.VMEM((n_mid, LANES), BF16)] * 2
        + [pltpu.VMEM(((plan.inner - group) * tile, LANES), BF16)],
    )
    middles, lead_state = middle[:group], middle[group:]
    uppers = call(
        functools.partial(top_kernel, plan),
        (table, *lead_state, *middles, *tops),
        [shape(mid_rows, LANES)] * group,
    )
    uppers = [uppers[0]] + [exchange(uppers[x], "inner", x) for x in range(1, group)]
    ordered = call(functools.partial(order_kernel, plan), rests, [shape(rows, HEADS * HEAD_DIM)])[0]
    return call(
        functools.partial(project_kernel, plan),
        (out_weight, ordered, *uppers),
        [shape(rows, out_weight.shape[1])],
        [pltpu.VMEM((rows, HEADS * HEAD_DIM), BF16)],
    )[0]


def solution(mesh):
    tokens = P(("outer", "inner"), None)

    return jax.shard_map(
        shards,
        mesh=mesh,
        in_specs=(tokens, tokens, tokens, P(), P()),
        out_specs=tokens,
        check_vma=False,
    )
```

time: 47.8 us -> 43.8 us (0.916)
  waiting for transfers between devices: 12.1 us -> 7.35 us
  starting transfers between devices: 21.2 us -> 23.7 us
  Pallas kernels: 13.4 us -> 12.3 us
  local copies, waits for them, and re-layouts: 0.71 us -> 0.03 us
    ppermute x19 -> x22, waiting for transfers between devices: 12.1 us -> 7.35 us  [exchange(): return lax.ppermute(block, axis, [(i, i ^ distance) for i in range(count)])]
    ppermute x19 -> x22, starting transfers between devices: 21.2 us -> 23.7 us  [exchange(): return lax.ppermute(block, axis, [(i, i ^ distance) for i in range(count)])]
    pallas_call x7, Pallas kernels: 13.4 us -> 12.3 us  [call(): pl.pallas_call(kernel, in_specs=in_specs or [vmem] * len(operands), out_s...]
    unnamed x7, local copies, waits for them, and re-layouts: 0.67 us -> 0.02 us
  transfers between devices with their start and end apart: 19 -> 22, of which waited for: 5 -> 9; matrix products, arithmetic and copies ran while one was open for 0% -> 0% of each run, Pallas kernels for 21% -> 19%
where the time goes in v3:
time: 43.8 us; the launch traced here: 43.6 us
  starting transfers between devices  23.7 us (54%)
  Pallas kernels  12.3 us (28%)
  waiting for transfers between devices  7.35 us (17%)
    ppermute x22, starting transfers between devices, exchange(): return lax.ppermute(block, axis, [(i, i ^ distance) for i in range(count)])  23.7 us
    pallas_call x7, Pallas kernels, call(): pl.pallas_call(kernel, in_specs=in_specs or [vmem] * len(operands), out_s...  12.3 us
    ppermute x22, waiting for transfers between devices, exchange(): return lax.ppermute(block, axis, [(i, i ^ distance) for i in range(count)])  7.35 us
  transfers between devices with their start and end apart: 22, of which 9 were waited for; matrix products, arithmetic and copies ran while one was open for 0% of the time, Pallas kernels for 19%

profile of v3, /device:TPU:0, one launch (start us, length us, event | category | flops | bytes accessed | tf_op | source)
XLA Modules:
  0.0 43.6 jit_solution(15689111285426472100)
XLA Ops:
  0.0 2.5 %shard_map.55 = (bf16[256,384]{1,0:T(8,128)(2,1)S(1)}, bf16[256,384]{1,0:T(8,128)(2,1)S(1)}, bf16[256,256]{1,0:T(8,128)(2,1)S(1)}, bf16[256,256]{1,0:T(8,128)(2,...) custom-call(s32[16]{0:T(128)} %lengths_ref.1, ...), custom_call_target="tpu_custom_call" | custom-call | tf_op jit(solution)/shard_map/pallas_call | solution.py:354
  2.5 3.1 %collective-permute-start.3 = (bf16[256,128]{1,0:T(8,128)(2,1)S(1)}, bf16[256,128]{1,0:T(8,128)(2,1)S(1)}, u32[]{:S(2)}, u32[]{:S(2)}) collective-permute-start(bf16[256,128]{1,0:T(8,128)(2,1)S(1)} %get-tuple-element.44), channel_id=1, source_target_pairs={{0,2},{1,3},{2,0},{3,1},{4,6},{5,7},{6,4},{7,5},{8,10},{9,11},{10,... | collective-permute-start | bytes 196616 | tf_op jit(solution)/shard_map/ppermute | solution.py:22
  5.6 0.0 collective-permute-start.4
  5.6 0.2 collective-permute-start
  5.8 1.9 %collective-permute-start.1 = (bf16[256,256]{1,0:T(8,128)(2,1)S(1)}, bf16[256,256]{1,0:T(8,128)(2,1)S(1)}, u32[]{:S(2)}, u32[]{:S(2)}) collective-permute-start(bf16[256,256]{1,0:T(8,128)(2,1)S(1)} %get-tuple-element.42), channel_id=1, source_target_pairs={{0,2},{1,3},{2,0},{3,1},{4,6},{5,7},{6,4},{7,5},{8,10},{9,11},{10,... | collective-permute-start | bytes 393224 | tf_op jit(solution)/shard_map/ppermute | solution.py:22
  7.8 0.0 collective-permute-start.2
  7.8 0.1 collective-permute-done.3.refs_2_
  7.9 3.0 %collective-permute-start.8 = (bf16[32,512]{1,0:T(8,128)(2,1)S(1)}, bf16[32,512]{1,0:T(8,128)(2,1)S(1)}, u32[]{:S(2)}, u32[]{:S(2)}) collective-permute-start(bf16[32,512]{1,0:T(8,128)(2,1)S(1)} %get-tuple-element.55), channel_id=1, source_target_pairs={{0,4},{1,5},{2,6},{3,7},{4,0},{5,1},{6,2},{7,3},{8,12},{9,13},{10,... | collective-permute-start | bytes 98312 | tf_op jit(solution)/shard_map/ppermute | solution.py:22
  10.9 0.0 collective-permute-done.4.refs_3_
  10.9 1.7 %collective-permute-start.10 = (bf16[32,512]{1,0:T(8,128)(2,1)S(1)}, bf16[32,512]{1,0:T(8,128)(2,1)S(1)}, u32[]{:S(2)}, u32[]{:S(2)}) collective-permute-start(bf16[32,512]{1,0:T(8,128)(2,1)S(1)} %get-tuple-element.56), channel_id=1, source_target_pairs={{0,6},{1,7},{2,4},{3,5},{4,2},{5,3},{6,0},{7,1},{8,14},{9,15},{10,... | collective-permute-start | bytes 98312 | tf_op jit(solution)/shard_map/ppermute | solution.py:22
  12.6 0.4 collective-permute-done.1.refs_0_.refs_6_
  13.0 2.4 %collective-permute-start.12 = (bf16[96,512]{1,0:T(8,128)(2,1)S(1)}, bf16[96,512]{1,0:T(8,128)(2,1)S(1)}, u32[]{:S(2)}, u32[]{:S(2)}) collective-permute-start(bf16[96,512]{1,0:T(8,128)(2,1)S(1)} %get-tuple-element.57), channel_id=1, source_target_pairs={{0,4},{1,5},{2,6},{3,7},{4,0},{5,1},{6,2},{7,3},{8,12},{9,13},{10,... | collective-permute-start | bytes 294920 | tf_op jit(solution)/shard_map/ppermute | solution.py:22
  15.4 0.0 collective-permute-done.8.refs_8_
  15.4 2.3 %collective-permute-start.14 = (bf16[96,512]{1,0:T(8,128)(2,1)S(1)}, bf16[96,512]{1,0:T(8,128)(2,1)S(1)}, u32[]{:S(2)}, u32[]{:S(2)}) collective-permute-start(bf16[96,512]{1,0:T(8,128)(2,1)S(1)} %get-tuple-element.58), channel_id=1, source_target_pairs={{0,6},{1,7},{2,4},{3,5},{4,2},{5,3},{6,0},{7,1},{8,14},{9,15},{10,... | collective-permute-start | bytes 294920 | tf_op jit(solution)/shard_map/ppermute | solution.py:22
  17.7 1.3 %collective-permute-done.10.refs_10_ = bf16[32,512]{1,0:T(8,128)(2,1)S(1)} collective-permute-done((bf16[32,512]{1,0:T(8,128)(2,1)S(1)}, bf16[32,512]{1,0:T(8,128)(2,1)S(1)}, u32[]{:S(2)}, u32[]{:S(2)}) %collective-permute-start.10) | collective-permute-done | bytes 32800 | tf_op jit(solution)/shard_map/ppermute | solution.py:22
  18.9 0.1 collective-permute-start.9
  19.0 0.0 collective-permute-done.2.refs_1_.refs_7_
  19.0 0.5 %collective-permute-start.11 = (bf16[32,512]{1,0:T(8,128)(2,1)S(1)}, bf16[32,512]{1,0:T(8,128)(2,1)S(1)}, u32[]{:S(2)}, u32[]{:S(2)}) collective-permute-start(bf16[32,512]{1,0:T(8,128)(2,1)S(1)} %collective-permute-done.10.refs_10_), channel_id=1, source_target_pairs={{0,1},{1,0},{2,3},{3,2},{4,5},{5,4},{6,7},{7,6},{8,9},{9,8},{10,11... | collective-permute-start | bytes 98312 | tf_op jit(solution)/shard_map/ppermute | solution.py:22
  19.4 0.0 collective-permute-done.near.refs_5_
  19.5 0.7 %collective-permute-done.9.refs_9_ = bf16[32,512]{1,0:T(8,128)(2,1)S(1)} collective-permute-done((bf16[32,512]{1,0:T(8,128)(2,1)S(1)}, bf16[32,512]{1,0:T(8,128)(2,1)S(1)}, u32[]{:S(2)}, u32[]{:S(2)}) %collective-permute-start.9) | collective-permute-done | bytes 32800 | tf_op jit(solution)/shard_map/ppermute | solution.py:22
  20.1 0.2 collective-permute-done.11.refs_11_
  20.3 1.5 %collective-permute-start.16 = (bf16[256,256]{1,0:T(8,128)(2,1)S(1)}, bf16[256,256]{1,0:T(8,128)(2,1)S(1)}, u32[]{:S(2)}, u32[]{:S(2)}) collective-permute-start(bf16[256,256]{1,0:T(8,128)(2,1)S(1)} %constant_dynamic-update-slice_fusion), channel_id=1, source_target_pairs={{0,8},{8,0},{16,24},{24,16},{1,9},{9,1},{17,25},{25,17},{2,10},{10... | collective-permute-start | bytes 393224 | tf_op jit(solution)/shard_map/ppermute | solution.py:22
  21.8 1.5 %collective-permute-start.17 = (bf16[256,256]{1,0:T(8,128)(2,1)S(1)}, bf16[256,256]{1,0:T(8,128)(2,1)S(1)}, u32[]{:S(2)}, u32[]{:S(2)}) collective-permute-start(bf16[256,256]{1,0:T(8,128)(2,1)S(1)} %constant_dynamic-update-slice_fusion), channel_id=1, source_target_pairs={{0,16},{8,24},{16,0},{24,8},{1,17},{9,25},{17,1},{25,9},{2,18},{10... | collective-permute-start | bytes 393224 | tf_op jit(solution)/shard_map/ppermute | solution.py:22
  23.3 0.5 %collective-permute-start.18 = (bf16[256,256]{1,0:T(8,128)(2,1)S(1)}, bf16[256,256]{1,0:T(8,128)(2,1)S(1)}, u32[]{:S(2)}, u32[]{:S(2)}) collective-permute-start(bf16[256,256]{1,0:T(8,128)(2,1)S(1)} %constant_dynamic-update-slice_fusion), channel_id=1, source_target_pairs={{0,24},{8,16},{16,8},{24,0},{1,25},{9,17},{17,9},{25,1},{2,26},{10... | collective-permute-start | bytes 393224 | tf_op jit(solution)/shard_map/ppermute | solution.py:22
  23.8 1.4 %collective-permute-done.12.refs_12_ = bf16[96,512]{1,0:T(8,128)(2,1)S(1)} collective-permute-done((bf16[96,512]{1,0:T(8,128)(2,1)S(1)}, bf16[96,512]{1,0:T(8,128)(2,1)S(1)}, u32[]{:S(2)}, u32[]{:S(2)}) %collective-permute-start.12) | collective-permute-done | bytes 98336 | tf_op jit(solution)/shard_map/ppermute | solution.py:22
  25.2 0.0 collective-permute-start.13
  25.2 0.0 collective-permute-done.14.refs_14_
  25.2 0.5 %collective-permute-start.15 = (bf16[96,512]{1,0:T(8,128)(2,1)S(1)}, bf16[96,512]{1,0:T(8,128)(2,1)S(1)}, u32[]{:S(2)}, u32[]{:S(2)}) collective-permute-start(bf16[96,512]{1,0:T(8,128)(2,1)S(1)} %collective-permute-done.14.refs_14_), channel_id=1, source_target_pairs={{0,1},{1,0},{2,3},{3,2},{4,5},{5,4},{6,7},{7,6},{8,9},{9,8},{10,11... | collective-permute-start | bytes 294920 | tf_op jit(solution)/shard_map/ppermute | solution.py:22
  25.7 2.4 %shard_map.56 = (f32[512,128]{1,0:T(8,128)S(1)}, f32[512,128]{1,0:T(8,128)S(1)}, f32[512,128]{1,0:T(8,128)S(1)}) custom-call(s32[8,128]{1,0:T(8,128)S(1)} %get-tuple-element.39.table_ref, bf16[256,384]{1,0:T(8,128)(2,1)S(1)} %get-tuple-element.40.own.refs_4_, bf16[256,384]{1,0:T(8,128)(2,1)S(1)} %collective-permute-done.near.refs_5_, ...), custom_call_target="tpu_custom_call" | custom-call | tf_op jit(solution)/shard_map/pallas_call | solution.py:354
  28.1 2.4 %shard_map.57 = (bf16[128,128]{1,0:T(8,128)(2,1)S(1)}, bf16[128,128]{1,0:T(8,128)(2,1)S(1)}, bf16[128,128]{1,0:T(8,128)(2,1)S(1)}, bf16[128,128]{1,0:T(8,128)(2,...) custom-call(s32[8,128]{1,0:T(8,128)S(1)} %get-tuple-element.39.table_ref, ...), custom_call_target="tpu_custom_call" | custom-call | tf_op jit(solution)/shard_map/pallas_call | solution.py:354
  30.6 0.0 collective-permute-done.13.refs_13_
  30.6 0.1 collective-permute-start.5
  30.7 0.0 collective-permute-done.15.refs_15_
  30.7 2.3 %collective-permute-start.6 = (bf16[128,128]{1,0:T(8,128)(2,1)S(1)}, bf16[128,128]{1,0:T(8,128)(2,1)S(1)}, u32[]{:S(2)}, u32[]{:S(2)}) collective-permute-start(bf16[128,128]{1,0:T(8,128)(2,1)S(1)} %get-tuple-element.49), channel_id=1, source_target_pairs={{0,2},{1,3},{2,0},{3,1},{4,6},{5,7},{6,4},{7,5},{8,10},{9,11},{10,... | collective-permute-start | bytes 98312 | tf_op jit(solution)/shard_map/ppermute | solution.py:22
  33.0 2.1 %shard_map.59 = (bf16[96,128]{1,0:T(8,128)(2,1)S(1)}, bf16[96,128]{1,0:T(8,128)(2,1)S(1)}, bf16[96,128]{1,0:T(8,128)(2,1)S(1)}, bf16[96,128]{1,0:T(8,128)(2,1)S(...) custom-call(s32[8,128]{1,0:T(8,128)S(1)} %get-tuple-element.39.table, ...), custom_call_target="tpu_custom_call" | custom-call | tf_op jit(solution)/shard_map/pallas_call | solution.py:354
  35.1 0.0 copy-start
  35.1 0.0 collective-permute-done.16.refs_10_
  35.1 0.1 collective-permute-start.7
  35.2 0.0 collective-permute-done.17.refs_11_
  35.2 1.2 %shard_map.60 = (bf16[128,128]{1,0:T(8,128)(2,1)S(1)}, bf16[128,128]{1,0:T(8,128)(2,1)S(1)}, bf16[128,128]{1,0:T(8,128)(2,1)S(1)}, bf16[128,128]{1,0:T(8,128)(2,1)S(1)}) custom-call(s32[8,128]{1,0:T(8,128)S(1)} %get-tuple-element.39.table_ref, f32[128,128]{1,0:T(8,128)S(1)} %get-tuple-element.59.refs_0_, f32[128,128]{1,0:T(8,128)S(1)} %get-tuple-element.60.refs_1_, ...), custom_call_target="tpu_custom_call" | custom-call | tf_op jit(solution)/shard_map/pallas_call | solution.py:354
  36.4 0.2 collective-permute-start.19
  36.5 2.0 %collective-permute-start.20 = (bf16[128,128]{1,0:T(8,128)(2,1)S(1)}, bf16[128,128]{1,0:T(8,128)(2,1)S(1)}, u32[]{:S(2)}, u32[]{:S(2)}) collective-permute-start(bf16[128,128]{1,0:T(8,128)(2,1)S(1)} %get-tuple-element.71), channel_id=1, source_target_pairs={{0,2},{1,3},{2,0},{3,1},{4,6},{5,7},{6,4},{7,5},{8,10},{9,11},{10,... | collective-permute-start | bytes 98312 | tf_op jit(solution)/shard_map/ppermute | solution.py:22
  38.6 0.0 collective-permute-done.5.refs_1_
  38.6 0.2 collective-permute-done.7.refs_3_
  38.8 0.3 shard_map.58.rest_ref
  39.1 1.3 %collective-permute-done.20.refs_2_ = bf16[128,128]{1,0:T(8,128)(2,1)S(1)} collective-permute-done((bf16[128,128]{1,0:T(8,128)(2,1)S(1)}, bf16[128,128]{1,0:T(8,128)(2,1)S(1)}, u32[]{:S(2)}, u32[]{:S(2)}) %collective-permute-start.20) | collective-permute-done | bytes 32800 | tf_op jit(solution)/shard_map/ppermute | solution.py:22
  40.5 1.8 %collective-permute-done.21.refs_3_ = bf16[128,128]{1,0:T(8,128)(2,1)S(1)} collective-permute-done((bf16[128,128]{1,0:T(8,128)(2,1)S(1)}, bf16[128,128]{1,0:T(8,128)(2,1)S(1)}, u32[]{:S(2)}, u32[]{:S(2)}) %collective-permute-start.21) | collective-permute-done | bytes 32800 | tf_op jit(solution)/shard_map/ppermute | solution.py:22
  42.2 1.4 %shard_map.61 = bf16[256,768]{1,0:T(8,128)(2,1)} custom-call(bf16[512,768]{1,0:T(8,128)(2,1)S(1)} %copy-done, bf16[256,512]{1,0:T(8,128)(2,1)S(1)} %shard_map.58.rest_ref, bf16[128,128]{1,0:T(8,128)(2,1)S(1)} %get-tuple-element.69.refs_0_, bf16[128,128]{1,0:T(8,128)(2,1)S(1)} %collective-permute-done.19.refs_1_, ...), custom_call_target="tpu_custom_call" | custom-call | tf_op jit(solution)/shard_map/pallas_call | solution.py:354
  (17 shorter events, 0.0 us)
Async XLA Ops:
  2.5 5.4 %collective-permute-start.3 = (bf16[256,128]{1,0:T(8,128)(2,1)S(1)}, bf16[256,128]{1,0:T(8,128)(2,1)S(1)}, u32[]{:S(2)}, u32[]{:S(2)}) collective-permute-start(bf16[256,128]{1,0:T(8,128)(2,1)S(1)} %get-tuple-element.44), channel_id=1, source_target_pairs={{0,2},{1,3},{2,0},{3,1},{4,6},{5,7},{6,4},{7,5},{8,10},{9,11},{10,... | collective-permute-start | bytes 196616 | tf_op jit(solution)/shard_map/ppermute | solution.py:22
  5.6 5.3 %collective-permute-start.4 = (bf16[256,128]{1,0:T(8,128)(2,1)S(1)}, bf16[256,128]{1,0:T(8,128)(2,1)S(1)}, u32[]{:S(2)}, u32[]{:S(2)}) collective-permute-start(bf16[256,128]{1,0:T(8,128)(2,1)S(1)} %get-tuple-element.45), channel_id=1, source_target_pairs={{0,3},{1,2},{2,1},{3,0},{4,7},{5,6},{6,5},{7,4},{8,11},{9,10},{10,... | collective-permute-start | bytes 196616 | tf_op jit(solution)/shard_map/ppermute | solution.py:22
  5.6 13.8 %collective-permute-start = (bf16[256,384]{1,0:T(8,128)(2,1)S(1)}, bf16[256,384]{1,0:T(8,128)(2,1)S(1)}, u32[]{:S(2)}, u32[]{:S(2)}) collective-permute-start(bf16[256,384]{1,0:T(8,128)(2,1)S(1)} %get-tuple-element.41), channel_id=1, source_target_pairs={{0,1},{1,0},{2,3},{3,2},{4,5},{5,4},{6,7},{7,6},{8,9},{9,8},{10,11... | collective-permute-start | bytes 589832 | tf_op jit(solution)/shard_map/ppermute | solution.py:22
  5.8 7.2 %collective-permute-start.1 = (bf16[256,256]{1,0:T(8,128)(2,1)S(1)}, bf16[256,256]{1,0:T(8,128)(2,1)S(1)}, u32[]{:S(2)}, u32[]{:S(2)}) collective-permute-start(bf16[256,256]{1,0:T(8,128)(2,1)S(1)} %get-tuple-element.42), channel_id=1, source_target_pairs={{0,2},{1,3},{2,0},{3,1},{4,6},{5,7},{6,4},{7,5},{8,10},{9,11},{10,... | collective-permute-start | bytes 393224 | tf_op jit(solution)/shard_map/ppermute | solution.py:22
  7.8 11.2 %collective-permute-start.2 = (bf16[256,256]{1,0:T(8,128)(2,1)S(1)}, bf16[256,256]{1,0:T(8,128)(2,1)S(1)}, u32[]{:S(2)}, u32[]{:S(2)}) collective-permute-start(bf16[256,256]{1,0:T(8,128)(2,1)S(1)} %get-tuple-element.43), channel_id=1, source_target_pairs={{0,3},{1,2},{2,1},{3,0},{4,7},{5,6},{6,5},{7,4},{8,11},{9,10},{10,... | collective-permute-start | bytes 393224 | tf_op jit(solution)/shard_map/ppermute | solution.py:22
  7.9 7.5 %collective-permute-start.8 = (bf16[32,512]{1,0:T(8,128)(2,1)S(1)}, bf16[32,512]{1,0:T(8,128)(2,1)S(1)}, u32[]{:S(2)}, u32[]{:S(2)}) collective-permute-start(bf16[32,512]{1,0:T(8,128)(2,1)S(1)} %get-tuple-element.55), channel_id=1, source_target_pairs={{0,4},{1,5},{2,6},{3,7},{4,0},{5,1},{6,2},{7,3},{8,12},{9,13},{10,... | collective-permute-start | bytes 98312 | tf_op jit(solution)/shard_map/ppermute | solution.py:22
  10.9 8.0 %collective-permute-start.10 = (bf16[32,512]{1,0:T(8,128)(2,1)S(1)}, bf16[32,512]{1,0:T(8,128)(2,1)S(1)}, u32[]{:S(2)}, u32[]{:S(2)}) collective-permute-start(bf16[32,512]{1,0:T(8,128)(2,1)S(1)} %get-tuple-element.56), channel_id=1, source_target_pairs={{0,6},{1,7},{2,4},{3,5},{4,2},{5,3},{6,0},{7,1},{8,14},{9,15},{10,... | collective-permute-start | bytes 98312 | tf_op jit(solution)/shard_map/ppermute | solution.py:22
  13.0 12.2 %collective-permute-start.12 = (bf16[96,512]{1,0:T(8,128)(2,1)S(1)}, bf16[96,512]{1,0:T(8,128)(2,1)S(1)}, u32[]{:S(2)}, u32[]{:S(2)}) collective-permute-start(bf16[96,512]{1,0:T(8,128)(2,1)S(1)} %get-tuple-element.57), channel_id=1, source_target_pairs={{0,4},{1,5},{2,6},{3,7},{4,0},{5,1},{6,2},{7,3},{8,12},{9,13},{10,... | collective-permute-start | bytes 294920 | tf_op jit(solution)/shard_map/ppermute | solution.py:22
  15.4 9.8 %collective-permute-start.14 = (bf16[96,512]{1,0:T(8,128)(2,1)S(1)}, bf16[96,512]{1,0:T(8,128)(2,1)S(1)}, u32[]{:S(2)}, u32[]{:S(2)}) collective-permute-start(bf16[96,512]{1,0:T(8,128)(2,1)S(1)} %get-tuple-element.58), channel_id=1, source_target_pairs={{0,6},{1,7},{2,4},{3,5},{4,2},{5,3},{6,0},{7,1},{8,14},{9,15},{10,... | collective-permute-start | bytes 294920 | tf_op jit(solution)/shard_map/ppermute | solution.py:22
  18.9 1.2 %collective-permute-start.9 = (bf16[32,512]{1,0:T(8,128)(2,1)S(1)}, bf16[32,512]{1,0:T(8,128)(2,1)S(1)}, u32[]{:S(2)}, u32[]{:S(2)}) collective-permute-start(bf16[32,512]{1,0:T(8,128)(2,1)S(1)} %collective-permute-done.8.refs_8_), channel_id=1, source_target_pairs={{0,1},{1,0},{2,3},{3,2},{4,5},{5,4},{6,7},{7,6},{8,9},{9,8},{10,11... | collective-permute-start | bytes 98312 | tf_op jit(solution)/shard_map/ppermute | solution.py:22
  19.0 1.3 %collective-permute-start.11 = (bf16[32,512]{1,0:T(8,128)(2,1)S(1)}, bf16[32,512]{1,0:T(8,128)(2,1)S(1)}, u32[]{:S(2)}, u32[]{:S(2)}) collective-permute-start(bf16[32,512]{1,0:T(8,128)(2,1)S(1)} %collective-permute-done.10.refs_10_), channel_id=1, source_target_pairs={{0,1},{1,0},{2,3},{3,2},{4,5},{5,4},{6,7},{7,6},{8,9},{9,8},{10,11... | collective-permute-start | bytes 98312 | tf_op jit(solution)/shard_map/ppermute | solution.py:22
  20.3 14.8 %collective-permute-start.16 = (bf16[256,256]{1,0:T(8,128)(2,1)S(1)}, bf16[256,256]{1,0:T(8,128)(2,1)S(1)}, u32[]{:S(2)}, u32[]{:S(2)}) collective-permute-start(bf16[256,256]{1,0:T(8,128)(2,1)S(1)} %constant_dynamic-update-slice_fusion), channel_id=1, source_target_pairs={{0,8},{8,0},{16,24},{24,16},{1,9},{9,1},{17,25},{25,17},{2,10},{10... | collective-permute-start | bytes 393224 | tf_op jit(solution)/shard_map/ppermute | solution.py:22
  21.8 13.4 %collective-permute-start.17 = (bf16[256,256]{1,0:T(8,128)(2,1)S(1)}, bf16[256,256]{1,0:T(8,128)(2,1)S(1)}, u32[]{:S(2)}, u32[]{:S(2)}) collective-permute-start(bf16[256,256]{1,0:T(8,128)(2,1)S(1)} %constant_dynamic-update-slice_fusion), channel_id=1, source_target_pairs={{0,16},{8,24},{16,0},{24,8},{1,17},{9,25},{17,1},{25,9},{2,18},{10... | collective-permute-start | bytes 393224 | tf_op jit(solution)/shard_map/ppermute | solution.py:22
  23.3 11.9 %collective-permute-start.18 = (bf16[256,256]{1,0:T(8,128)(2,1)S(1)}, bf16[256,256]{1,0:T(8,128)(2,1)S(1)}, u32[]{:S(2)}, u32[]{:S(2)}) collective-permute-start(bf16[256,256]{1,0:T(8,128)(2,1)S(1)} %constant_dynamic-update-slice_fusion), channel_id=1, source_target_pairs={{0,24},{8,16},{16,8},{24,0},{1,25},{9,17},{17,9},{25,1},{2,26},{10... | collective-permute-start | bytes 393224 | tf_op jit(solution)/shard_map/ppermute | solution.py:22
  25.2 5.4 %collective-permute-start.13 = (bf16[96,512]{1,0:T(8,128)(2,1)S(1)}, bf16[96,512]{1,0:T(8,128)(2,1)S(1)}, u32[]{:S(2)}, u32[]{:S(2)}) collective-permute-start(bf16[96,512]{1,0:T(8,128)(2,1)S(1)} %collective-permute-done.12.refs_12_), channel_id=1, source_target_pairs={{0,1},{1,0},{2,3},{3,2},{4,5},{5,4},{6,7},{7,6},{8,9},{9,8},{10,11... | collective-permute-start | bytes 294920 | tf_op jit(solution)/shard_map/ppermute | solution.py:22
  25.2 5.5 %collective-permute-start.15 = (bf16[96,512]{1,0:T(8,128)(2,1)S(1)}, bf16[96,512]{1,0:T(8,128)(2,1)S(1)}, u32[]{:S(2)}, u32[]{:S(2)}) collective-permute-start(bf16[96,512]{1,0:T(8,128)(2,1)S(1)} %collective-permute-done.14.refs_14_), channel_id=1, source_target_pairs={{0,1},{1,0},{2,3},{3,2},{4,5},{5,4},{6,7},{7,6},{8,9},{9,8},{10,11... | collective-permute-start | bytes 294920 | tf_op jit(solution)/shard_map/ppermute | solution.py:22
  30.6 8.0 %collective-permute-start.5 = (bf16[128,128]{1,0:T(8,128)(2,1)S(1)}, bf16[128,128]{1,0:T(8,128)(2,1)S(1)}, u32[]{:S(2)}, u32[]{:S(2)}) collective-permute-start(bf16[128,128]{1,0:T(8,128)(2,1)S(1)} %get-tuple-element.48), channel_id=1, source_target_pairs={{0,1},{1,0},{2,3},{3,2},{4,5},{5,4},{6,7},{7,6},{8,9},{9,8},{10,11... | collective-permute-start | bytes 98312 | tf_op jit(solution)/shard_map/ppermute | solution.py:22
  30.7 7.9 %collective-permute-start.6 = (bf16[128,128]{1,0:T(8,128)(2,1)S(1)}, bf16[128,128]{1,0:T(8,128)(2,1)S(1)}, u32[]{:S(2)}, u32[]{:S(2)}) collective-permute-start(bf16[128,128]{1,0:T(8,128)(2,1)S(1)} %get-tuple-element.49), channel_id=1, source_target_pairs={{0,2},{1,3},{2,0},{3,1},{4,6},{5,7},{6,4},{7,5},{8,10},{9,11},{10,... | collective-permute-start | bytes 98312 | tf_op jit(solution)/shard_map/ppermute | solution.py:22
  35.1 7.2 %copy-start = (bf16[512,768]{1,0:T(8,128)(2,1)S(1)}, bf16[512,768]{1,0:T(8,128)(2,1)}, u32[]{:S(2)}) copy-start(bf16[512,768]{1,0:T(8,128)(2,1)} %weight_ref.1) | copy-start | bytes 2359300
  35.1 3.7 %collective-permute-start.7 = (bf16[128,128]{1,0:T(8,128)(2,1)S(1)}, bf16[128,128]{1,0:T(8,128)(2,1)S(1)}, u32[]{:S(2)}, u32[]{:S(2)}) collective-permute-start(bf16[128,128]{1,0:T(8,128)(2,1)S(1)} %get-tuple-element.50), channel_id=1, source_target_pairs={{0,3},{1,2},{2,1},{3,0},{4,7},{5,6},{6,5},{7,4},{8,11},{9,10},{10,... | collective-permute-start | bytes 98312 | tf_op jit(solution)/shard_map/ppermute | solution.py:22
  36.4 2.7 %collective-permute-start.19 = (bf16[128,128]{1,0:T(8,128)(2,1)S(1)}, bf16[128,128]{1,0:T(8,128)(2,1)S(1)}, u32[]{:S(2)}, u32[]{:S(2)}) collective-permute-start(bf16[128,128]{1,0:T(8,128)(2,1)S(1)} %get-tuple-element.70), channel_id=1, source_target_pairs={{0,1},{1,0},{2,3},{3,2},{4,5},{5,4},{6,7},{7,6},{8,9},{9,8},{10,11... | collective-permute-start | bytes 98312 | tf_op jit(solution)/shard_map/ppermute | solution.py:22
  36.5 3.9 %collective-permute-start.20 = (bf16[128,128]{1,0:T(8,128)(2,1)S(1)}, bf16[128,128]{1,0:T(8,128)(2,1)S(1)}, u32[]{:S(2)}, u32[]{:S(2)}) collective-permute-start(bf16[128,128]{1,0:T(8,128)(2,1)S(1)} %get-tuple-element.71), channel_id=1, source_target_pairs={{0,2},{1,3},{2,0},{3,1},{4,6},{5,7},{6,4},{7,5},{8,10},{9,11},{10,... | collective-permute-start | bytes 98312 | tf_op jit(solution)/shard_map/ppermute | solution.py:22
  38.6 3.7 %collective-permute-start.21 = (bf16[128,128]{1,0:T(8,128)(2,1)S(1)}, bf16[128,128]{1,0:T(8,128)(2,1)S(1)}, u32[]{:S(2)}, u32[]{:S(2)}) collective-permute-start(bf16[128,128]{1,0:T(8,128)(2,1)S(1)} %get-tuple-element.72), channel_id=1, source_target_pairs={{0,3},{1,2},{2,1},{3,0},{4,7},{5,6},{6,5},{7,4},{8,11},{9,10},{10,... | collective-permute-start | bytes 98312 | tf_op jit(solution)/shard_map/ppermute | solution.py:22

commit v4 on v3

--- a/solution.py
+++ b/solution.py
@@ -80,8 +80,9 @@
     for s, x in enumerate((2, 3, 0, 1)):
         pair = plan.pair() ^ x
         one_hot = [pick(wrapped, 2 * pair + t, rows) for t in range(2)]
-        for part in range(3):
-            copies[3 * s + part].wait()
+        if s % 2 == 0:
+            for copy in copies[3 * s : 3 * s + 6]:
+                copy.wait()
         block = jnp.concatenate([taken[x, part] for part in range(3)], axis=1)
         one, two = [dot(m, block, ((1,), (0,))) for m in one_hot]
         query = jnp.where(first, one[:, :LANES], two[:, :LANES]) * HEAD_DIM**-0.5
@@ -118,20 +119,6 @@
     return (positions >= starts) & (positions < ends)
 
 
-def features(plan, table_ref, t, base, slot_shift, count):
-    r = lax.broadcasted_iota(jnp.int32, (count, LANES), 0)
-    lane = lax.broadcasted_iota(jnp.int32, (count, LANES), 1)
-    head = 2 * plan.pair() + t
-    source = plan.me() ^ (base + (r >> slot_shift))
-    k = r & ((1 << slot_shift) - 1)
-    position = source * plan.rows + ((plan.source_row(k) + head) & (plan.rows - 1))
-    starts = table_ref[2 * t : 2 * t + 1, :]
-    ends = table_ref[2 * t + 1 : 2 * t + 2, :]
-    inside = (position >= starts) & (position < ends)
-    own = (lane < HEAD_DIM) if t == 0 else (lane >= HEAD_DIM)
-    return inside, own
-
-
 def as_query(block, inside, own):
     return jnp.where(own, block.astype(F32), jnp.where(inside, BARRED, 0.0)).astype(BF16)
 
@@ -166,7 +153,7 @@
         before, rests, refs = refs[0], refs[1 : 1 + group], refs[1 + group :]
     else:
         rest, refs = refs[0], refs[1:]
-    sums_ref, maxima_ref, q_s, k_s, v_s, v2_s, vt_s = refs
+    sums_ref, maxima_ref, q_mid, q_s, k_s, v_s, vt_s, s_s = refs
     queries, firsts, seconds = chunks(own, near, leads, seconds)
     positions = block_positions(plan, t, rows)
     lane = lax.broadcasted_iota(jnp.int32, (rows, LANES), 1)
@@ -177,26 +164,33 @@
         mid_here = pl.ds(x * mid_rows, mid_rows)
         inside = block_inside(plan, table_ref, t, positions, x)
         kv = (seconds if t else firsts)[x][...].astype(F32)
-        q_s[here, :] = as_query(queries[x][...], inside, keys)
+        query = as_query(queries[x][...], inside, keys)
+        q_s[here, :] = query
+        q_mid[mid_here, :] = query[:mid_rows]
         k_s[here, :] = as_key(kv, inside, keys)
         value = as_value(kv, keys)
         low = value.astype(BF16)
-        v_s[here, :] = low
-        v2_s[pl.ds(x * rows, mid_rows), :] = (2.0 * value[:mid_rows]).astype(BF16)
-        v2_s[pl.ds(x * rows + mid_rows, rows - mid_rows), :] = low[mid_rows:]
+        v_s[here, :LANES] = low
+        v_s[pl.ds(x * rows, mid_rows), LANES:] = (2.0 * value[:mid_rows]).astype(BF16)
+        v_s[pl.ds(x * rows + mid_rows, rows - mid_rows), LANES:] = low[mid_rows:]
         vt_s[mid_here, :] = jnp.where(is_top, value[:mid_rows], 0.0).astype(BF16)
     lane = lax.broadcasted_iota(jnp.int32, (rows - mid_rows, LANES), 1)
     for x in range(group):
         here = pl.ds(x * rows, rows)
         mid_here = pl.ds(x * mid_rows, mid_rows)
         rest_here = pl.ds(x * (rows - mid_rows), rows - mid_rows)
-        scores = dot(q_s[here, :], k_s[...], ((1,), (1,)))
+        if x == 0:
+            s_s[0] = dot(q_s[here, :], k_s[...], ((1,), (1,)))
+        if x + 1 < group:
+            there = pl.ds((x + 1) * rows, rows)
+            s_s[(x + 1) % 2] = dot(q_s[there, :], k_s[...], ((1,), (1,)))
+        scores = s_s[x % 2]
         largest = jnp.max(scores, axis=1, keepdims=True)
         probs = jnp.exp(scores - largest).astype(BF16)
-        mid_sum = dot(probs[:mid_rows], v2_s[...], ((1,), (0,)))
+        mid_sum = dot(probs[:mid_rows], v_s[:, LANES:], ((1,), (0,)))
         top_probs = [probs[:tile, y * rows : y * rows + mid_rows] for y in range(group)]
         top_sum = dot(jnp.concatenate(top_probs, axis=1), vt_s[...], ((1,), (0,)))
-        rest_sum = share(dot(probs[mid_rows:], v_s[...], ((1,), (0,))))
+        rest_sum = share(dot(probs[mid_rows:], v_s[:, :LANES], ((1,), (0,))))
         top_sum = jnp.where(row_iota(tile) < plan.top_rows, top_sum, 0.0)
         sums_ref[mid_here, :] = mid_sum
         sums_ref[pl.ds(x * mid_rows, tile), :] += top_sum
@@ -222,17 +216,13 @@
 def mid_kernel(plan, table_ref, *refs):
     group, mid_rows, tile = plan.group, plan.mid_rows, plan.top_tile
     n = plan.inner - group
-    states, refs = refs[:4], refs[4:]
-    queries, refs = [ref.at[:, :LANES] for ref in refs[:4]], refs[4:]
+    states, refs = refs[:6], refs[6:]
     heads, tails, refs = other_chunks(refs[:n]), other_chunks(refs[n : 2 * n]), refs[2 * n :]
-    outs, lead_states, (k_s, v_s, vt_s) = refs[:group], refs[group : group + 6], refs[group + 6 :]
+    outs, lead_states, (k_s, v_s, vt_s, s_s) = refs[:group], refs[group : group + 6], refs[group + 6 :]
     count = group * mid_rows
-    queries = jnp.concatenate([query[:mid_rows, :] for query in queries], axis=0)
     key_lane = lax.broadcasted_iota(jnp.int32, (mid_rows, LANES), 1)
     results = []
     for t in range(2):
-        inside, own = features(plan, table_ref, t, 0, shift_of(mid_rows), count)
-        q = as_query(queries, inside, own)
         positions = block_positions(plan, t, mid_rows)
         keys = (key_lane < HEAD_DIM) if t == 0 else (key_lane >= HEAD_DIM)
         columns = slice(t * LANES, (t + 1) * LANES)
@@ -246,28 +236,30 @@
                 kv = ref[:, columns].astype(F32)
                 there = pl.ds(at, high - low)
                 value = as_value(kv, keys[low:high])
-                k_s[there, :] = as_key(kv, inside[low:high], keys[low:high])
-                v_s[there, :] = value.astype(BF16)
+                k_s[t, there, :] = as_key(kv, inside[low:high], keys[low:high])
+                v_s[t, there, :] = value.astype(BF16)
                 if low == 0:
                     is_top = row_iota(tile) < plan.top_rows
-                    vt_s[there, :] = jnp.where(is_top, value, 0.0).astype(BF16)
-        old = states[2 * t + 1][:, :1]
-        scores = dot(q, k_s[...], ((1,), (1,)))
+                    vt_s[t, there, :] = jnp.where(is_top, value, 0.0).astype(BF16)
+        s_s[t] = dot(states[3 * t + 2][...], k_s[t], ((1,), (1,)))
+    for t in range(2):
+        old = states[3 * t + 1][...]
+        scores = s_s[t]
         new = jnp.maximum(old, jnp.max(scores, axis=1, keepdims=True))
-        probs = jnp.exp(scores - new).astype(BF16)
-        sums = states[2 * t][...] * jnp.exp(old - new)
-        sums = sums + dot(probs, v_s[...], ((1,), (0,)))
+        probs = jnp.exp(scores - new[:, :1]).astype(BF16)
+        sums = states[3 * t][...] * jnp.exp(old - new)
+        sums = sums + dot(probs, v_s[t], ((1,), (0,)))
 
         def leading(array):
             return jnp.concatenate(
                 [array[x * mid_rows : x * mid_rows + tile] for x in range(group)], axis=0
             )
 
-        extra = dot(leading(probs[:, : n * tile]), vt_s[...], ((1,), (0,)))
+        extra = dot(leading(probs[:, : n * tile]), vt_s[t], ((1,), (0,)))
         keep = (row_iota(group * tile) & (tile - 1)) < plan.top_rows
         lead_states[3 * t][...] = leading(sums) + jnp.where(keep, extra, 0.0)
-        lead_states[3 * t + 1][...] = jnp.broadcast_to(leading(new), (group * tile, LANES))
-        lead_states[3 * t + 2][...] = leading(q)
+        lead_states[3 * t + 1][...] = leading(new)
+        lead_states[3 * t + 2][...] = leading(states[3 * t + 2])
         results.append(share(sums))
     lane = lax.broadcasted_iota(jnp.int32, (count, LANES), 1)
     both = jnp.where(lane < HEAD_DIM, results[0], results[1]).astype(BF16)
@@ -279,24 +271,36 @@
     group, tile = plan.group, plan.top_tile
     states, refs = refs[:6], refs[6:]
     middles, refs = refs[:group], refs[group:]
-    tops, outs = refs[: plan.outer - 1], refs[plan.outer - 1 :]
+    tops, refs = refs[: plan.outer - 1], refs[plan.outer - 1 :]
+    outs, (k_s, v_s, s_s) = refs[:group], refs[group:]
     count = group * tile
     shift = shift_of(plan.top_rows)
     is_top = (row_iota(count) & (tile - 1)) < plan.top_rows
+    n = tops[0].shape[0]
+    row = row_iota(n)
+    key_lane = lax.broadcasted_iota(jnp.int32, (n, LANES), 1)
+    source = plan.me() ^ (row >> shift)
+    bases = [(source ^ (e * plan.inner)) * plan.rows for e in range(1, plan.outer)]
+    for t in range(2):
+        keys = (key_lane < HEAD_DIM) if t == 0 else (key_lane >= HEAD_DIM)
+        head = 2 * plan.pair() + t
+        offset = (plan.source_row(row & (plan.top_rows - 1)) + head) & (plan.rows - 1)
+        starts, ends = table_ref[2 * t : 2 * t + 1, :], table_ref[2 * t + 1 : 2 * t + 2, :]
+        for e in range(1, plan.outer):
+            kv = tops[e - 1][:, t * LANES : (t + 1) * LANES].astype(F32)
+            position = bases[e - 1] + offset
+            inside = (position >= starts) & (position < ends)
+            there = pl.ds((e - 1) * n, n)
+            k_s[t, there, :] = as_key(kv, inside, keys)
+            v_s[t, there, :] = as_value(kv, keys).astype(BF16)
+        s_s[t] = dot(states[3 * t + 2][...], k_s[t], ((1,), (1,)))
     results = []
     for t in range(2):
-        keys, values = [], []
-        for e in range(1, plan.outer):
-            kv = tops[e - 1][:, t * LANES : (t + 1) * LANES]
-            inside, own = features(plan, table_ref, t, e * plan.inner, shift, kv.shape[0])
-            keys.append(as_key(kv, inside, own))
-            values.append(as_value(kv, own).astype(BF16))
-        sums, old, q = states[3 * t][...], states[3 * t + 1][:, :1], states[3 * t + 2][...]
-        scores = dot(q, jnp.concatenate(keys, axis=0), ((1,), (1,)))
+        sums, old = states[3 * t][...], states[3 * t + 1][...]
+        scores = s_s[t]
         new = jnp.maximum(old, jnp.max(scores, axis=1, keepdims=True))
-        probs = jnp.exp(scores - new).astype(BF16)
-        merged = sums * jnp.exp(old - new)
-        merged = merged + dot(probs, jnp.concatenate(values, axis=0), ((1,), (0,)))
+        probs = jnp.exp(scores - new[:, :1]).astype(BF16)
+        merged = sums * jnp.exp(old - new) + dot(probs, v_s[t], ((1,), (0,)))
         results.append(share(jnp.where(is_top, merged, sums)))
     lane = lax.broadcasted_iota(jnp.int32, (count, LANES), 1)
     both = jnp.where(lane < HEAD_DIM, results[0], results[1]).astype(BF16)
@@ -403,42 +407,49 @@
     tops = [exchange(top_own, "outer", x) for x in range(1, plan.outer)]
 
     count = group * rows
-    scratch = [pltpu.VMEM((count, LANES), BF16)] * 4
+    scratch = [pltpu.VMEM((count, LANES), BF16)] * 2
+    scratch += [pltpu.VMEM((count, 2 * LANES), BF16)]
     scratch += [pltpu.VMEM((group * mid_rows, LANES), BF16)]
-    state = [shape(group * mid_rows, LANES, F32)] * 2
-    rest_one, sums_one, maxima_one = call(
+    scratch += [pltpu.VMEM((2, rows, count), F32)]
+    state = [shape(group * mid_rows, LANES, F32)] * 2 + [shape(group * mid_rows, LANES)]
+    rest_one, *state_one = call(
         functools.partial(local_kernel, plan, 0),
         (table, own, near, *leads),
         [shape(group * (rows - mid_rows), LANES, F32), *state],
         scratch,
     )
-    *rests, sums_two, maxima_two = call(
+    local_two = call(
         functools.partial(local_kernel, plan, 1),
         (table, own, near, *leads, *seconds, rest_one),
         [shape(rows - mid_rows, LANES)] * group + state,
         scratch,
     )
+    rests, state_two = local_two[:group], local_two[group:]
     rests = [rests[0]] + [exchange(rests[x], "inner", x) for x in range(1, group)]
     lead_state = [shape(group * tile, LANES, F32)] * 2 + [shape(group * tile, LANES)]
+    n_top = (plan.outer - 1) * plan.inner * plan.top_rows
     n_mid = (plan.inner - group) * mid_rows
     middle = call(
         functools.partial(mid_kernel, plan),
         (
             table,
-            *(sums_one, maxima_one, sums_two, maxima_two),
-            *(own, near, *leads),
+            *state_one,
+            *state_two,
             *other_heads,
             *other_tails,
         ),
         [shape(mid_rows - tile, LANES)] * group + lead_state * 2,
-        [pltpu.VMEM((n_mid, LANES), BF16)] * 2
-        + [pltpu.VMEM(((plan.inner - group) * tile, LANES), BF16)],
+        [pltpu.VMEM((2, n_mid, LANES), BF16)] * 2
+        + [pltpu.VMEM((2, (plan.inner - group) * tile, LANES), BF16)]
+        + [pltpu.VMEM((2, group * mid_rows, n_mid), F32)],
     )
     middles, lead_state = middle[:group], middle[group:]
     uppers = call(
         functools.partial(top_kernel, plan),
         (table, *lead_state, *middles, *tops),
         [shape(mid_rows, LANES)] * group,
+        [pltpu.VMEM((2, n_top, LANES), BF16)] * 2
+        + [pltpu.VMEM((2, group * tile, n_top), F32)],
     )
     uppers = [uppers[0]] + [exchange(uppers[x], "inner", x) for x in range(1, group)]
     ordered = call(functools.partial(order_kernel, plan), rests, [shape(rows, HEADS * HEAD_DIM)])[0]

time: 43.8 us -> 41.4 us (0.945)
  Pallas kernels: 12.3 us -> 9.92 us
    pallas_call x7, Pallas kernels: 12.3 us -> 9.92 us  [call(): pl.pallas_call(kernel, in_specs=in_specs or [vmem] * len(operands), out_s...]
  transfers between devices with their start and end apart: 22 -> 22, of which waited for: 9 -> 9; matrix products, arithmetic and copies ran while one was open for 0% -> 0% of each run, Pallas kernels for 19% -> 15%
where the time goes in v4:
time: 41.4 us; the launch traced here: 41.2 us
  starting transfers between devices  23.8 us (57%)
  Pallas kernels  9.92 us (24%)
  waiting for transfers between devices  7.35 us (18%)
    ppermute x22, starting transfers between devices, exchange(): return lax.ppermute(block, axis, [(i, i ^ distance) for i in range(count)])  23.8 us
    pallas_call x7, Pallas kernels, call(): pl.pallas_call(kernel, in_specs=in_specs or [vmem] * len(operands), out_s...  9.92 us
    ppermute x22, waiting for transfers between devices, exchange(): return lax.ppermute(block, axis, [(i, i ^ distance) for i in range(count)])  7.35 us
  transfers between devices with their start and end apart: 22, of which 9 were waited for; matrix products, arithmetic and copies ran while one was open for 0% of the time, Pallas kernels for 15%

profile of v4, /device:TPU:0, one launch (start us, length us, event | category | flops | bytes accessed | tf_op | source)
XLA Modules:
  0.0 41.2 jit_solution(16442779359792134080)
XLA Ops:
  0.0 2.2 %shard_map.55 = (bf16[256,384]{1,0:T(8,128)(2,1)S(1)}, bf16[256,384]{1,0:T(8,128)(2,1)S(1)}, bf16[256,256]{1,0:T(8,128)(2,1)S(1)}, bf16[256,256]{1,0:T(8,128)(2,...) custom-call(s32[16]{0:T(128)} %lengths_ref.1, ...), custom_call_target="tpu_custom_call" | custom-call | tf_op jit(solution)/shard_map/pallas_call | solution.py:358
  2.2 3.1 %collective-permute-start.3 = (bf16[256,128]{1,0:T(8,128)(2,1)S(1)}, bf16[256,128]{1,0:T(8,128)(2,1)S(1)}, u32[]{:S(2)}, u32[]{:S(2)}) collective-permute-start(bf16[256,128]{1,0:T(8,128)(2,1)S(1)} %get-tuple-element.46), channel_id=1, source_target_pairs={{0,2},{1,3},{2,0},{3,1},{4,6},{5,7},{6,4},{7,5},{8,10},{9,11},{10,... | collective-permute-start | bytes 196616 | tf_op jit(solution)/shard_map/ppermute | solution.py:22
  5.3 0.0 collective-permute-start.4
  5.3 0.2 collective-permute-start
  5.5 1.9 %collective-permute-start.1 = (bf16[256,256]{1,0:T(8,128)(2,1)S(1)}, bf16[256,256]{1,0:T(8,128)(2,1)S(1)}, u32[]{:S(2)}, u32[]{:S(2)}) collective-permute-start(bf16[256,256]{1,0:T(8,128)(2,1)S(1)} %get-tuple-element.44), channel_id=1, source_target_pairs={{0,2},{1,3},{2,0},{3,1},{4,6},{5,7},{6,4},{7,5},{8,10},{9,11},{10,... | collective-permute-start | bytes 393224 | tf_op jit(solution)/shard_map/ppermute | solution.py:22
  7.4 0.0 collective-permute-start.2
  7.4 0.1 collective-permute-done.3.refs_2_
  7.5 3.0 %collective-permute-start.8 = (bf16[32,512]{1,0:T(8,128)(2,1)S(1)}, bf16[32,512]{1,0:T(8,128)(2,1)S(1)}, u32[]{:S(2)}, u32[]{:S(2)}) collective-permute-start(bf16[32,512]{1,0:T(8,128)(2,1)S(1)} %get-tuple-element.59), channel_id=1, source_target_pairs={{0,4},{1,5},{2,6},{3,7},{4,0},{5,1},{6,2},{7,3},{8,12},{9,13},{10,... | collective-permute-start | bytes 98312 | tf_op jit(solution)/shard_map/ppermute | solution.py:22
  10.6 0.0 collective-permute-done.4.refs_3_
  10.6 1.7 %collective-permute-start.10 = (bf16[32,512]{1,0:T(8,128)(2,1)S(1)}, bf16[32,512]{1,0:T(8,128)(2,1)S(1)}, u32[]{:S(2)}, u32[]{:S(2)}) collective-permute-start(bf16[32,512]{1,0:T(8,128)(2,1)S(1)} %get-tuple-element.60), channel_id=1, source_target_pairs={{0,6},{1,7},{2,4},{3,5},{4,2},{5,3},{6,0},{7,1},{8,14},{9,15},{10,... | collective-permute-start | bytes 98312 | tf_op jit(solution)/shard_map/ppermute | solution.py:22
  12.3 0.4 collective-permute-done.1.refs_0_
  12.7 2.4 %collective-permute-start.12 = (bf16[96,512]{1,0:T(8,128)(2,1)S(1)}, bf16[96,512]{1,0:T(8,128)(2,1)S(1)}, u32[]{:S(2)}, u32[]{:S(2)}) collective-permute-start(bf16[96,512]{1,0:T(8,128)(2,1)S(1)} %get-tuple-element.61), channel_id=1, source_target_pairs={{0,4},{1,5},{2,6},{3,7},{4,0},{5,1},{6,2},{7,3},{8,12},{9,13},{10,... | collective-permute-start | bytes 294920 | tf_op jit(solution)/shard_map/ppermute | solution.py:22
  15.0 0.0 collective-permute-done.8.refs_6_
  15.0 2.3 %collective-permute-start.14 = (bf16[96,512]{1,0:T(8,128)(2,1)S(1)}, bf16[96,512]{1,0:T(8,128)(2,1)S(1)}, u32[]{:S(2)}, u32[]{:S(2)}) collective-permute-start(bf16[96,512]{1,0:T(8,128)(2,1)S(1)} %get-tuple-element.62), channel_id=1, source_target_pairs={{0,6},{1,7},{2,4},{3,5},{4,2},{5,3},{6,0},{7,1},{8,14},{9,15},{10,... | collective-permute-start | bytes 294920 | tf_op jit(solution)/shard_map/ppermute | solution.py:22
  17.3 1.3 %collective-permute-done.10.refs_8_ = bf16[32,512]{1,0:T(8,128)(2,1)S(1)} collective-permute-done((bf16[32,512]{1,0:T(8,128)(2,1)S(1)}, bf16[32,512]{1,0:T(8,128)(2,1)S(1)}, u32[]{:S(2)}, u32[]{:S(2)}) %collective-permute-start.10) | collective-permute-done | bytes 32800 | tf_op jit(solution)/shard_map/ppermute | solution.py:22
  18.6 0.1 collective-permute-start.9
  18.6 0.0 collective-permute-done.2.refs_1_
  18.6 0.5 %collective-permute-start.11 = (bf16[32,512]{1,0:T(8,128)(2,1)S(1)}, bf16[32,512]{1,0:T(8,128)(2,1)S(1)}, u32[]{:S(2)}, u32[]{:S(2)}) collective-permute-start(bf16[32,512]{1,0:T(8,128)(2,1)S(1)} %collective-permute-done.10.refs_8_), channel_id=1, source_target_pairs={{0,1},{1,0},{2,3},{3,2},{4,5},{5,4},{6,7},{7,6},{8,9},{9,8},{10,11... | collective-permute-start | bytes 98312 | tf_op jit(solution)/shard_map/ppermute | solution.py:22
  19.1 0.0 collective-permute-done.near
  19.1 0.7 %collective-permute-done.9.refs_7_ = bf16[32,512]{1,0:T(8,128)(2,1)S(1)} collective-permute-done((bf16[32,512]{1,0:T(8,128)(2,1)S(1)}, bf16[32,512]{1,0:T(8,128)(2,1)S(1)}, u32[]{:S(2)}, u32[]{:S(2)}) %collective-permute-start.9) | collective-permute-done | bytes 32800 | tf_op jit(solution)/shard_map/ppermute | solution.py:22
  19.8 0.2 collective-permute-done.11.refs_9_
  20.0 1.5 %collective-permute-start.16 = (bf16[256,256]{1,0:T(8,128)(2,1)S(1)}, bf16[256,256]{1,0:T(8,128)(2,1)S(1)}, u32[]{:S(2)}, u32[]{:S(2)}) collective-permute-start(bf16[256,256]{1,0:T(8,128)(2,1)S(1)} %constant_dynamic-update-slice_fusion), channel_id=1, source_target_pairs={{0,8},{8,0},{16,24},{24,16},{1,9},{9,1},{17,25},{25,17},{2,10},{10... | collective-permute-start | bytes 393224 | tf_op jit(solution)/shard_map/ppermute | solution.py:22
  21.4 1.5 %collective-permute-start.17 = (bf16[256,256]{1,0:T(8,128)(2,1)S(1)}, bf16[256,256]{1,0:T(8,128)(2,1)S(1)}, u32[]{:S(2)}, u32[]{:S(2)}) collective-permute-start(bf16[256,256]{1,0:T(8,128)(2,1)S(1)} %constant_dynamic-update-slice_fusion), channel_id=1, source_target_pairs={{0,16},{8,24},{16,0},{24,8},{1,17},{9,25},{17,1},{25,9},{2,18},{10... | collective-permute-start | bytes 393224 | tf_op jit(solution)/shard_map/ppermute | solution.py:22
  23.0 0.5 %collective-permute-start.18 = (bf16[256,256]{1,0:T(8,128)(2,1)S(1)}, bf16[256,256]{1,0:T(8,128)(2,1)S(1)}, u32[]{:S(2)}, u32[]{:S(2)}) collective-permute-start(bf16[256,256]{1,0:T(8,128)(2,1)S(1)} %constant_dynamic-update-slice_fusion), channel_id=1, source_target_pairs={{0,24},{8,16},{16,8},{24,0},{1,25},{9,17},{17,9},{25,1},{2,26},{10... | collective-permute-start | bytes 393224 | tf_op jit(solution)/shard_map/ppermute | solution.py:22
  23.4 1.4 %collective-permute-done.12.refs_10_ = bf16[96,512]{1,0:T(8,128)(2,1)S(1)} collective-permute-done((bf16[96,512]{1,0:T(8,128)(2,1)S(1)}, bf16[96,512]{1,0:T(8,128)(2,1)S(1)}, u32[]{:S(2)}, u32[]{:S(2)}) %collective-permute-start.12) | collective-permute-done | bytes 98336 | tf_op jit(solution)/shard_map/ppermute | solution.py:22
  24.9 0.0 collective-permute-start.13
  24.9 0.0 collective-permute-done.14.refs_12_
  24.9 0.5 %collective-permute-start.15 = (bf16[96,512]{1,0:T(8,128)(2,1)S(1)}, bf16[96,512]{1,0:T(8,128)(2,1)S(1)}, u32[]{:S(2)}, u32[]{:S(2)}) collective-permute-start(bf16[96,512]{1,0:T(8,128)(2,1)S(1)} %collective-permute-done.14.refs_12_), channel_id=1, source_target_pairs={{0,1},{1,0},{2,3},{3,2},{4,5},{5,4},{6,7},{7,6},{8,9},{9,8},{10,11... | collective-permute-start | bytes 294920 | tf_op jit(solution)/shard_map/ppermute | solution.py:22
  25.4 1.8 %shard_map.56 = (f32[512,128]{1,0:T(8,128)S(1)}, f32[512,128]{1,0:T(8,128)S(1)}, f32[512,128]{1,0:T(8,128)S(1)}, bf16[512,128]{1,0:T(8,128)(2,1)S(1)}) custom-call(s32[8,128]{1,0:T(8,128)S(1)} %get-tuple-element.41.table_ref, bf16[256,384]{1,0:T(8,128)(2,1)S(1)} %get-tuple-element.42.own, bf16[256,384]{1,0:T(8,128)(2,1)S(1)} %collective-permute-done.near, ...), custom_call_target="tpu_custom_call" | custom-call | tf_op jit(solution)/shard_map/pallas_call | solution.py:358
  27.2 1.8 %shard_map.57 = (bf16[128,128]{1,0:T(8,128)(2,1)S(1)}, bf16[128,128]{1,0:T(8,128)(2,1)S(1)}, bf16[128,128]{1,0:T(8,128)(2,1)S(1)}, bf16[128,128]{1,0:T(8,128)(2,...) custom-call(s32[8,128]{1,0:T(8,128)S(1)} %get-tuple-element.41.table_ref, ...), custom_call_target="tpu_custom_call" | custom-call | tf_op jit(solution)/shard_map/pallas_call | solution.py:358
  29.1 0.1 collective-permute-start.5
  29.1 0.0 collective-permute-done.15.refs_13_
  29.1 2.3 %collective-permute-start.6 = (bf16[128,128]{1,0:T(8,128)(2,1)S(1)}, bf16[128,128]{1,0:T(8,128)(2,1)S(1)}, u32[]{:S(2)}, u32[]{:S(2)}) collective-permute-start(bf16[128,128]{1,0:T(8,128)(2,1)S(1)} %get-tuple-element.51), channel_id=1, source_target_pairs={{0,2},{1,3},{2,0},{3,1},{4,6},{5,7},{6,4},{7,5},{8,10},{9,11},{10,... | collective-permute-start | bytes 98312 | tf_op jit(solution)/shard_map/ppermute | solution.py:22
  31.4 1.4 %shard_map.59 = (bf16[96,128]{1,0:T(8,128)(2,1)S(1)}, bf16[96,128]{1,0:T(8,128)(2,1)S(1)}, bf16[96,128]{1,0:T(8,128)(2,1)S(1)}, bf16[96,128]{1,0:T(8,128)(2,1)S(...) custom-call(s32[8,128]{1,0:T(8,128)S(1)} %get-tuple-element.41.table, ...), custom_call_target="tpu_custom_call" | custom-call | tf_op jit(solution)/shard_map/pallas_call | solution.py:358
  32.8 0.0 collective-permute-done.16.refs_10_
  32.8 0.1 collective-permute-start.7
  32.9 0.0 collective-permute-done.17.refs_11_
  32.9 0.0 collective-permute-done.18.refs_12_
  32.9 1.0 %shard_map.60 = (bf16[128,128]{1,0:T(8,128)(2,1)S(1)}, bf16[128,128]{1,0:T(8,128)(2,1)S(1)}, bf16[128,128]{1,0:T(8,128)(2,1)S(1)}, bf16[128,128]{1,0:T(8,128)(2,1)S(1)}) custom-call(s32[8,128]{1,0:T(8,128)S(1)} %get-tuple-element.41.table_ref, f32[128,128]{1,0:T(8,128)S(1)} %get-tuple-element.63.refs_0_, f32[128,128]{1,0:T(8,128)S(1)} %get-tuple-element.64.refs_1_, ...), custom_call_target="tpu_custom_call" | custom-call | tf_op jit(solution)/shard_map/pallas_call | solution.py:358
  34.0 0.2 collective-permute-start.19
  34.1 2.0 %collective-permute-start.20 = (bf16[128,128]{1,0:T(8,128)(2,1)S(1)}, bf16[128,128]{1,0:T(8,128)(2,1)S(1)}, u32[]{:S(2)}, u32[]{:S(2)}) collective-permute-start(bf16[128,128]{1,0:T(8,128)(2,1)S(1)} %get-tuple-element.75), channel_id=1, source_target_pairs={{0,2},{1,3},{2,0},{3,1},{4,6},{5,7},{6,4},{7,5},{8,10},{9,11},{10,... | collective-permute-start | bytes 98312 | tf_op jit(solution)/shard_map/ppermute | solution.py:22
  36.2 0.0 collective-permute-done.5.refs_1_
  36.2 0.4 collective-permute-done.7.refs_3_
  36.6 0.3 shard_map.58.rest_ref
  36.9 0.0 collective-permute-done.19.refs_1_
  36.9 1.2 %collective-permute-done.20.refs_2_ = bf16[128,128]{1,0:T(8,128)(2,1)S(1)} collective-permute-done((bf16[128,128]{1,0:T(8,128)(2,1)S(1)}, bf16[128,128]{1,0:T(8,128)(2,1)S(1)}, u32[]{:S(2)}, u32[]{:S(2)}) %collective-permute-start.20) | collective-permute-done | bytes 32800 | tf_op jit(solution)/shard_map/ppermute | solution.py:22
  38.0 1.8 %collective-permute-done.21.refs_3_ = bf16[128,128]{1,0:T(8,128)(2,1)S(1)} collective-permute-done((bf16[128,128]{1,0:T(8,128)(2,1)S(1)}, bf16[128,128]{1,0:T(8,128)(2,1)S(1)}, u32[]{:S(2)}, u32[]{:S(2)}) %collective-permute-start.21) | collective-permute-done | bytes 32800 | tf_op jit(solution)/shard_map/ppermute | solution.py:22
  39.8 1.4 %shard_map.61 = bf16[256,768]{1,0:T(8,128)(2,1)} custom-call(bf16[512,768]{1,0:T(8,128)(2,1)S(1)} %copy-done, bf16[256,512]{1,0:T(8,128)(2,1)S(1)} %shard_map.58.rest_ref, bf16[128,128]{1,0:T(8,128)(2,1)S(1)} %get-tuple-element.73.refs_0_, bf16[128,128]{1,0:T(8,128)(2,1)S(1)} %collective-permute-done.19.refs_1_, ...), custom_call_target="tpu_custom_call" | custom-call | tf_op jit(solution)/shard_map/pallas_call | solution.py:358
  (17 shorter events, 0.0 us)
Async XLA Ops:
  2.2 5.4 %collective-permute-start.3 = (bf16[256,128]{1,0:T(8,128)(2,1)S(1)}, bf16[256,128]{1,0:T(8,128)(2,1)S(1)}, u32[]{:S(2)}, u32[]{:S(2)}) collective-permute-start(bf16[256,128]{1,0:T(8,128)(2,1)S(1)} %get-tuple-element.46), channel_id=1, source_target_pairs={{0,2},{1,3},{2,0},{3,1},{4,6},{5,7},{6,4},{7,5},{8,10},{9,11},{10,... | collective-permute-start | bytes 196616 | tf_op jit(solution)/shard_map/ppermute | solution.py:22
  5.3 5.3 %collective-permute-start.4 = (bf16[256,128]{1,0:T(8,128)(2,1)S(1)}, bf16[256,128]{1,0:T(8,128)(2,1)S(1)}, u32[]{:S(2)}, u32[]{:S(2)}) collective-permute-start(bf16[256,128]{1,0:T(8,128)(2,1)S(1)} %get-tuple-element.47), channel_id=1, source_target_pairs={{0,3},{1,2},{2,1},{3,0},{4,7},{5,6},{6,5},{7,4},{8,11},{9,10},{10,... | collective-permute-start | bytes 196616 | tf_op jit(solution)/shard_map/ppermute | solution.py:22
  5.3 13.8 %collective-permute-start = (bf16[256,384]{1,0:T(8,128)(2,1)S(1)}, bf16[256,384]{1,0:T(8,128)(2,1)S(1)}, u32[]{:S(2)}, u32[]{:S(2)}) collective-permute-start(bf16[256,384]{1,0:T(8,128)(2,1)S(1)} %get-tuple-element.43), channel_id=1, source_target_pairs={{0,1},{1,0},{2,3},{3,2},{4,5},{5,4},{6,7},{7,6},{8,9},{9,8},{10,11... | collective-permute-start | bytes 589832 | tf_op jit(solution)/shard_map/ppermute | solution.py:22
  5.5 7.2 %collective-permute-start.1 = (bf16[256,256]{1,0:T(8,128)(2,1)S(1)}, bf16[256,256]{1,0:T(8,128)(2,1)S(1)}, u32[]{:S(2)}, u32[]{:S(2)}) collective-permute-start(bf16[256,256]{1,0:T(8,128)(2,1)S(1)} %get-tuple-element.44), channel_id=1, source_target_pairs={{0,2},{1,3},{2,0},{3,1},{4,6},{5,7},{6,4},{7,5},{8,10},{9,11},{10,... | collective-permute-start | bytes 393224 | tf_op jit(solution)/shard_map/ppermute | solution.py:22
  7.4 11.2 %collective-permute-start.2 = (bf16[256,256]{1,0:T(8,128)(2,1)S(1)}, bf16[256,256]{1,0:T(8,128)(2,1)S(1)}, u32[]{:S(2)}, u32[]{:S(2)}) collective-permute-start(bf16[256,256]{1,0:T(8,128)(2,1)S(1)} %get-tuple-element.45), channel_id=1, source_target_pairs={{0,3},{1,2},{2,1},{3,0},{4,7},{5,6},{6,5},{7,4},{8,11},{9,10},{10,... | collective-permute-start | bytes 393224 | tf_op jit(solution)/shard_map/ppermute | solution.py:22
  7.5 7.5 %collective-permute-start.8 = (bf16[32,512]{1,0:T(8,128)(2,1)S(1)}, bf16[32,512]{1,0:T(8,128)(2,1)S(1)}, u32[]{:S(2)}, u32[]{:S(2)}) collective-permute-start(bf16[32,512]{1,0:T(8,128)(2,1)S(1)} %get-tuple-element.59), channel_id=1, source_target_pairs={{0,4},{1,5},{2,6},{3,7},{4,0},{5,1},{6,2},{7,3},{8,12},{9,13},{10,... | collective-permute-start | bytes 98312 | tf_op jit(solution)/shard_map/ppermute | solution.py:22
  10.6 8.0 %collective-permute-start.10 = (bf16[32,512]{1,0:T(8,128)(2,1)S(1)}, bf16[32,512]{1,0:T(8,128)(2,1)S(1)}, u32[]{:S(2)}, u32[]{:S(2)}) collective-permute-start(bf16[32,512]{1,0:T(8,128)(2,1)S(1)} %get-tuple-element.60), channel_id=1, source_target_pairs={{0,6},{1,7},{2,4},{3,5},{4,2},{5,3},{6,0},{7,1},{8,14},{9,15},{10,... | collective-permute-start | bytes 98312 | tf_op jit(solution)/shard_map/ppermute | solution.py:22
  12.7 12.2 %collective-permute-start.12 = (bf16[96,512]{1,0:T(8,128)(2,1)S(1)}, bf16[96,512]{1,0:T(8,128)(2,1)S(1)}, u32[]{:S(2)}, u32[]{:S(2)}) collective-permute-start(bf16[96,512]{1,0:T(8,128)(2,1)S(1)} %get-tuple-element.61), channel_id=1, source_target_pairs={{0,4},{1,5},{2,6},{3,7},{4,0},{5,1},{6,2},{7,3},{8,12},{9,13},{10,... | collective-permute-start | bytes 294920 | tf_op jit(solution)/shard_map/ppermute | solution.py:22
  15.0 9.8 %collective-permute-start.14 = (bf16[96,512]{1,0:T(8,128)(2,1)S(1)}, bf16[96,512]{1,0:T(8,128)(2,1)S(1)}, u32[]{:S(2)}, u32[]{:S(2)}) collective-permute-start(bf16[96,512]{1,0:T(8,128)(2,1)S(1)} %get-tuple-element.62), channel_id=1, source_target_pairs={{0,6},{1,7},{2,4},{3,5},{4,2},{5,3},{6,0},{7,1},{8,14},{9,15},{10,... | collective-permute-start | bytes 294920 | tf_op jit(solution)/shard_map/ppermute | solution.py:22
  18.6 1.2 %collective-permute-start.9 = (bf16[32,512]{1,0:T(8,128)(2,1)S(1)}, bf16[32,512]{1,0:T(8,128)(2,1)S(1)}, u32[]{:S(2)}, u32[]{:S(2)}) collective-permute-start(bf16[32,512]{1,0:T(8,128)(2,1)S(1)} %collective-permute-done.8.refs_6_), channel_id=1, source_target_pairs={{0,1},{1,0},{2,3},{3,2},{4,5},{5,4},{6,7},{7,6},{8,9},{9,8},{10,11... | collective-permute-start | bytes 98312 | tf_op jit(solution)/shard_map/ppermute | solution.py:22
  18.6 1.3 %collective-permute-start.11 = (bf16[32,512]{1,0:T(8,128)(2,1)S(1)}, bf16[32,512]{1,0:T(8,128)(2,1)S(1)}, u32[]{:S(2)}, u32[]{:S(2)}) collective-permute-start(bf16[32,512]{1,0:T(8,128)(2,1)S(1)} %collective-permute-done.10.refs_8_), channel_id=1, source_target_pairs={{0,1},{1,0},{2,3},{3,2},{4,5},{5,4},{6,7},{7,6},{8,9},{9,8},{10,11... | collective-permute-start | bytes 98312 | tf_op jit(solution)/shard_map/ppermute | solution.py:22
  20.0 12.9 %collective-permute-start.16 = (bf16[256,256]{1,0:T(8,128)(2,1)S(1)}, bf16[256,256]{1,0:T(8,128)(2,1)S(1)}, u32[]{:S(2)}, u32[]{:S(2)}) collective-permute-start(bf16[256,256]{1,0:T(8,128)(2,1)S(1)} %constant_dynamic-update-slice_fusion), channel_id=1, source_target_pairs={{0,8},{8,0},{16,24},{24,16},{1,9},{9,1},{17,25},{25,17},{2,10},{10... | collective-permute-start | bytes 393224 | tf_op jit(solution)/shard_map/ppermute | solution.py:22
  21.4 11.5 %collective-permute-start.17 = (bf16[256,256]{1,0:T(8,128)(2,1)S(1)}, bf16[256,256]{1,0:T(8,128)(2,1)S(1)}, u32[]{:S(2)}, u32[]{:S(2)}) collective-permute-start(bf16[256,256]{1,0:T(8,128)(2,1)S(1)} %constant_dynamic-update-slice_fusion), channel_id=1, source_target_pairs={{0,16},{8,24},{16,0},{24,8},{1,17},{9,25},{17,1},{25,9},{2,18},{10... | collective-permute-start | bytes 393224 | tf_op jit(solution)/shard_map/ppermute | solution.py:22
  23.0 10.0 %collective-permute-start.18 = (bf16[256,256]{1,0:T(8,128)(2,1)S(1)}, bf16[256,256]{1,0:T(8,128)(2,1)S(1)}, u32[]{:S(2)}, u32[]{:S(2)}) collective-permute-start(bf16[256,256]{1,0:T(8,128)(2,1)S(1)} %constant_dynamic-update-slice_fusion), channel_id=1, source_target_pairs={{0,24},{8,16},{16,8},{24,0},{1,25},{9,17},{17,9},{25,1},{2,26},{10... | collective-permute-start | bytes 393224 | tf_op jit(solution)/shard_map/ppermute | solution.py:22
  24.9 4.2 %collective-permute-start.13 = (bf16[96,512]{1,0:T(8,128)(2,1)S(1)}, bf16[96,512]{1,0:T(8,128)(2,1)S(1)}, u32[]{:S(2)}, u32[]{:S(2)}) collective-permute-start(bf16[96,512]{1,0:T(8,128)(2,1)S(1)} %collective-permute-done.12.refs_10_), channel_id=1, source_target_pairs={{0,1},{1,0},{2,3},{3,2},{4,5},{5,4},{6,7},{7,6},{8,9},{9,8},{10,11... | collective-permute-start | bytes 294920 | tf_op jit(solution)/shard_map/ppermute | solution.py:22
  24.9 4.3 %collective-permute-start.15 = (bf16[96,512]{1,0:T(8,128)(2,1)S(1)}, bf16[96,512]{1,0:T(8,128)(2,1)S(1)}, u32[]{:S(2)}, u32[]{:S(2)}) collective-permute-start(bf16[96,512]{1,0:T(8,128)(2,1)S(1)} %collective-permute-done.14.refs_12_), channel_id=1, source_target_pairs={{0,1},{1,0},{2,3},{3,2},{4,5},{5,4},{6,7},{7,6},{8,9},{9,8},{10,11... | collective-permute-start | bytes 294920 | tf_op jit(solution)/shard_map/ppermute | solution.py:22
  29.1 7.1 %collective-permute-start.5 = (bf16[128,128]{1,0:T(8,128)(2,1)S(1)}, bf16[128,128]{1,0:T(8,128)(2,1)S(1)}, u32[]{:S(2)}, u32[]{:S(2)}) collective-permute-start(bf16[128,128]{1,0:T(8,128)(2,1)S(1)} %get-tuple-element.50), channel_id=1, source_target_pairs={{0,1},{1,0},{2,3},{3,2},{4,5},{5,4},{6,7},{7,6},{8,9},{9,8},{10,11... | collective-permute-start | bytes 98312 | tf_op jit(solution)/shard_map/ppermute | solution.py:22
  29.1 7.0 %collective-permute-start.6 = (bf16[128,128]{1,0:T(8,128)(2,1)S(1)}, bf16[128,128]{1,0:T(8,128)(2,1)S(1)}, u32[]{:S(2)}, u32[]{:S(2)}) collective-permute-start(bf16[128,128]{1,0:T(8,128)(2,1)S(1)} %get-tuple-element.51), channel_id=1, source_target_pairs={{0,2},{1,3},{2,0},{3,1},{4,6},{5,7},{6,4},{7,5},{8,10},{9,11},{10,... | collective-permute-start | bytes 98312 | tf_op jit(solution)/shard_map/ppermute | solution.py:22
  32.8 7.0 %copy-start = (bf16[512,768]{1,0:T(8,128)(2,1)S(1)}, bf16[512,768]{1,0:T(8,128)(2,1)}, u32[]{:S(2)}) copy-start(bf16[512,768]{1,0:T(8,128)(2,1)} %weight_ref.1) | copy-start | bytes 2359300
  32.8 3.7 %collective-permute-start.7 = (bf16[128,128]{1,0:T(8,128)(2,1)S(1)}, bf16[128,128]{1,0:T(8,128)(2,1)S(1)}, u32[]{:S(2)}, u32[]{:S(2)}) collective-permute-start(bf16[128,128]{1,0:T(8,128)(2,1)S(1)} %get-tuple-element.52), channel_id=1, source_target_pairs={{0,3},{1,2},{2,1},{3,0},{4,7},{5,6},{6,5},{7,4},{8,11},{9,10},{10,... | collective-permute-start | bytes 98312 | tf_op jit(solution)/shard_map/ppermute | solution.py:22
  34.0 2.9 %collective-permute-start.19 = (bf16[128,128]{1,0:T(8,128)(2,1)S(1)}, bf16[128,128]{1,0:T(8,128)(2,1)S(1)}, u32[]{:S(2)}, u32[]{:S(2)}) collective-permute-start(bf16[128,128]{1,0:T(8,128)(2,1)S(1)} %get-tuple-element.74), channel_id=1, source_target_pairs={{0,1},{1,0},{2,3},{3,2},{4,5},{5,4},{6,7},{7,6},{8,9},{9,8},{10,11... | collective-permute-start | bytes 98312 | tf_op jit(solution)/shard_map/ppermute | solution.py:22
  34.1 3.9 %collective-permute-start.20 = (bf16[128,128]{1,0:T(8,128)(2,1)S(1)}, bf16[128,128]{1,0:T(8,128)(2,1)S(1)}, u32[]{:S(2)}, u32[]{:S(2)}) collective-permute-start(bf16[128,128]{1,0:T(8,128)(2,1)S(1)} %get-tuple-element.75), channel_id=1, source_target_pairs={{0,2},{1,3},{2,0},{3,1},{4,6},{5,7},{6,4},{7,5},{8,10},{9,11},{10,... | collective-permute-start | bytes 98312 | tf_op jit(solution)/shard_map/ppermute | solution.py:22
  36.2 3.7 %collective-permute-start.21 = (bf16[128,128]{1,0:T(8,128)(2,1)S(1)}, bf16[128,128]{1,0:T(8,128)(2,1)S(1)}, u32[]{:S(2)}, u32[]{:S(2)}) collective-permute-start(bf16[128,128]{1,0:T(8,128)(2,1)S(1)} %get-tuple-element.76), channel_id=1, source_target_pairs={{0,3},{1,2},{2,1},{3,0},{4,7},{5,6},{6,5},{7,4},{8,11},{9,10},{10,... | collective-permute-start | bytes 98312 | tf_op jit(solution)/shard_map/ppermute | solution.py:22

commit v5 on v4

--- a/solution.py
+++ b/solution.py
@@ -62,7 +62,7 @@
 
 def pack_kernel(plan, lengths_ref, q_ref, k_ref, v_ref, *refs):
     rows, mid_rows, tile = plan.rows, plan.mid_rows, plan.top_tile
-    own, near, *outs, table, taken, lengths, sems, length_sem = refs
+    own, near, *outs, table, taken, one_hot, lengths, sems, length_sem = refs
     leads, seconds, heads, tails = [outs[n : n + 2] for n in range(0, 8, 2)]
     copies = []
     for x in (2, 3, 0, 1):
@@ -78,13 +78,14 @@
     wrapped = (plan.source_row(k) - i) & (rows - 1)
     first = lax.broadcasted_iota(jnp.int32, (rows, LANES), 1) < HEAD_DIM
     for s, x in enumerate((2, 3, 0, 1)):
-        pair = plan.pair() ^ x
-        one_hot = [pick(wrapped, 2 * pair + t, rows) for t in range(2)]
+        for t in range(2):
+            one_hot[s, t] = pick(wrapped, 2 * (plan.pair() ^ x) + t, rows)
+    for s, x in enumerate((2, 3, 0, 1)):
         if s % 2 == 0:
             for copy in copies[3 * s : 3 * s + 6]:
                 copy.wait()
         block = jnp.concatenate([taken[x, part] for part in range(3)], axis=1)
-        one, two = [dot(m, block, ((1,), (0,))) for m in one_hot]
+        one, two = [dot(one_hot[s, t], block, ((1,), (0,))) for t in range(2)]
         query = jnp.where(first, one[:, :LANES], two[:, :LANES]) * HEAD_DIM**-0.5
         kv_one = jnp.where(
             first, one[:, LANES : 2 * LANES], pltpu.roll(one[:, 2 * LANES :], HEAD_DIM, axis=1)
@@ -92,13 +93,18 @@
         kv_two = jnp.where(
             first, pltpu.roll(two[:, 2 * LANES :], HEAD_DIM, axis=1), two[:, LANES : 2 * LANES]
         ).astype(BF16)
-        lead = leads[x - 2] if x >= 2 else (own, near)[x]
-        lead[:, :LANES] = query.astype(BF16)
-        lead[:, LANES : 2 * LANES] = kv_one
         if x >= 2:
-            seconds[x - 2][...] = kv_two
+            low, high = query[: rows // 2], pltpu.roll(query[rows // 2 :], HEAD_DIM, axis=1)
+            leads[x - 2][:rows, :] = kv_one
+            leads[x - 2][rows + tile :, :] = jnp.where(first[: rows // 2], low, high).astype(BF16)
+            leads[x - 2][rows : rows + tile, :] = kv_two[:tile]
+            seconds[x - 2][:rows, :] = kv_two
+            seconds[x - 2][rows:, :] = jnp.where(first[: rows // 2], high, low).astype(BF16)
         else:
-            lead[:, 2 * LANES :] = kv_two
+            out = (own, near)[x]
+            out[:, :LANES] = query.astype(BF16)
+            out[:, LANES : 2 * LANES] = kv_one
+            out[:, 2 * LANES :] = kv_two
         at = (x & 1) * 2 * LANES
         for out, low, high in ((heads[x >> 1], 0, tile), (tails[x >> 1], tile, mid_rows)):
             out[:, at : at + LANES] = kv_one[low:high]
@@ -139,22 +145,22 @@
     return pltpu.roll(sums, HEAD_DIM, axis=1) / sums
 
 
-def chunks(own, near, leads, seconds):
-    part = lambda ref, n: ref.at[:, n * LANES : (n + 1) * LANES]
-    queries = [part(ref, 0) for ref in (own, near, *leads)]
-    firsts = [part(ref, 1) for ref in (own, near, *leads)]
-    return queries, firsts, [part(own, 2), part(near, 2), *seconds]
-
-
-def local_kernel(plan, t, table_ref, own, near, *refs):
+def chunk(refs, x, t, rows):
+    ref = refs[x]
+    if x < 2:
+        return ref[:, :LANES].astype(F32), ref[:, (1 + t) * LANES : (2 + t) * LANES]
+    low = ref[ref.shape[0] - rows // 2 :, :].astype(F32)
+    return jnp.concatenate([low, pltpu.roll(low, HEAD_DIM, axis=1)], axis=0), ref[:rows, :]
+
+
+def local_kernel(plan, t, table_ref, *refs):
     rows, group, mid_rows, tile = plan.rows, plan.group, plan.mid_rows, plan.top_tile
-    leads, seconds, refs = refs[:2], refs[2 : 2 + 2 * t], refs[2 + 2 * t :]
+    slots, refs = refs[:group], refs[group:]
     if t:
         before, rests, refs = refs[0], refs[1 : 1 + group], refs[1 + group :]
     else:
         rest, refs = refs[0], refs[1:]
     sums_ref, maxima_ref, q_mid, q_s, k_s, v_s, vt_s, s_s = refs
-    queries, firsts, seconds = chunks(own, near, leads, seconds)
     positions = block_positions(plan, t, rows)
     lane = lax.broadcasted_iota(jnp.int32, (rows, LANES), 1)
     keys = (lane < HEAD_DIM) if t == 0 else (lane >= HEAD_DIM)
@@ -163,10 +169,13 @@
         here = pl.ds(x * rows, rows)
         mid_here = pl.ds(x * mid_rows, mid_rows)
         inside = block_inside(plan, table_ref, t, positions, x)
-        kv = (seconds if t else firsts)[x][...].astype(F32)
-        query = as_query(queries[x][...], inside, keys)
-        q_s[here, :] = query
+        query, kv = chunk(slots, x, t, rows)
+        kv = kv.astype(F32)
+        query = as_query(query, inside, keys)
+        q_s[mid_here, :] = query[:mid_rows]
         q_mid[mid_here, :] = query[:mid_rows]
+        others = rows - mid_rows
+        q_s[pl.ds(group * mid_rows + x * others, others), :] = query[mid_rows:]
         k_s[here, :] = as_key(kv, inside, keys)
         value = as_value(kv, keys)
         low = value.astype(BF16)
@@ -174,32 +183,47 @@
         v_s[pl.ds(x * rows, mid_rows), LANES:] = (2.0 * value[:mid_rows]).astype(BF16)
         v_s[pl.ds(x * rows + mid_rows, rows - mid_rows), LANES:] = low[mid_rows:]
         vt_s[mid_here, :] = jnp.where(is_top, value[:mid_rows], 0.0).astype(BF16)
-    lane = lax.broadcasted_iota(jnp.int32, (rows - mid_rows, LANES), 1)
-    for x in range(group):
-        here = pl.ds(x * rows, rows)
-        mid_here = pl.ds(x * mid_rows, mid_rows)
-        rest_here = pl.ds(x * (rows - mid_rows), rows - mid_rows)
-        if x == 0:
-            s_s[0] = dot(q_s[here, :], k_s[...], ((1,), (1,)))
-        if x + 1 < group:
-            there = pl.ds((x + 1) * rows, rows)
-            s_s[(x + 1) % 2] = dot(q_s[there, :], k_s[...], ((1,), (1,)))
-        scores = s_s[x % 2]
+    blocks = [(0, y) for y in range(0, group, 2)] + [(1, y) for y in range(0, group, 2)]
+    sizes, first_row = (mid_rows, others), (0, group * mid_rows)
+
+    def score(block):
+        kind, y = block
+        taken = q_s[pl.ds(first_row[kind] + y * sizes[kind], 2 * sizes[kind]), :]
+        return dot(taken, k_s[...], ((1,), (1,)))
+
+    def held(n):
+        return s_s.at[n % 2, pl.ds(0, 2 * sizes[blocks[n][0]]), :]
+
+    held(0)[...] = score(blocks[0])
+    for n, (kind, y) in enumerate(blocks):
+        if n + 1 < len(blocks):
+            held(n + 1)[...] = score(blocks[n + 1])
+        scores = held(n)[...]
         largest = jnp.max(scores, axis=1, keepdims=True)
         probs = jnp.exp(scores - largest).astype(BF16)
-        mid_sum = dot(probs[:mid_rows], v_s[:, LANES:], ((1,), (0,)))
-        top_probs = [probs[:tile, y * rows : y * rows + mid_rows] for y in range(group)]
-        top_sum = dot(jnp.concatenate(top_probs, axis=1), vt_s[...], ((1,), (0,)))
-        rest_sum = share(dot(probs[mid_rows:], v_s[:, :LANES], ((1,), (0,))))
-        top_sum = jnp.where(row_iota(tile) < plan.top_rows, top_sum, 0.0)
-        sums_ref[mid_here, :] = mid_sum
-        sums_ref[pl.ds(x * mid_rows, tile), :] += top_sum
-        maxima_ref[mid_here, :] = jnp.broadcast_to(largest[:mid_rows], (mid_rows, LANES))
-        if t:
-            both = jnp.where(lane < HEAD_DIM, before[rest_here, :], rest_sum)
-            rests[x][...] = both.astype(BF16)
+        there = pl.ds(y * sizes[kind], 2 * sizes[kind])
+        if kind == 0:
+            leads_of = [probs[z * mid_rows : z * mid_rows + tile] for z in range(2)]
+            top_probs = jnp.concatenate(leads_of, axis=0)
+            top_probs = jnp.concatenate(
+                [top_probs[:, z * rows : z * rows + mid_rows] for z in range(group)], axis=1
+            )
+            sums_ref[there, :] = dot(probs, v_s[:, LANES:], ((1,), (0,)))
+            top_sum = dot(top_probs, vt_s[...], ((1,), (0,)))
+            for z in range(2):
+                sums_ref[pl.ds((y + z) * mid_rows, tile), :] += jnp.where(
+                    row_iota(tile) < plan.top_rows, top_sum[z * tile : (z + 1) * tile], 0.0
+                )
+            maxima_ref[there, :] = jnp.broadcast_to(largest, (2 * mid_rows, LANES))
         else:
-            rest[rest_here, :] = rest_sum
+            rest_sum = share(dot(probs, v_s[:, :LANES], ((1,), (0,))))
+            if t:
+                lane = lax.broadcasted_iota(jnp.int32, (2 * others, LANES), 1)
+                both = jnp.where(lane < HEAD_DIM, before[there, :], rest_sum).astype(BF16)
+                for z in range(2):
+                    rests[y + z][...] = both[z * others : (z + 1) * others]
+            else:
+                rest[there, :] = rest_sum
 
 
 def other_chunks(arrays):
@@ -376,13 +400,14 @@
             for a in (slide_lengths, queries, keys, values)
         ],
         [shape(rows, 3 * LANES)] * 2
-        + [shape(rows, 2 * LANES)] * 2
-        + [shape(rows, LANES)] * 2
+        + [shape(rows + tile + rows // 2, LANES)] * 2
+        + [shape(rows + rows // 2, LANES)] * 2
         + [shape(tile, 4 * LANES)] * 2
         + [shape(mid_rows - tile, 4 * LANES)] * 2
         + [shape(8, LANES, jnp.int32)],
         [
             pltpu.VMEM((group, 3, rows, LANES), BF16),
+            pltpu.VMEM((group, 2, rows, rows), BF16),
             pltpu.SMEM(slide_lengths.shape, jnp.int32),
             pltpu.SemaphoreType.DMA((group, 3)),
             pltpu.SemaphoreType.DMA,
@@ -400,8 +425,10 @@
             slots += [other, exchange(other, "inner", 1)]
 
     top = plan.top_rows
-    firsts = [a[:top, LANES : 2 * LANES] for a in (own, near, *leads)]
-    lasts = [a[:top, 2 * LANES :] for a in (own, near)] + [a[:top] for a in seconds]
+    firsts = [a[:top, LANES : 2 * LANES] for a in (own, near)] + [a[:top] for a in leads]
+    lasts = [a[:top, 2 * LANES :] for a in (own, near)] + [
+        a[rows : rows + top] for a in leads
+    ]
     kv = [jnp.concatenate(slot, axis=1) for slot in zip(firsts, lasts)]
     top_own = jnp.concatenate(kv + [slot[:top] for slot in other_chunks(other_heads)], axis=0)
     tops = [exchange(top_own, "outer", x) for x in range(1, plan.outer)]
@@ -410,7 +437,7 @@
     scratch = [pltpu.VMEM((count, LANES), BF16)] * 2
     scratch += [pltpu.VMEM((count, 2 * LANES), BF16)]
     scratch += [pltpu.VMEM((group * mid_rows, LANES), BF16)]
-    scratch += [pltpu.VMEM((2, rows, count), F32)]
+    scratch += [pltpu.VMEM((2, 2 * max(mid_rows, rows - mid_rows), count), F32)]
     state = [shape(group * mid_rows, LANES, F32)] * 2 + [shape(group * mid_rows, LANES)]
     rest_one, *state_one = call(
         functools.partial(local_kernel, plan, 0),
@@ -420,7 +447,7 @@
     )
     local_two = call(
         functools.partial(local_kernel, plan, 1),
-        (table, own, near, *leads, *seconds, rest_one),
+        (table, own, near, *seconds, rest_one),
         [shape(rows - mid_rows, LANES)] * group + state,
         scratch,
     )

time: 41.4 us -> 40.7 us (0.983)
  waiting for transfers between devices: 7.35 us -> 6.67 us
    ppermute x22, waiting for transfers between devices: 7.35 us -> 6.67 us  [exchange(): return lax.ppermute(block, axis, [(i, i ^ distance) for i in range(count)])]
  transfers between devices with their start and end apart: 22 -> 22, of which waited for: 9 -> 7; matrix products, arithmetic and copies ran while one was open for 0% -> 0% of each run, Pallas kernels for 15% -> 16%
where the time goes in v5:
time: 40.7 us; the launch traced here: 40.5 us
  starting transfers between devices  23.8 us (58%)
  Pallas kernels  9.93 us (24%)
  waiting for transfers between devices  6.67 us (16%)
    ppermute x22, starting transfers between devices, exchange(): return lax.ppermute(block, axis, [(i, i ^ distance) for i in range(count)])  23.8 us
    pallas_call x7, Pallas kernels, call(): pl.pallas_call(kernel, in_specs=in_specs or [vmem] * len(operands), out_s...  9.93 us
    ppermute x22, waiting for transfers between devices, exchange(): return lax.ppermute(block, axis, [(i, i ^ distance) for i in range(count)])  6.67 us
  transfers between devices with their start and end apart: 22, of which 7 were waited for; matrix products, arithmetic and copies ran while one was open for 0% of the time, Pallas kernels for 16%

profile of v5, /device:TPU:0, one launch (start us, length us, event | category | flops | bytes accessed | tf_op | source)
XLA Modules:
  0.0 40.5 jit_solution(119087679686839108)
XLA Ops:
  0.0 2.2 %shard_map.55 = (bf16[256,384]{1,0:T(8,128)(2,1)S(1)}, bf16[256,384]{1,0:T(8,128)(2,1)S(1)}, bf16[416,128]{1,0:T(8,128)(2,1)S(1)}, bf16[416,128]{1,0:T(8,128)(2,...) custom-call(s32[16]{0:T(128)} %lengths_ref.1, ...), custom_call_target="tpu_custom_call" | custom-call | tf_op jit(solution)/shard_map/pallas_call | solution.py:382
  2.2 0.6 %collective-permute-start = (bf16[256,384]{1,0:T(8,128)(2,1)S(1)}, bf16[256,384]{1,0:T(8,128)(2,1)S(1)}, u32[]{:S(2)}, u32[]{:S(2)}) collective-permute-start(bf16[256,384]{1,0:T(8,128)(2,1)S(1)} %get-tuple-element.43), channel_id=1, source_target_pairs={{0,1},{1,0},{2,3},{3,2},{4,5},{5,4},{6,7},{7,6},{8,9},{9,8},{10,11... | collective-permute-start | bytes 589832 | tf_op jit(solution)/shard_map/ppermute | solution.py:22
  2.8 2.6 %collective-permute-start.3 = (bf16[416,128]{1,0:T(8,128)(2,1)S(1)}, bf16[416,128]{1,0:T(8,128)(2,1)S(1)}, u32[]{:S(2)}, u32[]{:S(2)}) collective-permute-start(bf16[416,128]{1,0:T(8,128)(2,1)S(1)} %get-tuple-element.46), channel_id=1, source_target_pairs={{0,2},{1,3},{2,0},{3,1},{4,6},{5,7},{6,4},{7,5},{8,10},{9,11},{10,... | collective-permute-start | bytes 319496 | tf_op jit(solution)/shard_map/ppermute | solution.py:22
  5.4 0.0 collective-permute-start.4
  5.4 2.8 %collective-permute-start.8 = (bf16[32,512]{1,0:T(8,128)(2,1)S(1)}, bf16[32,512]{1,0:T(8,128)(2,1)S(1)}, u32[]{:S(2)}, u32[]{:S(2)}) collective-permute-start(bf16[32,512]{1,0:T(8,128)(2,1)S(1)} %get-tuple-element.59), channel_id=1, source_target_pairs={{0,4},{1,5},{2,6},{3,7},{4,0},{5,1},{6,2},{7,3},{8,12},{9,13},{10,... | collective-permute-start | bytes 98312 | tf_op jit(solution)/shard_map/ppermute | solution.py:22
  8.2 1.3 %collective-permute-start.10 = (bf16[32,512]{1,0:T(8,128)(2,1)S(1)}, bf16[32,512]{1,0:T(8,128)(2,1)S(1)}, u32[]{:S(2)}, u32[]{:S(2)}) collective-permute-start(bf16[32,512]{1,0:T(8,128)(2,1)S(1)} %get-tuple-element.60), channel_id=1, source_target_pairs={{0,6},{1,7},{2,4},{3,5},{4,2},{5,3},{6,0},{7,1},{8,14},{9,15},{10,... | collective-permute-start | bytes 98312 | tf_op jit(solution)/shard_map/ppermute | solution.py:22
  9.5 0.0 collective-permute-done.3.refs_2_
  9.5 1.7 %collective-permute-start.1 = (bf16[384,128]{1,0:T(8,128)(2,1)S(1)}, bf16[384,128]{1,0:T(8,128)(2,1)S(1)}, u32[]{:S(2)}, u32[]{:S(2)}) collective-permute-start(bf16[384,128]{1,0:T(8,128)(2,1)S(1)} %get-tuple-element.44), channel_id=1, source_target_pairs={{0,2},{1,3},{2,0},{3,1},{4,6},{5,7},{6,4},{7,5},{8,10},{9,11},{10,... | collective-permute-start | bytes 294920 | tf_op jit(solution)/shard_map/ppermute | solution.py:22
  11.2 0.4 %collective-permute-done.4.refs_3_ = bf16[416,128]{1,0:T(8,128)(2,1)S(1)} collective-permute-done((bf16[416,128]{1,0:T(8,128)(2,1)S(1)}, bf16[416,128]{1,0:T(8,128)(2,1)S(1)}, u32[]{:S(2)}, u32[]{:S(2)}) %collective-permute-start.4) | collective-permute-done | bytes 106528 | tf_op jit(solution)/shard_map/ppermute | solution.py:22
  11.7 1.6 %collective-permute-start.2 = (bf16[384,128]{1,0:T(8,128)(2,1)S(1)}, bf16[384,128]{1,0:T(8,128)(2,1)S(1)}, u32[]{:S(2)}, u32[]{:S(2)}) collective-permute-start(bf16[384,128]{1,0:T(8,128)(2,1)S(1)} %get-tuple-element.45), channel_id=1, source_target_pairs={{0,3},{1,2},{2,1},{3,0},{4,7},{5,6},{6,5},{7,4},{8,11},{9,10},{10,... | collective-permute-start | bytes 294920 | tf_op jit(solution)/shard_map/ppermute | solution.py:22
  13.2 0.0 collective-permute-done.8.refs_6_
  13.2 3.8 %collective-permute-start.12 = (bf16[96,512]{1,0:T(8,128)(2,1)S(1)}, bf16[96,512]{1,0:T(8,128)(2,1)S(1)}, u32[]{:S(2)}, u32[]{:S(2)}) collective-permute-start(bf16[96,512]{1,0:T(8,128)(2,1)S(1)} %get-tuple-element.61), channel_id=1, source_target_pairs={{0,4},{1,5},{2,6},{3,7},{4,0},{5,1},{6,2},{7,3},{8,12},{9,13},{10,... | collective-permute-start | bytes 294920 | tf_op jit(solution)/shard_map/ppermute | solution.py:22
  17.0 0.0 collective-permute-done.refs_1_
  17.0 0.0 collective-permute-start.9
  17.1 0.0 collective-permute-done.10.refs_8_
  17.1 0.6 %collective-permute-start.14 = (bf16[96,512]{1,0:T(8,128)(2,1)S(1)}, bf16[96,512]{1,0:T(8,128)(2,1)S(1)}, u32[]{:S(2)}, u32[]{:S(2)}) collective-permute-start(bf16[96,512]{1,0:T(8,128)(2,1)S(1)} %get-tuple-element.62), channel_id=1, source_target_pairs={{0,6},{1,7},{2,4},{3,5},{4,2},{5,3},{6,0},{7,1},{8,14},{9,15},{10,... | collective-permute-start | bytes 294920 | tf_op jit(solution)/shard_map/ppermute | solution.py:22
  17.7 0.5 %collective-permute-done.9.refs_7_ = bf16[32,512]{1,0:T(8,128)(2,1)S(1)} collective-permute-done((bf16[32,512]{1,0:T(8,128)(2,1)S(1)}, bf16[32,512]{1,0:T(8,128)(2,1)S(1)}, u32[]{:S(2)}, u32[]{:S(2)}) %collective-permute-start.9) | collective-permute-done | bytes 32800 | tf_op jit(solution)/shard_map/ppermute | solution.py:22
  18.2 0.2 collective-permute-start.11
  18.4 1.0 %collective-permute-done.11.refs_9_ = bf16[32,512]{1,0:T(8,128)(2,1)S(1)} collective-permute-done((bf16[32,512]{1,0:T(8,128)(2,1)S(1)}, bf16[32,512]{1,0:T(8,128)(2,1)S(1)}, u32[]{:S(2)}, u32[]{:S(2)}) %collective-permute-start.11) | collective-permute-done | bytes 32800 | tf_op jit(solution)/shard_map/ppermute | solution.py:22
  19.4 1.5 %collective-permute-start.16 = (bf16[256,256]{1,0:T(8,128)(2,1)S(1)}, bf16[256,256]{1,0:T(8,128)(2,1)S(1)}, u32[]{:S(2)}, u32[]{:S(2)}) collective-permute-start(bf16[256,256]{1,0:T(8,128)(2,1)S(1)} %constant_dynamic-update-slice_fusion), channel_id=1, source_target_pairs={{0,8},{8,0},{16,24},{24,16},{1,9},{9,1},{17,25},{25,17},{2,10},{10... | collective-permute-start | bytes 393224 | tf_op jit(solution)/shard_map/ppermute | solution.py:22
  20.9 0.0 collective-permute-done.1.refs_2_
  20.9 1.5 %collective-permute-start.17 = (bf16[256,256]{1,0:T(8,128)(2,1)S(1)}, bf16[256,256]{1,0:T(8,128)(2,1)S(1)}, u32[]{:S(2)}, u32[]{:S(2)}) collective-permute-start(bf16[256,256]{1,0:T(8,128)(2,1)S(1)} %constant_dynamic-update-slice_fusion), channel_id=1, source_target_pairs={{0,16},{8,24},{16,0},{24,8},{1,17},{9,25},{17,1},{25,9},{2,18},{10... | collective-permute-start | bytes 393224 | tf_op jit(solution)/shard_map/ppermute | solution.py:22
  22.4 0.0 collective-permute-done.2.refs_3_
  22.5 0.5 %collective-permute-start.18 = (bf16[256,256]{1,0:T(8,128)(2,1)S(1)}, bf16[256,256]{1,0:T(8,128)(2,1)S(1)}, u32[]{:S(2)}, u32[]{:S(2)}) collective-permute-start(bf16[256,256]{1,0:T(8,128)(2,1)S(1)} %constant_dynamic-update-slice_fusion), channel_id=1, source_target_pairs={{0,24},{8,16},{16,8},{24,0},{1,25},{9,17},{17,9},{25,1},{2,26},{10... | collective-permute-start | bytes 393224 | tf_op jit(solution)/shard_map/ppermute | solution.py:22
  22.9 0.0 collective-permute-done.12.refs_10_
  22.9 0.0 collective-permute-start.13
  22.9 1.3 %collective-permute-done.14.refs_12_ = bf16[96,512]{1,0:T(8,128)(2,1)S(1)} collective-permute-done((bf16[96,512]{1,0:T(8,128)(2,1)S(1)}, bf16[96,512]{1,0:T(8,128)(2,1)S(1)}, u32[]{:S(2)}, u32[]{:S(2)}) %collective-permute-start.14) | collective-permute-done | bytes 98336 | tf_op jit(solution)/shard_map/ppermute | solution.py:22
  24.2 0.0 collective-permute-start.15
  24.2 1.8 %shard_map.56 = (f32[512,128]{1,0:T(8,128)S(1)}, f32[512,128]{1,0:T(8,128)S(1)}, f32[512,128]{1,0:T(8,128)S(1)}, bf16[512,128]{1,0:T(8,128)(2,1)S(1)}) custom-call(s32[8,128]{1,0:T(8,128)S(1)} %get-tuple-element.41.table_ref, bf16[256,384]{1,0:T(8,128)(2,1)S(1)} %get-tuple-element.42.refs_0_, bf16[256,384]{1,0:T(8,128)(2,1)S(1)} %collective-permute-done.refs_1_, ...), custom_call_target="tpu_custom_call" | custom-call | tf_op jit(solution)/shard_map/pallas_call | solution.py:382
  26.1 1.9 %shard_map.57 = (bf16[128,128]{1,0:T(8,128)(2,1)S(1)}, bf16[128,128]{1,0:T(8,128)(2,1)S(1)}, bf16[128,128]{1,0:T(8,128)(2,1)S(1)}, bf16[128,128]{1,0:T(8,128)(2,...) custom-call(s32[8,128]{1,0:T(8,128)S(1)} %get-tuple-element.41.table_ref, ...), custom_call_target="tpu_custom_call" | custom-call | tf_op jit(solution)/shard_map/pallas_call | solution.py:382
  27.9 0.6 %collective-permute-start.5 = (bf16[128,128]{1,0:T(8,128)(2,1)S(1)}, bf16[128,128]{1,0:T(8,128)(2,1)S(1)}, u32[]{:S(2)}, u32[]{:S(2)}) collective-permute-start(bf16[128,128]{1,0:T(8,128)(2,1)S(1)} %get-tuple-element.50), channel_id=1, source_target_pairs={{0,1},{1,0},{2,3},{3,2},{4,5},{5,4},{6,7},{7,6},{8,9},{9,8},{10,11... | collective-permute-start | bytes 98312 | tf_op jit(solution)/shard_map/ppermute | solution.py:22
  28.5 2.3 %collective-permute-start.6 = (bf16[128,128]{1,0:T(8,128)(2,1)S(1)}, bf16[128,128]{1,0:T(8,128)(2,1)S(1)}, u32[]{:S(2)}, u32[]{:S(2)}) collective-permute-start(bf16[128,128]{1,0:T(8,128)(2,1)S(1)} %get-tuple-element.51), channel_id=1, source_target_pairs={{0,2},{1,3},{2,0},{3,1},{4,6},{5,7},{6,4},{7,5},{8,10},{9,11},{10,... | collective-permute-start | bytes 98312 | tf_op jit(solution)/shard_map/ppermute | solution.py:22
  30.8 1.4 %shard_map.59 = (bf16[96,128]{1,0:T(8,128)(2,1)S(1)}, bf16[96,128]{1,0:T(8,128)(2,1)S(1)}, bf16[96,128]{1,0:T(8,128)(2,1)S(1)}, bf16[96,128]{1,0:T(8,128)(2,1)S(...) custom-call(s32[8,128]{1,0:T(8,128)S(1)} %get-tuple-element.41.table, ...), custom_call_target="tpu_custom_call" | custom-call | tf_op jit(solution)/shard_map/pallas_call | solution.py:382
  32.1 0.0 collective-permute-done.16.refs_10_
  32.2 0.1 collective-permute-start.7
  32.2 0.0 collective-permute-done.18.refs_12_
  32.3 1.0 %shard_map.60 = (bf16[128,128]{1,0:T(8,128)(2,1)S(1)}, bf16[128,128]{1,0:T(8,128)(2,1)S(1)}, bf16[128,128]{1,0:T(8,128)(2,1)S(1)}, bf16[128,128]{1,0:T(8,128)(2,1)S(1)}) custom-call(s32[8,128]{1,0:T(8,128)S(1)} %get-tuple-element.41.table_ref, f32[128,128]{1,0:T(8,128)S(1)} %get-tuple-element.63.refs_0_, f32[128,128]{1,0:T(8,128)S(1)} %get-tuple-element.64.refs_1_, ...), custom_call_target="tpu_custom_call" | custom-call | tf_op jit(solution)/shard_map/pallas_call | solution.py:382
  33.3 0.2 collective-permute-start.19
  33.5 2.0 %collective-permute-start.20 = (bf16[128,128]{1,0:T(8,128)(2,1)S(1)}, bf16[128,128]{1,0:T(8,128)(2,1)S(1)}, u32[]{:S(2)}, u32[]{:S(2)}) collective-permute-start(bf16[128,128]{1,0:T(8,128)(2,1)S(1)} %get-tuple-element.75), channel_id=1, source_target_pairs={{0,2},{1,3},{2,0},{3,1},{4,6},{5,7},{6,4},{7,5},{8,10},{9,11},{10,... | collective-permute-start | bytes 98312 | tf_op jit(solution)/shard_map/ppermute | solution.py:22
  35.5 0.0 collective-permute-done.5.refs_1_
  35.5 0.0 collective-permute-start.21
  35.5 0.0 collective-permute-done.6.refs_2_
  35.5 0.4 %collective-permute-done.7.refs_3_ = bf16[128,128]{1,0:T(8,128)(2,1)S(1)} collective-permute-done((bf16[128,128]{1,0:T(8,128)(2,1)S(1)}, bf16[128,128]{1,0:T(8,128)(2,1)S(1)}, u32[]{:S(2)}, u32[]{:S(2)}) %collective-permute-start.7) | collective-permute-done | bytes 32800 | tf_op jit(solution)/shard_map/ppermute | solution.py:22
  35.9 0.3 shard_map.58.rest_ref
  36.2 0.0 collective-permute-done.19.refs_1_
  36.2 1.2 %collective-permute-done.20.refs_2_ = bf16[128,128]{1,0:T(8,128)(2,1)S(1)} collective-permute-done((bf16[128,128]{1,0:T(8,128)(2,1)S(1)}, bf16[128,128]{1,0:T(8,128)(2,1)S(1)}, u32[]{:S(2)}, u32[]{:S(2)}) %collective-permute-start.20) | collective-permute-done | bytes 32800 | tf_op jit(solution)/shard_map/ppermute | solution.py:22
  37.4 1.8 %collective-permute-done.21.refs_3_ = bf16[128,128]{1,0:T(8,128)(2,1)S(1)} collective-permute-done((bf16[128,128]{1,0:T(8,128)(2,1)S(1)}, bf16[128,128]{1,0:T(8,128)(2,1)S(1)}, u32[]{:S(2)}, u32[]{:S(2)}) %collective-permute-start.21) | collective-permute-done | bytes 32800 | tf_op jit(solution)/shard_map/ppermute | solution.py:22
  39.2 1.4 %shard_map.61 = bf16[256,768]{1,0:T(8,128)(2,1)} custom-call(bf16[512,768]{1,0:T(8,128)(2,1)S(1)} %copy-done, bf16[256,512]{1,0:T(8,128)(2,1)S(1)} %shard_map.58.rest_ref, bf16[128,128]{1,0:T(8,128)(2,1)S(1)} %get-tuple-element.73.refs_0_, bf16[128,128]{1,0:T(8,128)(2,1)S(1)} %collective-permute-done.19.refs_1_, ...), custom_call_target="tpu_custom_call" | custom-call | tf_op jit(solution)/shard_map/pallas_call | solution.py:382
  (15 shorter events, 0.0 us)
Async XLA Ops:
  2.2 14.8 %collective-permute-start = (bf16[256,384]{1,0:T(8,128)(2,1)S(1)}, bf16[256,384]{1,0:T(8,128)(2,1)S(1)}, u32[]{:S(2)}, u32[]{:S(2)}) collective-permute-start(bf16[256,384]{1,0:T(8,128)(2,1)S(1)} %get-tuple-element.43), channel_id=1, source_target_pairs={{0,1},{1,0},{2,3},{3,2},{4,5},{5,4},{6,7},{7,6},{8,9},{9,8},{10,11... | collective-permute-start | bytes 589832 | tf_op jit(solution)/shard_map/ppermute | solution.py:22
  2.8 6.8 %collective-permute-start.3 = (bf16[416,128]{1,0:T(8,128)(2,1)S(1)}, bf16[416,128]{1,0:T(8,128)(2,1)S(1)}, u32[]{:S(2)}, u32[]{:S(2)}) collective-permute-start(bf16[416,128]{1,0:T(8,128)(2,1)S(1)} %get-tuple-element.46), channel_id=1, source_target_pairs={{0,2},{1,3},{2,0},{3,1},{4,6},{5,7},{6,4},{7,5},{8,10},{9,11},{10,... | collective-permute-start | bytes 319496 | tf_op jit(solution)/shard_map/ppermute | solution.py:22
  5.4 6.3 %collective-permute-start.4 = (bf16[416,128]{1,0:T(8,128)(2,1)S(1)}, bf16[416,128]{1,0:T(8,128)(2,1)S(1)}, u32[]{:S(2)}, u32[]{:S(2)}) collective-permute-start(bf16[416,128]{1,0:T(8,128)(2,1)S(1)} %get-tuple-element.47), channel_id=1, source_target_pairs={{0,3},{1,2},{2,1},{3,0},{4,7},{5,6},{6,5},{7,4},{8,11},{9,10},{10,... | collective-permute-start | bytes 319496 | tf_op jit(solution)/shard_map/ppermute | solution.py:22
  5.4 7.8 %collective-permute-start.8 = (bf16[32,512]{1,0:T(8,128)(2,1)S(1)}, bf16[32,512]{1,0:T(8,128)(2,1)S(1)}, u32[]{:S(2)}, u32[]{:S(2)}) collective-permute-start(bf16[32,512]{1,0:T(8,128)(2,1)S(1)} %get-tuple-element.59), channel_id=1, source_target_pairs={{0,4},{1,5},{2,6},{3,7},{4,0},{5,1},{6,2},{7,3},{8,12},{9,13},{10,... | collective-permute-start | bytes 98312 | tf_op jit(solution)/shard_map/ppermute | solution.py:22
  8.2 8.9 %collective-permute-start.10 = (bf16[32,512]{1,0:T(8,128)(2,1)S(1)}, bf16[32,512]{1,0:T(8,128)(2,1)S(1)}, u32[]{:S(2)}, u32[]{:S(2)}) collective-permute-start(bf16[32,512]{1,0:T(8,128)(2,1)S(1)} %get-tuple-element.60), channel_id=1, source_target_pairs={{0,6},{1,7},{2,4},{3,5},{4,2},{5,3},{6,0},{7,1},{8,14},{9,15},{10,... | collective-permute-start | bytes 98312 | tf_op jit(solution)/shard_map/ppermute | solution.py:22
  9.5 11.4 %collective-permute-start.1 = (bf16[384,128]{1,0:T(8,128)(2,1)S(1)}, bf16[384,128]{1,0:T(8,128)(2,1)S(1)}, u32[]{:S(2)}, u32[]{:S(2)}) collective-permute-start(bf16[384,128]{1,0:T(8,128)(2,1)S(1)} %get-tuple-element.44), channel_id=1, source_target_pairs={{0,2},{1,3},{2,0},{3,1},{4,6},{5,7},{6,4},{7,5},{8,10},{9,11},{10,... | collective-permute-start | bytes 294920 | tf_op jit(solution)/shard_map/ppermute | solution.py:22
  11.7 10.8 %collective-permute-start.2 = (bf16[384,128]{1,0:T(8,128)(2,1)S(1)}, bf16[384,128]{1,0:T(8,128)(2,1)S(1)}, u32[]{:S(2)}, u32[]{:S(2)}) collective-permute-start(bf16[384,128]{1,0:T(8,128)(2,1)S(1)} %get-tuple-element.45), channel_id=1, source_target_pairs={{0,3},{1,2},{2,1},{3,0},{4,7},{5,6},{6,5},{7,4},{8,11},{9,10},{10,... | collective-permute-start | bytes 294920 | tf_op jit(solution)/shard_map/ppermute | solution.py:22
  13.2 9.7 %collective-permute-start.12 = (bf16[96,512]{1,0:T(8,128)(2,1)S(1)}, bf16[96,512]{1,0:T(8,128)(2,1)S(1)}, u32[]{:S(2)}, u32[]{:S(2)}) collective-permute-start(bf16[96,512]{1,0:T(8,128)(2,1)S(1)} %get-tuple-element.61), channel_id=1, source_target_pairs={{0,4},{1,5},{2,6},{3,7},{4,0},{5,1},{6,2},{7,3},{8,12},{9,13},{10,... | collective-permute-start | bytes 294920 | tf_op jit(solution)/shard_map/ppermute | solution.py:22
  17.0 1.2 %collective-permute-start.9 = (bf16[32,512]{1,0:T(8,128)(2,1)S(1)}, bf16[32,512]{1,0:T(8,128)(2,1)S(1)}, u32[]{:S(2)}, u32[]{:S(2)}) collective-permute-start(bf16[32,512]{1,0:T(8,128)(2,1)S(1)} %collective-permute-done.8.refs_6_), channel_id=1, source_target_pairs={{0,1},{1,0},{2,3},{3,2},{4,5},{5,4},{6,7},{7,6},{8,9},{9,8},{10,11... | collective-permute-start | bytes 98312 | tf_op jit(solution)/shard_map/ppermute | solution.py:22
  17.1 7.2 %collective-permute-start.14 = (bf16[96,512]{1,0:T(8,128)(2,1)S(1)}, bf16[96,512]{1,0:T(8,128)(2,1)S(1)}, u32[]{:S(2)}, u32[]{:S(2)}) collective-permute-start(bf16[96,512]{1,0:T(8,128)(2,1)S(1)} %get-tuple-element.62), channel_id=1, source_target_pairs={{0,6},{1,7},{2,4},{3,5},{4,2},{5,3},{6,0},{7,1},{8,14},{9,15},{10,... | collective-permute-start | bytes 294920 | tf_op jit(solution)/shard_map/ppermute | solution.py:22
  18.2 1.2 %collective-permute-start.11 = (bf16[32,512]{1,0:T(8,128)(2,1)S(1)}, bf16[32,512]{1,0:T(8,128)(2,1)S(1)}, u32[]{:S(2)}, u32[]{:S(2)}) collective-permute-start(bf16[32,512]{1,0:T(8,128)(2,1)S(1)} %collective-permute-done.10.refs_8_), channel_id=1, source_target_pairs={{0,1},{1,0},{2,3},{3,2},{4,5},{5,4},{6,7},{7,6},{8,9},{9,8},{10,11... | collective-permute-start | bytes 98312 | tf_op jit(solution)/shard_map/ppermute | solution.py:22
  19.4 12.7 %collective-permute-start.16 = (bf16[256,256]{1,0:T(8,128)(2,1)S(1)}, bf16[256,256]{1,0:T(8,128)(2,1)S(1)}, u32[]{:S(2)}, u32[]{:S(2)}) collective-permute-start(bf16[256,256]{1,0:T(8,128)(2,1)S(1)} %constant_dynamic-update-slice_fusion), channel_id=1, source_target_pairs={{0,8},{8,0},{16,24},{24,16},{1,9},{9,1},{17,25},{25,17},{2,10},{10... | collective-permute-start | bytes 393224 | tf_op jit(solution)/shard_map/ppermute | solution.py:22
  20.9 11.3 %collective-permute-start.17 = (bf16[256,256]{1,0:T(8,128)(2,1)S(1)}, bf16[256,256]{1,0:T(8,128)(2,1)S(1)}, u32[]{:S(2)}, u32[]{:S(2)}) collective-permute-start(bf16[256,256]{1,0:T(8,128)(2,1)S(1)} %constant_dynamic-update-slice_fusion), channel_id=1, source_target_pairs={{0,16},{8,24},{16,0},{24,8},{1,17},{9,25},{17,1},{25,9},{2,18},{10... | collective-permute-start | bytes 393224 | tf_op jit(solution)/shard_map/ppermute | solution.py:22
  22.5 9.8 %collective-permute-start.18 = (bf16[256,256]{1,0:T(8,128)(2,1)S(1)}, bf16[256,256]{1,0:T(8,128)(2,1)S(1)}, u32[]{:S(2)}, u32[]{:S(2)}) collective-permute-start(bf16[256,256]{1,0:T(8,128)(2,1)S(1)} %constant_dynamic-update-slice_fusion), channel_id=1, source_target_pairs={{0,24},{8,16},{16,8},{24,0},{1,25},{9,17},{17,9},{25,1},{2,26},{10... | collective-permute-start | bytes 393224 | tf_op jit(solution)/shard_map/ppermute | solution.py:22
  22.9 5.0 %collective-permute-start.13 = (bf16[96,512]{1,0:T(8,128)(2,1)S(1)}, bf16[96,512]{1,0:T(8,128)(2,1)S(1)}, u32[]{:S(2)}, u32[]{:S(2)}) collective-permute-start(bf16[96,512]{1,0:T(8,128)(2,1)S(1)} %collective-permute-done.12.refs_10_), channel_id=1, source_target_pairs={{0,1},{1,0},{2,3},{3,2},{4,5},{5,4},{6,7},{7,6},{8,9},{9,8},{10,11... | collective-permute-start | bytes 294920 | tf_op jit(solution)/shard_map/ppermute | solution.py:22
  24.2 4.3 %collective-permute-start.15 = (bf16[96,512]{1,0:T(8,128)(2,1)S(1)}, bf16[96,512]{1,0:T(8,128)(2,1)S(1)}, u32[]{:S(2)}, u32[]{:S(2)}) collective-permute-start(bf16[96,512]{1,0:T(8,128)(2,1)S(1)} %collective-permute-done.14.refs_12_), channel_id=1, source_target_pairs={{0,1},{1,0},{2,3},{3,2},{4,5},{5,4},{6,7},{7,6},{8,9},{9,8},{10,11... | collective-permute-start | bytes 294920 | tf_op jit(solution)/shard_map/ppermute | solution.py:22
  27.9 7.6 %collective-permute-start.5 = (bf16[128,128]{1,0:T(8,128)(2,1)S(1)}, bf16[128,128]{1,0:T(8,128)(2,1)S(1)}, u32[]{:S(2)}, u32[]{:S(2)}) collective-permute-start(bf16[128,128]{1,0:T(8,128)(2,1)S(1)} %get-tuple-element.50), channel_id=1, source_target_pairs={{0,1},{1,0},{2,3},{3,2},{4,5},{5,4},{6,7},{7,6},{8,9},{9,8},{10,11... | collective-permute-start | bytes 98312 | tf_op jit(solution)/shard_map/ppermute | solution.py:22
  28.5 7.0 %collective-permute-start.6 = (bf16[128,128]{1,0:T(8,128)(2,1)S(1)}, bf16[128,128]{1,0:T(8,128)(2,1)S(1)}, u32[]{:S(2)}, u32[]{:S(2)}) collective-permute-start(bf16[128,128]{1,0:T(8,128)(2,1)S(1)} %get-tuple-element.51), channel_id=1, source_target_pairs={{0,2},{1,3},{2,0},{3,1},{4,6},{5,7},{6,4},{7,5},{8,10},{9,11},{10,... | collective-permute-start | bytes 98312 | tf_op jit(solution)/shard_map/ppermute | solution.py:22
  32.1 7.0 %copy-start = (bf16[512,768]{1,0:T(8,128)(2,1)S(1)}, bf16[512,768]{1,0:T(8,128)(2,1)}, u32[]{:S(2)}) copy-start(bf16[512,768]{1,0:T(8,128)(2,1)} %weight_ref.1) | copy-start | bytes 2359300
  32.2 3.7 %collective-permute-start.7 = (bf16[128,128]{1,0:T(8,128)(2,1)S(1)}, bf16[128,128]{1,0:T(8,128)(2,1)S(1)}, u32[]{:S(2)}, u32[]{:S(2)}) collective-permute-start(bf16[128,128]{1,0:T(8,128)(2,1)S(1)} %get-tuple-element.52), channel_id=1, source_target_pairs={{0,3},{1,2},{2,1},{3,0},{4,7},{5,6},{6,5},{7,4},{8,11},{9,10},{10,... | collective-permute-start | bytes 98312 | tf_op jit(solution)/shard_map/ppermute | solution.py:22
  33.3 2.9 %collective-permute-start.19 = (bf16[128,128]{1,0:T(8,128)(2,1)S(1)}, bf16[128,128]{1,0:T(8,128)(2,1)S(1)}, u32[]{:S(2)}, u32[]{:S(2)}) collective-permute-start(bf16[128,128]{1,0:T(8,128)(2,1)S(1)} %get-tuple-element.74), channel_id=1, source_target_pairs={{0,1},{1,0},{2,3},{3,2},{4,5},{5,4},{6,7},{7,6},{8,9},{9,8},{10,11... | collective-permute-start | bytes 98312 | tf_op jit(solution)/shard_map/ppermute | solution.py:22
  33.5 3.9 %collective-permute-start.20 = (bf16[128,128]{1,0:T(8,128)(2,1)S(1)}, bf16[128,128]{1,0:T(8,128)(2,1)S(1)}, u32[]{:S(2)}, u32[]{:S(2)}) collective-permute-start(bf16[128,128]{1,0:T(8,128)(2,1)S(1)} %get-tuple-element.75), channel_id=1, source_target_pairs={{0,2},{1,3},{2,0},{3,1},{4,6},{5,7},{6,4},{7,5},{8,10},{9,11},{10,... | collective-permute-start | bytes 98312 | tf_op jit(solution)/shard_map/ppermute | solution.py:22
  35.5 3.7 %collective-permute-start.21 = (bf16[128,128]{1,0:T(8,128)(2,1)S(1)}, bf16[128,128]{1,0:T(8,128)(2,1)S(1)}, u32[]{:S(2)}, u32[]{:S(2)}) collective-permute-start(bf16[128,128]{1,0:T(8,128)(2,1)S(1)} %get-tuple-element.76), channel_id=1, source_target_pairs={{0,3},{1,2},{2,1},{3,0},{4,7},{5,6},{6,5},{7,4},{8,11},{9,10},{10,... | collective-permute-start | bytes 98312 | tf_op jit(solution)/shard_map/ppermute | solution.py:22

commit v6 on v5

--- a/solution.py
+++ b/solution.py
@@ -84,15 +84,13 @@
         if s % 2 == 0:
             for copy in copies[3 * s : 3 * s + 6]:
                 copy.wait()
-        block = jnp.concatenate([taken[x, part] for part in range(3)], axis=1)
-        one, two = [dot(one_hot[s, t], block, ((1,), (0,))) for t in range(2)]
+        key, value = taken[x, 1].astype(F32), taken[x, 2].astype(F32)
+        value = pltpu.roll(value, HEAD_DIM, axis=1)
+        pairs = [jnp.where(first, key, value), jnp.where(first, value, key)]
+        blocks = [jnp.concatenate([taken[x, 0], kv.astype(BF16)], axis=1) for kv in pairs]
+        one, two = [dot(one_hot[s, t], blocks[t], ((1,), (0,))) for t in range(2)]
         query = jnp.where(first, one[:, :LANES], two[:, :LANES]) * HEAD_DIM**-0.5
-        kv_one = jnp.where(
-            first, one[:, LANES : 2 * LANES], pltpu.roll(one[:, 2 * LANES :], HEAD_DIM, axis=1)
-        ).astype(BF16)
-        kv_two = jnp.where(
-            first, pltpu.roll(two[:, 2 * LANES :], HEAD_DIM, axis=1), two[:, LANES : 2 * LANES]
-        ).astype(BF16)
+        kv_one, kv_two = one[:, LANES:].astype(BF16), two[:, LANES:].astype(BF16)
         if x >= 2:
             low, high = query[: rows // 2], pltpu.roll(query[rows // 2 :], HEAD_DIM, axis=1)
             leads[x - 2][:rows, :] = kv_one

time: 40.7 us -> 40.5 us (level)
  no operation moved by 1% of the time
where the time goes in v6:
time: 40.5 us; the launch traced here: 40.3 us
  starting transfers between devices  23.8 us (59%)
  Pallas kernels  9.74 us (24%)
  waiting for transfers between devices  6.67 us (16%)
    ppermute x22, starting transfers between devices, exchange(): return lax.ppermute(block, axis, [(i, i ^ distance) for i in range(count)])  23.8 us
    pallas_call x7, Pallas kernels, call(): pl.pallas_call(kernel, in_specs=in_specs or [vmem] * len(operands), out_s...  9.74 us
    ppermute x22, waiting for transfers between devices, exchange(): return lax.ppermute(block, axis, [(i, i ^ distance) for i in range(count)])  6.67 us
  transfers between devices with their start and end apart: 22, of which 7 were waited for; matrix products, arithmetic and copies ran while one was open for 0% of the time, Pallas kernels for 16%

profile of v6, /device:TPU:0, one launch (start us, length us, event | category | flops | bytes accessed | tf_op | source)
XLA Modules:
  0.0 40.3 jit_solution(12574669043580936880)
XLA Ops:
  0.0 2.0 %shard_map.55 = (bf16[256,384]{1,0:T(8,128)(2,1)S(1)}, bf16[256,384]{1,0:T(8,128)(2,1)S(1)}, bf16[416,128]{1,0:T(8,128)(2,1)S(1)}, bf16[416,128]{1,0:T(8,128)(2,...) custom-call(s32[16]{0:T(128)} %lengths_ref.1, ...), custom_call_target="tpu_custom_call" | custom-call | tf_op jit(solution)/shard_map/pallas_call | solution.py:380
  2.0 0.6 %collective-permute-start = (bf16[256,384]{1,0:T(8,128)(2,1)S(1)}, bf16[256,384]{1,0:T(8,128)(2,1)S(1)}, u32[]{:S(2)}, u32[]{:S(2)}) collective-permute-start(bf16[256,384]{1,0:T(8,128)(2,1)S(1)} %get-tuple-element.43), channel_id=1, source_target_pairs={{0,1},{1,0},{2,3},{3,2},{4,5},{5,4},{6,7},{7,6},{8,9},{9,8},{10,11... | collective-permute-start | bytes 589832 | tf_op jit(solution)/shard_map/ppermute | solution.py:22
  2.6 2.6 %collective-permute-start.3 = (bf16[416,128]{1,0:T(8,128)(2,1)S(1)}, bf16[416,128]{1,0:T(8,128)(2,1)S(1)}, u32[]{:S(2)}, u32[]{:S(2)}) collective-permute-start(bf16[416,128]{1,0:T(8,128)(2,1)S(1)} %get-tuple-element.46), channel_id=1, source_target_pairs={{0,2},{1,3},{2,0},{3,1},{4,6},{5,7},{6,4},{7,5},{8,10},{9,11},{10,... | collective-permute-start | bytes 319496 | tf_op jit(solution)/shard_map/ppermute | solution.py:22
  5.2 0.0 collective-permute-start.4
  5.2 2.8 %collective-permute-start.8 = (bf16[32,512]{1,0:T(8,128)(2,1)S(1)}, bf16[32,512]{1,0:T(8,128)(2,1)S(1)}, u32[]{:S(2)}, u32[]{:S(2)}) collective-permute-start(bf16[32,512]{1,0:T(8,128)(2,1)S(1)} %get-tuple-element.59), channel_id=1, source_target_pairs={{0,4},{1,5},{2,6},{3,7},{4,0},{5,1},{6,2},{7,3},{8,12},{9,13},{10,... | collective-permute-start | bytes 98312 | tf_op jit(solution)/shard_map/ppermute | solution.py:22
  8.0 1.3 %collective-permute-start.10 = (bf16[32,512]{1,0:T(8,128)(2,1)S(1)}, bf16[32,512]{1,0:T(8,128)(2,1)S(1)}, u32[]{:S(2)}, u32[]{:S(2)}) collective-permute-start(bf16[32,512]{1,0:T(8,128)(2,1)S(1)} %get-tuple-element.60), channel_id=1, source_target_pairs={{0,6},{1,7},{2,4},{3,5},{4,2},{5,3},{6,0},{7,1},{8,14},{9,15},{10,... | collective-permute-start | bytes 98312 | tf_op jit(solution)/shard_map/ppermute | solution.py:22
  9.3 0.0 collective-permute-done.3.refs_2_
  9.3 1.7 %collective-permute-start.1 = (bf16[384,128]{1,0:T(8,128)(2,1)S(1)}, bf16[384,128]{1,0:T(8,128)(2,1)S(1)}, u32[]{:S(2)}, u32[]{:S(2)}) collective-permute-start(bf16[384,128]{1,0:T(8,128)(2,1)S(1)} %get-tuple-element.44), channel_id=1, source_target_pairs={{0,2},{1,3},{2,0},{3,1},{4,6},{5,7},{6,4},{7,5},{8,10},{9,11},{10,... | collective-permute-start | bytes 294920 | tf_op jit(solution)/shard_map/ppermute | solution.py:22
  11.0 0.4 %collective-permute-done.4.refs_3_ = bf16[416,128]{1,0:T(8,128)(2,1)S(1)} collective-permute-done((bf16[416,128]{1,0:T(8,128)(2,1)S(1)}, bf16[416,128]{1,0:T(8,128)(2,1)S(1)}, u32[]{:S(2)}, u32[]{:S(2)}) %collective-permute-start.4) | collective-permute-done | bytes 106528 | tf_op jit(solution)/shard_map/ppermute | solution.py:22
  11.5 1.6 %collective-permute-start.2 = (bf16[384,128]{1,0:T(8,128)(2,1)S(1)}, bf16[384,128]{1,0:T(8,128)(2,1)S(1)}, u32[]{:S(2)}, u32[]{:S(2)}) collective-permute-start(bf16[384,128]{1,0:T(8,128)(2,1)S(1)} %get-tuple-element.45), channel_id=1, source_target_pairs={{0,3},{1,2},{2,1},{3,0},{4,7},{5,6},{6,5},{7,4},{8,11},{9,10},{10,... | collective-permute-start | bytes 294920 | tf_op jit(solution)/shard_map/ppermute | solution.py:22
  13.0 0.0 collective-permute-done.8.refs_6_
  13.0 3.8 %collective-permute-start.12 = (bf16[96,512]{1,0:T(8,128)(2,1)S(1)}, bf16[96,512]{1,0:T(8,128)(2,1)S(1)}, u32[]{:S(2)}, u32[]{:S(2)}) collective-permute-start(bf16[96,512]{1,0:T(8,128)(2,1)S(1)} %get-tuple-element.61), channel_id=1, source_target_pairs={{0,4},{1,5},{2,6},{3,7},{4,0},{5,1},{6,2},{7,3},{8,12},{9,13},{10,... | collective-permute-start | bytes 294920 | tf_op jit(solution)/shard_map/ppermute | solution.py:22
  16.8 0.0 collective-permute-done.refs_1_
  16.8 0.0 collective-permute-start.9
  16.9 0.0 collective-permute-done.10.refs_8_
  16.9 0.6 %collective-permute-start.14 = (bf16[96,512]{1,0:T(8,128)(2,1)S(1)}, bf16[96,512]{1,0:T(8,128)(2,1)S(1)}, u32[]{:S(2)}, u32[]{:S(2)}) collective-permute-start(bf16[96,512]{1,0:T(8,128)(2,1)S(1)} %get-tuple-element.62), channel_id=1, source_target_pairs={{0,6},{1,7},{2,4},{3,5},{4,2},{5,3},{6,0},{7,1},{8,14},{9,15},{10,... | collective-permute-start | bytes 294920 | tf_op jit(solution)/shard_map/ppermute | solution.py:22
  17.5 0.5 %collective-permute-done.9.refs_7_ = bf16[32,512]{1,0:T(8,128)(2,1)S(1)} collective-permute-done((bf16[32,512]{1,0:T(8,128)(2,1)S(1)}, bf16[32,512]{1,0:T(8,128)(2,1)S(1)}, u32[]{:S(2)}, u32[]{:S(2)}) %collective-permute-start.9) | collective-permute-done | bytes 32800 | tf_op jit(solution)/shard_map/ppermute | solution.py:22
  18.0 0.2 collective-permute-start.11
  18.2 1.0 %collective-permute-done.11.refs_9_ = bf16[32,512]{1,0:T(8,128)(2,1)S(1)} collective-permute-done((bf16[32,512]{1,0:T(8,128)(2,1)S(1)}, bf16[32,512]{1,0:T(8,128)(2,1)S(1)}, u32[]{:S(2)}, u32[]{:S(2)}) %collective-permute-start.11) | collective-permute-done | bytes 32800 | tf_op jit(solution)/shard_map/ppermute | solution.py:22
  19.2 1.5 %collective-permute-start.16 = (bf16[256,256]{1,0:T(8,128)(2,1)S(1)}, bf16[256,256]{1,0:T(8,128)(2,1)S(1)}, u32[]{:S(2)}, u32[]{:S(2)}) collective-permute-start(bf16[256,256]{1,0:T(8,128)(2,1)S(1)} %constant_dynamic-update-slice_fusion), channel_id=1, source_target_pairs={{0,8},{8,0},{16,24},{24,16},{1,9},{9,1},{17,25},{25,17},{2,10},{10... | collective-permute-start | bytes 393224 | tf_op jit(solution)/shard_map/ppermute | solution.py:22
  20.7 0.0 collective-permute-done.1.refs_2_
  20.7 1.5 %collective-permute-start.17 = (bf16[256,256]{1,0:T(8,128)(2,1)S(1)}, bf16[256,256]{1,0:T(8,128)(2,1)S(1)}, u32[]{:S(2)}, u32[]{:S(2)}) collective-permute-start(bf16[256,256]{1,0:T(8,128)(2,1)S(1)} %constant_dynamic-update-slice_fusion), channel_id=1, source_target_pairs={{0,16},{8,24},{16,0},{24,8},{1,17},{9,25},{17,1},{25,9},{2,18},{10... | collective-permute-start | bytes 393224 | tf_op jit(solution)/shard_map/ppermute | solution.py:22
  22.3 0.0 collective-permute-done.2.refs_3_
  22.3 0.5 %collective-permute-start.18 = (bf16[256,256]{1,0:T(8,128)(2,1)S(1)}, bf16[256,256]{1,0:T(8,128)(2,1)S(1)}, u32[]{:S(2)}, u32[]{:S(2)}) collective-permute-start(bf16[256,256]{1,0:T(8,128)(2,1)S(1)} %constant_dynamic-update-slice_fusion), channel_id=1, source_target_pairs={{0,24},{8,16},{16,8},{24,0},{1,25},{9,17},{17,9},{25,1},{2,26},{10... | collective-permute-start | bytes 393224 | tf_op jit(solution)/shard_map/ppermute | solution.py:22
  22.7 0.0 collective-permute-done.12.refs_10_
  22.7 0.0 collective-permute-start.13
  22.7 1.3 %collective-permute-done.14.refs_12_ = bf16[96,512]{1,0:T(8,128)(2,1)S(1)} collective-permute-done((bf16[96,512]{1,0:T(8,128)(2,1)S(1)}, bf16[96,512]{1,0:T(8,128)(2,1)S(1)}, u32[]{:S(2)}, u32[]{:S(2)}) %collective-permute-start.14) | collective-permute-done | bytes 98336 | tf_op jit(solution)/shard_map/ppermute | solution.py:22
  24.0 0.0 collective-permute-start.15
  24.0 1.8 %shard_map.56 = (f32[512,128]{1,0:T(8,128)S(1)}, f32[512,128]{1,0:T(8,128)S(1)}, f32[512,128]{1,0:T(8,128)S(1)}, bf16[512,128]{1,0:T(8,128)(2,1)S(1)}) custom-call(s32[8,128]{1,0:T(8,128)S(1)} %get-tuple-element.41.table_ref, bf16[256,384]{1,0:T(8,128)(2,1)S(1)} %get-tuple-element.42.refs_0_, bf16[256,384]{1,0:T(8,128)(2,1)S(1)} %collective-permute-done.refs_1_, ...), custom_call_target="tpu_custom_call" | custom-call | tf_op jit(solution)/shard_map/pallas_call | solution.py:380
  25.9 1.9 %shard_map.57 = (bf16[128,128]{1,0:T(8,128)(2,1)S(1)}, bf16[128,128]{1,0:T(8,128)(2,1)S(1)}, bf16[128,128]{1,0:T(8,128)(2,1)S(1)}, bf16[128,128]{1,0:T(8,128)(2,...) custom-call(s32[8,128]{1,0:T(8,128)S(1)} %get-tuple-element.41.table_ref, ...), custom_call_target="tpu_custom_call" | custom-call | tf_op jit(solution)/shard_map/pallas_call | solution.py:380
  27.7 0.6 %collective-permute-start.5 = (bf16[128,128]{1,0:T(8,128)(2,1)S(1)}, bf16[128,128]{1,0:T(8,128)(2,1)S(1)}, u32[]{:S(2)}, u32[]{:S(2)}) collective-permute-start(bf16[128,128]{1,0:T(8,128)(2,1)S(1)} %get-tuple-element.50), channel_id=1, source_target_pairs={{0,1},{1,0},{2,3},{3,2},{4,5},{5,4},{6,7},{7,6},{8,9},{9,8},{10,11... | collective-permute-start | bytes 98312 | tf_op jit(solution)/shard_map/ppermute | solution.py:22
  28.3 0.0 collective-permute-done.15.refs_13_
  28.3 2.3 %collective-permute-start.6 = (bf16[128,128]{1,0:T(8,128)(2,1)S(1)}, bf16[128,128]{1,0:T(8,128)(2,1)S(1)}, u32[]{:S(2)}, u32[]{:S(2)}) collective-permute-start(bf16[128,128]{1,0:T(8,128)(2,1)S(1)} %get-tuple-element.51), channel_id=1, source_target_pairs={{0,2},{1,3},{2,0},{3,1},{4,6},{5,7},{6,4},{7,5},{8,10},{9,11},{10,... | collective-permute-start | bytes 98312 | tf_op jit(solution)/shard_map/ppermute | solution.py:22
  30.6 1.4 %shard_map.59 = (bf16[96,128]{1,0:T(8,128)(2,1)S(1)}, bf16[96,128]{1,0:T(8,128)(2,1)S(1)}, bf16[96,128]{1,0:T(8,128)(2,1)S(1)}, bf16[96,128]{1,0:T(8,128)(2,1)S(...) custom-call(s32[8,128]{1,0:T(8,128)S(1)} %get-tuple-element.41.table, ...), custom_call_target="tpu_custom_call" | custom-call | tf_op jit(solution)/shard_map/pallas_call | solution.py:380
  32.0 0.0 collective-permute-done.16.refs_10_
  32.0 0.1 collective-permute-start.7
  32.0 0.0 collective-permute-done.17.refs_11_
  32.1 0.0 collective-permute-done.18.refs_12_
  32.1 1.0 %shard_map.60 = (bf16[128,128]{1,0:T(8,128)(2,1)S(1)}, bf16[128,128]{1,0:T(8,128)(2,1)S(1)}, bf16[128,128]{1,0:T(8,128)(2,1)S(1)}, bf16[128,128]{1,0:T(8,128)(2,1)S(1)}) custom-call(s32[8,128]{1,0:T(8,128)S(1)} %get-tuple-element.41.table_ref, f32[128,128]{1,0:T(8,128)S(1)} %get-tuple-element.63.refs_0_, f32[128,128]{1,0:T(8,128)S(1)} %get-tuple-element.64.refs_1_, ...), custom_call_target="tpu_custom_call" | custom-call | tf_op jit(solution)/shard_map/pallas_call | solution.py:380
  33.1 0.1 collective-permute-start.19
  33.3 2.0 %collective-permute-start.20 = (bf16[128,128]{1,0:T(8,128)(2,1)S(1)}, bf16[128,128]{1,0:T(8,128)(2,1)S(1)}, u32[]{:S(2)}, u32[]{:S(2)}) collective-permute-start(bf16[128,128]{1,0:T(8,128)(2,1)S(1)} %get-tuple-element.75), channel_id=1, source_target_pairs={{0,2},{1,3},{2,0},{3,1},{4,6},{5,7},{6,4},{7,5},{8,10},{9,11},{10,... | collective-permute-start | bytes 98312 | tf_op jit(solution)/shard_map/ppermute | solution.py:22
  35.3 0.0 collective-permute-start.21
  35.3 0.0 collective-permute-done.6.refs_2_
  35.3 0.4 %collective-permute-done.7.refs_3_ = bf16[128,128]{1,0:T(8,128)(2,1)S(1)} collective-permute-done((bf16[128,128]{1,0:T(8,128)(2,1)S(1)}, bf16[128,128]{1,0:T(8,128)(2,1)S(1)}, u32[]{:S(2)}, u32[]{:S(2)}) %collective-permute-start.7) | collective-permute-done | bytes 32800 | tf_op jit(solution)/shard_map/ppermute | solution.py:22
  35.7 0.3 shard_map.58.rest_ref
  36.0 1.2 %collective-permute-done.20.refs_2_ = bf16[128,128]{1,0:T(8,128)(2,1)S(1)} collective-permute-done((bf16[128,128]{1,0:T(8,128)(2,1)S(1)}, bf16[128,128]{1,0:T(8,128)(2,1)S(1)}, u32[]{:S(2)}, u32[]{:S(2)}) %collective-permute-start.20) | collective-permute-done | bytes 32800 | tf_op jit(solution)/shard_map/ppermute | solution.py:22
  37.2 1.8 %collective-permute-done.21.refs_3_ = bf16[128,128]{1,0:T(8,128)(2,1)S(1)} collective-permute-done((bf16[128,128]{1,0:T(8,128)(2,1)S(1)}, bf16[128,128]{1,0:T(8,128)(2,1)S(1)}, u32[]{:S(2)}, u32[]{:S(2)}) %collective-permute-start.21) | collective-permute-done | bytes 32800 | tf_op jit(solution)/shard_map/ppermute | solution.py:22
  39.0 1.4 %shard_map.61 = bf16[256,768]{1,0:T(8,128)(2,1)} custom-call(bf16[512,768]{1,0:T(8,128)(2,1)S(1)} %copy-done, bf16[256,512]{1,0:T(8,128)(2,1)S(1)} %shard_map.58.rest_ref, bf16[128,128]{1,0:T(8,128)(2,1)S(1)} %get-tuple-element.73.refs_0_, bf16[128,128]{1,0:T(8,128)(2,1)S(1)} %collective-permute-done.19.refs_1_, ...), custom_call_target="tpu_custom_call" | custom-call | tf_op jit(solution)/shard_map/pallas_call | solution.py:380
  (15 shorter events, 0.0 us)
Async XLA Ops:
  2.0 14.8 %collective-permute-start = (bf16[256,384]{1,0:T(8,128)(2,1)S(1)}, bf16[256,384]{1,0:T(8,128)(2,1)S(1)}, u32[]{:S(2)}, u32[]{:S(2)}) collective-permute-start(bf16[256,384]{1,0:T(8,128)(2,1)S(1)} %get-tuple-element.43), channel_id=1, source_target_pairs={{0,1},{1,0},{2,3},{3,2},{4,5},{5,4},{6,7},{7,6},{8,9},{9,8},{10,11... | collective-permute-start | bytes 589832 | tf_op jit(solution)/shard_map/ppermute | solution.py:22
  2.6 6.8 %collective-permute-start.3 = (bf16[416,128]{1,0:T(8,128)(2,1)S(1)}, bf16[416,128]{1,0:T(8,128)(2,1)S(1)}, u32[]{:S(2)}, u32[]{:S(2)}) collective-permute-start(bf16[416,128]{1,0:T(8,128)(2,1)S(1)} %get-tuple-element.46), channel_id=1, source_target_pairs={{0,2},{1,3},{2,0},{3,1},{4,6},{5,7},{6,4},{7,5},{8,10},{9,11},{10,... | collective-permute-start | bytes 319496 | tf_op jit(solution)/shard_map/ppermute | solution.py:22
  5.2 6.3 %collective-permute-start.4 = (bf16[416,128]{1,0:T(8,128)(2,1)S(1)}, bf16[416,128]{1,0:T(8,128)(2,1)S(1)}, u32[]{:S(2)}, u32[]{:S(2)}) collective-permute-start(bf16[416,128]{1,0:T(8,128)(2,1)S(1)} %get-tuple-element.47), channel_id=1, source_target_pairs={{0,3},{1,2},{2,1},{3,0},{4,7},{5,6},{6,5},{7,4},{8,11},{9,10},{10,... | collective-permute-start | bytes 319496 | tf_op jit(solution)/shard_map/ppermute | solution.py:22
  5.2 7.8 %collective-permute-start.8 = (bf16[32,512]{1,0:T(8,128)(2,1)S(1)}, bf16[32,512]{1,0:T(8,128)(2,1)S(1)}, u32[]{:S(2)}, u32[]{:S(2)}) collective-permute-start(bf16[32,512]{1,0:T(8,128)(2,1)S(1)} %get-tuple-element.59), channel_id=1, source_target_pairs={{0,4},{1,5},{2,6},{3,7},{4,0},{5,1},{6,2},{7,3},{8,12},{9,13},{10,... | collective-permute-start | bytes 98312 | tf_op jit(solution)/shard_map/ppermute | solution.py:22
  8.0 8.9 %collective-permute-start.10 = (bf16[32,512]{1,0:T(8,128)(2,1)S(1)}, bf16[32,512]{1,0:T(8,128)(2,1)S(1)}, u32[]{:S(2)}, u32[]{:S(2)}) collective-permute-start(bf16[32,512]{1,0:T(8,128)(2,1)S(1)} %get-tuple-element.60), channel_id=1, source_target_pairs={{0,6},{1,7},{2,4},{3,5},{4,2},{5,3},{6,0},{7,1},{8,14},{9,15},{10,... | collective-permute-start | bytes 98312 | tf_op jit(solution)/shard_map/ppermute | solution.py:22
  9.3 11.4 %collective-permute-start.1 = (bf16[384,128]{1,0:T(8,128)(2,1)S(1)}, bf16[384,128]{1,0:T(8,128)(2,1)S(1)}, u32[]{:S(2)}, u32[]{:S(2)}) collective-permute-start(bf16[384,128]{1,0:T(8,128)(2,1)S(1)} %get-tuple-element.44), channel_id=1, source_target_pairs={{0,2},{1,3},{2,0},{3,1},{4,6},{5,7},{6,4},{7,5},{8,10},{9,11},{10,... | collective-permute-start | bytes 294920 | tf_op jit(solution)/shard_map/ppermute | solution.py:22
  11.5 10.8 %collective-permute-start.2 = (bf16[384,128]{1,0:T(8,128)(2,1)S(1)}, bf16[384,128]{1,0:T(8,128)(2,1)S(1)}, u32[]{:S(2)}, u32[]{:S(2)}) collective-permute-start(bf16[384,128]{1,0:T(8,128)(2,1)S(1)} %get-tuple-element.45), channel_id=1, source_target_pairs={{0,3},{1,2},{2,1},{3,0},{4,7},{5,6},{6,5},{7,4},{8,11},{9,10},{10,... | collective-permute-start | bytes 294920 | tf_op jit(solution)/shard_map/ppermute | solution.py:22
  13.0 9.7 %collective-permute-start.12 = (bf16[96,512]{1,0:T(8,128)(2,1)S(1)}, bf16[96,512]{1,0:T(8,128)(2,1)S(1)}, u32[]{:S(2)}, u32[]{:S(2)}) collective-permute-start(bf16[96,512]{1,0:T(8,128)(2,1)S(1)} %get-tuple-element.61), channel_id=1, source_target_pairs={{0,4},{1,5},{2,6},{3,7},{4,0},{5,1},{6,2},{7,3},{8,12},{9,13},{10,... | collective-permute-start | bytes 294920 | tf_op jit(solution)/shard_map/ppermute | solution.py:22
  16.8 1.2 %collective-permute-start.9 = (bf16[32,512]{1,0:T(8,128)(2,1)S(1)}, bf16[32,512]{1,0:T(8,128)(2,1)S(1)}, u32[]{:S(2)}, u32[]{:S(2)}) collective-permute-start(bf16[32,512]{1,0:T(8,128)(2,1)S(1)} %collective-permute-done.8.refs_6_), channel_id=1, source_target_pairs={{0,1},{1,0},{2,3},{3,2},{4,5},{5,4},{6,7},{7,6},{8,9},{9,8},{10,11... | collective-permute-start | bytes 98312 | tf_op jit(solution)/shard_map/ppermute | solution.py:22
  16.9 7.2 %collective-permute-start.14 = (bf16[96,512]{1,0:T(8,128)(2,1)S(1)}, bf16[96,512]{1,0:T(8,128)(2,1)S(1)}, u32[]{:S(2)}, u32[]{:S(2)}) collective-permute-start(bf16[96,512]{1,0:T(8,128)(2,1)S(1)} %get-tuple-element.62), channel_id=1, source_target_pairs={{0,6},{1,7},{2,4},{3,5},{4,2},{5,3},{6,0},{7,1},{8,14},{9,15},{10,... | collective-permute-start | bytes 294920 | tf_op jit(solution)/shard_map/ppermute | solution.py:22
  18.0 1.2 %collective-permute-start.11 = (bf16[32,512]{1,0:T(8,128)(2,1)S(1)}, bf16[32,512]{1,0:T(8,128)(2,1)S(1)}, u32[]{:S(2)}, u32[]{:S(2)}) collective-permute-start(bf16[32,512]{1,0:T(8,128)(2,1)S(1)} %collective-permute-done.10.refs_8_), channel_id=1, source_target_pairs={{0,1},{1,0},{2,3},{3,2},{4,5},{5,4},{6,7},{7,6},{8,9},{9,8},{10,11... | collective-permute-start | bytes 98312 | tf_op jit(solution)/shard_map/ppermute | solution.py:22
  19.2 12.7 %collective-permute-start.16 = (bf16[256,256]{1,0:T(8,128)(2,1)S(1)}, bf16[256,256]{1,0:T(8,128)(2,1)S(1)}, u32[]{:S(2)}, u32[]{:S(2)}) collective-permute-start(bf16[256,256]{1,0:T(8,128)(2,1)S(1)} %constant_dynamic-update-slice_fusion), channel_id=1, source_target_pairs={{0,8},{8,0},{16,24},{24,16},{1,9},{9,1},{17,25},{25,17},{2,10},{10... | collective-permute-start | bytes 393224 | tf_op jit(solution)/shard_map/ppermute | solution.py:22
  20.7 11.3 %collective-permute-start.17 = (bf16[256,256]{1,0:T(8,128)(2,1)S(1)}, bf16[256,256]{1,0:T(8,128)(2,1)S(1)}, u32[]{:S(2)}, u32[]{:S(2)}) collective-permute-start(bf16[256,256]{1,0:T(8,128)(2,1)S(1)} %constant_dynamic-update-slice_fusion), channel_id=1, source_target_pairs={{0,16},{8,24},{16,0},{24,8},{1,17},{9,25},{17,1},{25,9},{2,18},{10... | collective-permute-start | bytes 393224 | tf_op jit(solution)/shard_map/ppermute | solution.py:22
  22.3 9.8 %collective-permute-start.18 = (bf16[256,256]{1,0:T(8,128)(2,1)S(1)}, bf16[256,256]{1,0:T(8,128)(2,1)S(1)}, u32[]{:S(2)}, u32[]{:S(2)}) collective-permute-start(bf16[256,256]{1,0:T(8,128)(2,1)S(1)} %constant_dynamic-update-slice_fusion), channel_id=1, source_target_pairs={{0,24},{8,16},{16,8},{24,0},{1,25},{9,17},{17,9},{25,1},{2,26},{10... | collective-permute-start | bytes 393224 | tf_op jit(solution)/shard_map/ppermute | solution.py:22
  22.7 5.0 %collective-permute-start.13 = (bf16[96,512]{1,0:T(8,128)(2,1)S(1)}, bf16[96,512]{1,0:T(8,128)(2,1)S(1)}, u32[]{:S(2)}, u32[]{:S(2)}) collective-permute-start(bf16[96,512]{1,0:T(8,128)(2,1)S(1)} %collective-permute-done.12.refs_10_), channel_id=1, source_target_pairs={{0,1},{1,0},{2,3},{3,2},{4,5},{5,4},{6,7},{7,6},{8,9},{9,8},{10,11... | collective-permute-start | bytes 294920 | tf_op jit(solution)/shard_map/ppermute | solution.py:22
  24.0 4.3 %collective-permute-start.15 = (bf16[96,512]{1,0:T(8,128)(2,1)S(1)}, bf16[96,512]{1,0:T(8,128)(2,1)S(1)}, u32[]{:S(2)}, u32[]{:S(2)}) collective-permute-start(bf16[96,512]{1,0:T(8,128)(2,1)S(1)} %collective-permute-done.14.refs_12_), channel_id=1, source_target_pairs={{0,1},{1,0},{2,3},{3,2},{4,5},{5,4},{6,7},{7,6},{8,9},{9,8},{10,11... | collective-permute-start | bytes 294920 | tf_op jit(solution)/shard_map/ppermute | solution.py:22
  27.7 7.6 %collective-permute-start.5 = (bf16[128,128]{1,0:T(8,128)(2,1)S(1)}, bf16[128,128]{1,0:T(8,128)(2,1)S(1)}, u32[]{:S(2)}, u32[]{:S(2)}) collective-permute-start(bf16[128,128]{1,0:T(8,128)(2,1)S(1)} %get-tuple-element.50), channel_id=1, source_target_pairs={{0,1},{1,0},{2,3},{3,2},{4,5},{5,4},{6,7},{7,6},{8,9},{9,8},{10,11... | collective-permute-start | bytes 98312 | tf_op jit(solution)/shard_map/ppermute | solution.py:22
  28.3 7.0 %collective-permute-start.6 = (bf16[128,128]{1,0:T(8,128)(2,1)S(1)}, bf16[128,128]{1,0:T(8,128)(2,1)S(1)}, u32[]{:S(2)}, u32[]{:S(2)}) collective-permute-start(bf16[128,128]{1,0:T(8,128)(2,1)S(1)} %get-tuple-element.51), channel_id=1, source_target_pairs={{0,2},{1,3},{2,0},{3,1},{4,6},{5,7},{6,4},{7,5},{8,10},{9,11},{10,... | collective-permute-start | bytes 98312 | tf_op jit(solution)/shard_map/ppermute | solution.py:22
  32.0 7.0 %copy-start = (bf16[512,768]{1,0:T(8,128)(2,1)S(1)}, bf16[512,768]{1,0:T(8,128)(2,1)}, u32[]{:S(2)}) copy-start(bf16[512,768]{1,0:T(8,128)(2,1)} %weight_ref.1) | copy-start | bytes 2359300
  32.0 3.7 %collective-permute-start.7 = (bf16[128,128]{1,0:T(8,128)(2,1)S(1)}, bf16[128,128]{1,0:T(8,128)(2,1)S(1)}, u32[]{:S(2)}, u32[]{:S(2)}) collective-permute-start(bf16[128,128]{1,0:T(8,128)(2,1)S(1)} %get-tuple-element.52), channel_id=1, source_target_pairs={{0,3},{1,2},{2,1},{3,0},{4,7},{5,6},{6,5},{7,4},{8,11},{9,10},{10,... | collective-permute-start | bytes 98312 | tf_op jit(solution)/shard_map/ppermute | solution.py:22
  33.1 2.9 %collective-permute-start.19 = (bf16[128,128]{1,0:T(8,128)(2,1)S(1)}, bf16[128,128]{1,0:T(8,128)(2,1)S(1)}, u32[]{:S(2)}, u32[]{:S(2)}) collective-permute-start(bf16[128,128]{1,0:T(8,128)(2,1)S(1)} %get-tuple-element.74), channel_id=1, source_target_pairs={{0,1},{1,0},{2,3},{3,2},{4,5},{5,4},{6,7},{7,6},{8,9},{9,8},{10,11... | collective-permute-start | bytes 98312 | tf_op jit(solution)/shard_map/ppermute | solution.py:22
  33.3 3.9 %collective-permute-start.20 = (bf16[128,128]{1,0:T(8,128)(2,1)S(1)}, bf16[128,128]{1,0:T(8,128)(2,1)S(1)}, u32[]{:S(2)}, u32[]{:S(2)}) collective-permute-start(bf16[128,128]{1,0:T(8,128)(2,1)S(1)} %get-tuple-element.75), channel_id=1, source_target_pairs={{0,2},{1,3},{2,0},{3,1},{4,6},{5,7},{6,4},{7,5},{8,10},{9,11},{10,... | collective-permute-start | bytes 98312 | tf_op jit(solution)/shard_map/ppermute | solution.py:22
  35.3 3.7 %collective-permute-start.21 = (bf16[128,128]{1,0:T(8,128)(2,1)S(1)}, bf16[128,128]{1,0:T(8,128)(2,1)S(1)}, u32[]{:S(2)}, u32[]{:S(2)}) collective-permute-start(bf16[128,128]{1,0:T(8,128)(2,1)S(1)} %get-tuple-element.76), channel_id=1, source_target_pairs={{0,3},{1,2},{2,1},{3,0},{4,7},{5,6},{6,5},{7,4},{8,11},{9,10},{10,... | collective-permute-start | bytes 98312 | tf_op jit(solution)/shard_map/ppermute | solution.py:22
